TPU v7x, 128 devices: a whole 4x4x4 slice. The times are simulated.
128 devices in a mesh: ax: 16 (over x, y), xs: 8 (over z, core).
Axes of the slice: x: 4, y: 4, z: 4, core: 2. Of those that a mesh axis runs over, the one named last changes fastest.
Arguments:
- state: float32 [5, 128, 128, 128], P(None, 'ax', 'xs'), may hold values from -0.2 to 6, as said below
- wall_code: int32 [128, 4, 128], replicated, may hold values from 0 to 3
Outputs:
- relaxed: float32 [5, 128, 128, 128], P(None, 'ax', 'xs')
Inputs may be any that keep to these rules, and one draw needn't show every extreme that they name: `state`: components are density, axial, y and z momentum, total energy; density and pressure are positive. wall_code[i, k, j] is the type of the wall face of side k (0: y index 0, 1: y index 127, 2: z index 0, 3: z index 127) at axial cell i and transverse cell j: 0 wall, 1 evaporator, 2 condenser, 3 adiabatic wick.
All inputs are finite; a program needn't handle non-finite values.
Results may differ from a plain program's by a relative error of at most 0.00002.
Values sent between devices are 32-bit elements; how exact they have to be, the bound alone decides.
No kernel may reach another device: no remote copies, remote signals or barrier semaphores. Data moves between devices by JAX's collectives and lax.ppermute only.
A program may use at most 192 MiB of HBM per device.

v0:
```python
import functools

import jax
import jax.numpy as jnp
from jax import lax
from jax.experimental import pallas as pl
from jax.experimental.pallas import tpu as pltpu
from jax.sharding import PartitionSpec as P

HEAT_RATIO = 1.4
CFL_NUMBER = 0.8
SECOND_COEF = 0.25
FOURTH_COEF = 0.0625
INFLOW_ENTHALPY = 3.0
SEGMENT_WEIGHTS = (0.25, 1.0 / 3.0, 0.5, 1.0)
LANES = 128
EXACT = lax.Precision.HIGHEST
INTERPRET = False


def up(x, axis):
    return pltpu.roll(x, x.shape[axis] - 1, axis)


def down(x, axis):
    return pltpu.roll(x, 1, axis)


def primitives(v):
    inv = 1.0 / v[0]
    kinetic = 0.5 * (v[1] * v[1] + v[2] * v[2] + v[3] * v[3]) * inv
    pressure = (HEAT_RATIO - 1.0) * (v[4] - kinetic)
    sound = jnp.sqrt(HEAT_RATIO * pressure * inv)
    return inv, pressure, sound


def fluxes(v, q, pressure, d):
    out = [v[d], v[1] * q, v[2] * q, v[3] * q, (v[4] + pressure) * q]
    out[d] = out[d] + pressure
    return out


def sensor(back, here, ahead):
    outer = ahead + back
    twice = here + here
    return jnp.abs(outer - twice) / (outer + twice)


def weights(nu, lam):
    e2 = SECOND_COEF * nu
    e4 = jnp.maximum(FOURTH_COEF - e2, 0.0)
    k4 = lam * e4
    return lam * e2 + (k4 + k4), k4


def depth_matrix(depth):
    a = lax.broadcasted_iota(jnp.int32, (LANES, LANES), 0)
    b = lax.broadcasted_iota(jnp.int32, (LANES, LANES), 1)

    def at(by):
        return jnp.where(a == mirror(b + by, depth), 1.0, 0.0)

    above = at(1)
    half = jnp.concatenate([above, at(2) - above + at(0) - at(-1)], axis=1)
    return jnp.concatenate([half, half], axis=0).astype(jnp.bfloat16)


EVEN = (0, 1, 2, 4)


def depth_shifts(rows, matrix, depth):
    x = jnp.concatenate([v[c] for v in rows for c in EVEN], axis=0)
    if depth < LANES:
        x = jnp.where(lax.broadcasted_iota(jnp.int32, x.shape, 1) < depth, x, 0.0)
    high = x.astype(jnp.bfloat16)
    low = (x - high.astype(jnp.float32)).astype(jnp.bfloat16)
    moved = jnp.dot(
        jnp.concatenate([high, low], axis=1), matrix[...], preferred_element_type=jnp.float32
    )
    n = rows[0][0].shape[0]
    out = []
    for k in range(len(rows)):
        at = [(4 * k + m) * n for m in range(4)]
        out.append(
            {c: (moved[i : i + n, :LANES], moved[i : i + n, LANES:]) for c, i in zip(EVEN, at)}
        )
    return out


def depth_terms(v, inv, pressure, sound, depth, moved):
    lane = lax.broadcasted_iota(jnp.int32, pressure.shape, 1)
    lo, hi, outside = lane == 0, lane == depth - 1, lane >= depth - 1
    q = v[3] * inv
    q_up = jnp.where(hi, -q, up(q, 1))
    p_up = jnp.where(hi, pressure, up(pressure, 1))
    p_dn = jnp.where(lo, pressure, down(pressure, 1))
    wave = jnp.abs(q) + sound
    wave_up = jnp.abs(q_up) + jnp.where(hi, sound, up(sound, 1))
    nu = sensor(p_dn, pressure, p_up)
    k2, k4 = weights(jnp.maximum(nu, jnp.where(hi, nu, up(nu, 1))), wave + wave_up)
    d1 = jnp.where(hi, -v[3], up(v[3], 1)) - v[3]
    d1_dn = jnp.where(lo, v[3] + v[3], down(d1, 1))
    d1_up = jnp.where(hi, d1_dn, up(d1, 1))
    above = {c: x[0] for c, x in moved.items()}
    above[3] = d1 + v[3]
    flux = fluxes(v, q, pressure, 3)
    flux_up = fluxes(above, q_up, p_up, 3)
    out = []
    for c in range(5):
        if c == 3:
            g = (flux[c] + flux_up[c]) - (k2 * d1 - k4 * (d1_up + d1_dn))
            w2, w4 = weights(nu, wave + wave)
            wall = (flux[c] + flux[c]) - (w2 * (v[c] + v[c]) - w4 * (d1 + d1))
            out.append(g - jnp.where(lo, wall, down(g, 1)))
        else:
            g = (flux[c] + flux_up[c]) - (k2 * (above[c] - v[c]) - k4 * moved[c][1])
            g = jnp.where(outside, 0.0, g)
            out.append(g - down(g, 1))
    return out


class Band:
    def __init__(self, base, count):
        self.base, self.count = base, count
        self.tall = -(-count // 8) * 8
        self.cross = -(-(count + 2) // 8) * 8
        self.cols = pl.ds(base, self.tall)


def cross_terms(w, prim, r, band, shift):
    n, base = band.cross, band.base - 1
    vm, v0, v1, v2 = [[w[c, r, pl.ds(base + k, n)] for c in range(5)] for k in (-1, 0, 1, 2)]
    pm, p0, p1 = [prim[1, r, pl.ds(base + k, n)] for k in (-1, 0, 1)]
    q = v0[2] * prim[0, r, pl.ds(base, n)]
    wave = jnp.abs(q) + prim[2, r, pl.ds(base, n)]
    nu = sensor(pm, p0, p1)
    flux = fluxes(v0, q, p0, 2)
    for k, x in enumerate([nu, wave] + flux):
        shift[k, 0:n] = x
    k2, k4 = weights(jnp.maximum(nu, shift[0, 1 : n + 1]), wave + shift[1, 1 : n + 1])
    out = []
    for c in range(5):
        side = (v2[c] - v1[c]) + (v0[c] - vm[c])
        g = (flux[c] + shift[2 + c, 1 : n + 1]) - (k2 * (v1[c] - v0[c]) - k4 * side)
        shift[7 + c, 0:n] = g
        out.append(shift[7 + c, 1 : band.tall + 1] - g[0 : band.tall])
    return out


class Level:
    def __init__(self, depth, fields, carry, shift, matrix):
        self.depth, self.fields, self.carry, self.shift = depth, fields, carry, shift
        self.matrix = matrix
        matrix[...] = depth_matrix(depth)

    def face(self, w, prim, r, band, carry):
        n, cols = band.tall, band.cols
        vm, v0, v1, v2 = [[w[c, r + k, cols] for c in range(5)] for k in (-1, 0, 1, 2)]
        p0, p1, p2 = [prim[1, r + k, cols] for k in (0, 1, 2)]
        q1 = v1[1] * prim[0, r + 1, cols]
        wave1 = jnp.abs(q1) + prim[2, r + 1, cols]
        nu1 = sensor(p0, p1, p2)
        f1 = fluxes(v1, q1, p1, 1)
        nu0 = carry[5, 0:n]
        wave0 = carry[6, 0:n]
        k2, k4 = weights(jnp.maximum(nu0, nu1), wave0 + wave1)
        g = []
        for c in range(5):
            d1 = v1[c] - v0[c]
            side = (v2[c] - v1[c]) + (v0[c] - vm[c])
            g.append((carry[7 + c, 0:n] + f1[c]) - (k2 * d1 - k4 * side))
        carry[5, 0:n] = nu1
        carry[6, 0:n] = wave1
        for c in range(5):
            carry[7 + c, 0:n] = f1[c]
        return g, v0

    def start(self, w, prim, r, band, carry):
        n, cols = band.tall, band.cols
        p = [prim[1, r + k, cols] for k in (-2, -1, 0)]
        v = [w[c, r - 1, cols] for c in range(5)]
        q = v[1] * prim[0, r - 1, cols]
        carry[5, 0:n] = sensor(*p)
        carry[6, 0:n] = jnp.abs(q) + prim[2, r - 1, cols]
        for c, f in enumerate(fluxes(v, q, p[1], 1)):
            carry[7 + c, 0:n] = f
        g, _ = self.face(w, prim, r - 1, band, carry)
        for c in range(5):
            carry[c, 0:n] = g[c]

    def rows(self, w, prim, begins, count, band, sink, unroll=2):
        for k, begin in enumerate(begins):
            self.start(w, prim, begin, band, self.carry.at[k])
        unroll = min(unroll, count)

        @pl.loop(0, count // unroll)
        def _(i):
            jobs = [(k, begin + i * unroll + u) for u in range(unroll) for k, begin in enumerate(begins)]
            vs = [[w[c, r, band.cols] for c in range(5)] for _, r in jobs]
            moved = depth_shifts(vs, self.matrix, self.depth)
            for j, (k, r) in enumerate(jobs):
                carry, shift = self.carry.at[k], self.shift.at[j]
                self.row(w, prim, r, band, sink, carry, shift, moved[j])

    def row(self, w, prim, r, band, sink, carry, shift, moved):
        fields, n, cols = self.fields, band.tall, band.cols
        g, v = self.face(w, prim, r, band, carry)
        total = [g[c] - carry[c, 0:n] for c in range(5)]
        for c in range(5):
            carry[c, 0:n] = g[c]
        part = depth_terms(
            v, prim[0, r, cols], prim[1, r, cols], prim[2, r, cols], self.depth, moved
        )
        total = [a + b for a, b in zip(total, part)]
        part = cross_terms(w, prim, r, band, shift)
        total = [a + b for a, b in zip(total, part)]
        evap = fields[0, r, cols]
        suction = fields[1, r, cols]
        both = suction + fields[2, r, cols]
        total = [
            total[0] + (suction * v[0] - evap),
            total[1] + both * v[1],
            total[2] + both * v[2],
            total[3] + both * v[3],
            total[4] + (suction * v[4] - INFLOW_ENTHALPY * evap),
        ]
        sink(r, v, total, band)


def fill_prim(w, prim, begin, end):
    @pl.loop(begin, end, unroll=4)
    def _(r):
        prim[0, r], prim[1, r], prim[2, r] = primitives([w[c, r] for c in range(5)])


def rate_row(v, pressure, sound, inv):
    wave = (jnp.abs(v[1]) + jnp.abs(v[2]) + jnp.abs(v[3])) * inv + 3.0 * sound
    return (0.5 * CFL_NUMBER) / wave


def store_row(w, prim, r, cols, new):
    for c in range(5):
        w[c, r, cols] = new[c]
    prim[0, r, cols], prim[1, r, cols], prim[2, r, cols] = primitives(new)


def flip8(x):
    sub = lax.broadcasted_iota(jnp.int32, x.shape, 0)
    for step in (1, 2, 4):
        if step == 4:
            x = pltpu.roll(x, 4, 0)
        else:
            x = jnp.where((sub & step) == 0, pltpu.roll(x, 8 - step, 0), pltpu.roll(x, step, 0))
    return x


def mirror(cell, extent):
    return jnp.where(cell < 0, -1 - cell, jnp.where(cell >= extent, 2 * extent - 1 - cell, cell))


def pick(shape, condition):
    a = lax.broadcasted_iota(jnp.int32, shape, 0)
    b = lax.broadcasted_iota(jnp.int32, shape, 1)
    return jnp.where(condition(a, b), 1.0, 0.0)


def matmul(a, b):
    return jnp.dot(a, b, precision=EXACT, preferred_element_type=jnp.float32)


def fine_window(pos, own, before, after, left, right, w, ends):
    for c in range(5):
        w[c, 0:8, 8:24] = before[c]
        w[c, 8:16, 8:24] = own[c]
        w[c, 16:24, 8:24] = after[c]
        w[c, 2:22, 0:8] = left[c]
        w[c, 2:22, 24:32] = right[c]

    def cross(at, to, source):
        @pl.when(pos[1] == at)
        def _():
            @pl.loop(2, 22)
            def _(r):
                for c in range(5):
                    x = flip8(w[c, r, source : source + 8])
                    w[c, r, to : to + 8] = -x if c == 2 else x

    cross(0, 0, 8)
    cross(ends[1] - 1, 24, 16)

    def axial(at, to, source, step):
        @pl.when(pos[0] == at)
        def _():
            @pl.loop(0, 8)
            def _(k):
                for c in range(5):
                    x = w[c, source + step * k, 0:32]
                    w[c, to - step * k, 0:32] = -x if c == 1 else x

    axial(0, 7, 8, 1)
    axial(ends[0] - 1, 16, 15, -1)


FINE_PLAN = (
    (((6,), 12, Band(2, 28)), ((2, 18), 4, Band(6, 20))),
    (((6,), 12, Band(4, 24)), ((4, 18), 2, Band(8, 16))),
    (((8,), 8, Band(6, 20)), ((6, 16), 2, Band(8, 16))),
    (((8,), 8, Band(8, 16)),),
)


def fine_relax_kernel(
    ends, pos, own, before, after, left, right, fields, out, *rest
):
    slabs, (wa, wb, wc, prim_a, prim_b, rate, carry, shift, matrix) = rest[:-9], rest[-9:]
    fine_window(pos, own, before, after, left, right, wa, ends)
    fill_prim(wa, prim_a, 0, 24)

    @pl.loop(2, 22, unroll=4)
    def _(r):
        rate[r] = rate_row([wa[c, r] for c in range(5)], prim_a[1, r], prim_a[2, r], prim_a[0, r])

    level = Level(LANES, fields, carry, shift, matrix)
    source, source_prim = wa, prim_a
    for k, weight in enumerate(SEGMENT_WEIGHTS):
        last = k == 3
        target = (wb, wc, wb, None)[k]
        target_prim = (prim_b, prim_a, prim_b, None)[k]

        def sink(r, v, total, band, weight=weight, last=last, target=target, prim=target_prim):
            cols = band.cols
            scale = weight * rate[r, cols]
            new = [wa[c, r, cols] - scale * total[c] for c in range(5)]
            if last:
                for c in range(5):
                    out[c, r - 8] = new[c]
                    if slabs:
                        slabs[2][c, r - 8] = new[c][14:16]
                        slabs[3][c, r - 8] = new[c][0:2]
            else:
                store_row(target, prim, r, cols, new)

        for begins, count, band in FINE_PLAN[k]:
            level.rows(source, source_prim, begins, count, band, sink)
        source, source_prim = target, target_prim
    if slabs:
        for c in range(5):
            for k in range(2):
                slabs[0][c, k] = out[c, 6 + k]
                slabs[1][c, k] = out[c, k]


def vmem(*shape):
    return pltpu.VMEM(shape, jnp.float32)


def call(kernel, out_shapes, scratch, flops, *args):
    specs = [pl.BlockSpec(memory_space=pltpu.SMEM)]
    specs += [pl.BlockSpec(memory_space=pltpu.VMEM)] * (len(args) - 1)
    single = len(out_shapes) == 1
    outs = [jax.ShapeDtypeStruct(s, jnp.float32) for s in out_shapes]
    out_specs = [pl.BlockSpec(memory_space=pltpu.VMEM)] * len(outs)
    moved = sum(4 * a.size for a in args) + sum(4 * o.size for o in outs)
    return pl.pallas_call(
        kernel,
        out_shape=outs[0] if single else outs,
        in_specs=specs,
        out_specs=out_specs[0] if single else out_specs,
        scratch_shapes=scratch,
        cost_estimate=pl.CostEstimate(flops=flops, bytes_accessed=moved, transcendentals=0),
        interpret=INTERPRET,
    )(*args)


MATRIX = pltpu.VMEM((2 * LANES, 2 * LANES), jnp.bfloat16)
FINE_COLS = 40
MIDDLE_COLS = 32
COARSE_COLS = 24


def fine_relax(ends, pos, own, halos, fields, slabs):
    scratch = [vmem(5, 24, FINE_COLS, LANES)] * 3 + [vmem(3, 24, FINE_COLS, LANES)] * 2
    scratch += [vmem(24, FINE_COLS, LANES), vmem(2, 12, 32, LANES), vmem(4, 12, 40, LANES), MATRIX]
    outs = [own.shape]
    if slabs:
        outs += [(5, 2, 16, LANES)] * 2 + [(5, 8, 2, LANES)] * 2
    return call(
        functools.partial(fine_relax_kernel, ends),
        outs,
        scratch,
        80_000_000,
        pos,
        own,
        *halos,
        fields,
    )


def restrict_rows(ref, scratch, rows, count):
    parts = []
    for c in range(5):
        for r in range(rows // 2):
            scratch[0:count] = ref[c, 2 * r] + ref[c, 2 * r + 1]
            parts.append(
                scratch[pl.ds(0, count // 2, stride=2)] + scratch[pl.ds(1, count // 2, stride=2)]
            )
    return jnp.concatenate(parts, axis=0)


def fine_residual_kernel(
    ends, pos, own, before, after, left, right, fields, out, w, prim, res, carry, shift, matrix,
    pair,
):
    for c in range(5):
        w[c, 0:2, 8:24] = before[c]
        w[c, 2:10, 8:24] = own[c]
        w[c, 10:12, 8:24] = after[c]
        w[c, 2:10, 6:8] = left[c]
        w[c, 2:10, 24:26] = right[c]

    def cross(at, to, source, step):
        @pl.when(pos[1] == at)
        def _():
            for k in range(2):
                for c in range(5):
                    x = w[c, 2:10, source + step * k : source + step * k + 1]
                    w[c, 2:10, to - step * k : to - step * k + 1] = -x if c == 2 else x

    cross(0, 7, 8, 1)
    cross(ends[1] - 1, 24, 23, -1)

    def axial(at, to, source, step):
        @pl.when(pos[0] == at)
        def _():
            for k in range(2):
                for c in range(5):
                    x = w[c, source + step * k]
                    w[c, to - step * k] = -x if c == 1 else x

    axial(0, 1, 2, 1)
    axial(ends[0] - 1, 10, 9, -1)
    fill_prim(w, prim, 0, 12)

    def sink(r, v, total, band):
        for c in range(5):
            res[c, r - 2] = 0.5 * total[c]

    level = Level(LANES, ShiftedRows(fields, 6), carry, shift, matrix)
    level.rows(w, prim, (2,), 8, Band(8, 16), sink)
    low = pick((LANES, LANES), lambda a, b: a // 2 == b)
    high = pick((LANES, LANES), lambda a, b: a // 2 + 64 == b)
    packed = matmul(0.125 * restrict_rows(own, pair, 8, 16), low)
    packed = packed + matmul(restrict_rows(res, pair, 8, 16), high)
    for c in range(5):
        for r in range(4):
            at = (c * 4 + r) * 8
            out[c, r] = packed[at : at + 8]


class ShiftedRows:
    def __init__(self, ref, by):
        self.ref, self.by = ref, by

    def __getitem__(self, index):
        c, r, cols = index
        return self.ref[c, r + self.by, cols]


def fine_residual(ends, pos, own, halos, fields):
    scratch = [vmem(5, 12, FINE_COLS, LANES), vmem(3, 12, FINE_COLS, LANES)]
    scratch += [vmem(5, 8, 16, LANES), vmem(1, 12, 16, LANES), vmem(2, 12, 32, LANES), MATRIX]
    scratch += [vmem(16, LANES)]
    return call(
        functools.partial(fine_residual_kernel, ends),
        [(5, 4, 8, LANES)],
        scratch,
        8_000_000,
        pos,
        own,
        *halos,
        fields,
    )


def middle_kernel(
    ends, pos, before2, before, own, after, after2, left, right, fields, out, diff,
    v0, wa, wb, force, prim_v, prim_a, prim_b, rate, res, carry, shift, matrix, pair,
):
    for k, ref in enumerate((before2, before, own, after, after2)):
        for c in range(5):
            v0[c, 4 * k : 4 * k + 4, 8:16] = ref[c]
    for c in range(5):
        v0[c, 2:18, 0:8] = left[c]
        v0[c, 2:18, 16:24] = right[c]
    begin = 4 * pos[0] - 8
    extent = 4 * ends[0]

    @pl.when((pos[0] < 2) | (pos[0] >= ends[0] - 2))
    def _():
        @pl.loop(0, 20)
        def _(r):
            at = mirror(begin + r, extent) - begin

            @pl.when(at != r)
            def _():
                for c in range(5):
                    x = v0[c, at, 0:24]
                    v0[c, r, 0:24] = -x if c == 1 else x

    def cross(at, to, source):
        @pl.when(pos[1] == at)
        def _():
            @pl.loop(0, 20)
            def _(r):
                for c in range(5):
                    x = flip8(v0[c, r, source : source + 8])
                    v0[c, r, to : to + 8] = -x if c == 2 else x

    cross(0, 0, 8)
    cross(ends[1] - 1, 16, 8)
    level = Level(64, fields, carry, shift, matrix)
    chain(level, MIDDLE_PLAN, 4.0, 20, 24, v0, wa, wb, force, prim_v, prim_a, prim_b, rate, 64)
    inner = pl.ds(8, 8)

    def sink(r, v, total, band):
        for c in range(5):
            res[c, r - 8] = 2.0 * (total[c] + force[c, r, inner])

    level.rows(wb, prim_a, (8,), 4, Band(8, 8), sink, 4)
    valid = lax.broadcasted_iota(jnp.int32, (8, LANES), 1) < 64
    for c in range(5):
        for r in range(4):
            x = wb[c, 8 + r, inner]
            diff[c, r] = jnp.where(valid, x - v0[c, 8 + r, inner], 0.0)
            res[c, r] = jnp.where(valid, res[c, r], 0.0)
            res[5 + c, r] = jnp.where(valid, x, 0.0)
    total = None
    for k, (ref, scale) in enumerate(((res.at[pl.ds(5, 5)], 0.125), (res.at[pl.ds(0, 5)], 1.0))):
        for r in range(2):
            parts = []
            for c in range(5):
                pair[0:8] = ref[c, 2 * r] + ref[c, 2 * r + 1]
                parts.append(
                    pair[pl.ds(0, 4, stride=2)] + pair[pl.ds(1, 4, stride=2)]
                )
                parts.append(jnp.zeros((4, LANES), jnp.float32))
            shift = 64 * r + 32 * k
            m = pick((LANES, LANES), lambda a, b, s=shift: (a // 2 + s == b) & (a < 64))
            part = matmul(scale * jnp.concatenate(parts, axis=0), m)
            total = part if total is None else total + part
    for k in range(out.shape[0]):
        for c in range(5):
            out[k, c] = total[8 * c : 8 * c + 4]


MIDDLE_PLAN = (
    (((6,), 8, Band(2, 20), 2), ((2, 14), 4, Band(6, 12), 1)),
    (((6,), 8, Band(4, 16), 2), ((4, 14), 2, Band(8, 8), 2)),
    (((8,), 4, Band(6, 12), 2), ((6, 12), 2, Band(8, 8), 2)),
)
COARSE_PLAN = (
    (((6,), 2, Band(2, 12), 2), ((2, 8), 4, Band(4, 8), 2)),
    (((4,), 6, Band(4, 8), 3),),
    (((6,), 2, Band(6, 4), 2),),
)


def chain(level, plan, area, rows, cols, v0, wa, wb, force, prim_v, prim_a, prim_b, rate, half):
    @pl.loop(0, rows, unroll=2)
    def _(r):
        every = pl.ds(0, cols)
        v = [v0[c, r, every] for c in range(5)]
        inv, pressure, sound = primitives(v)
        prim_v[0, r, every], prim_v[1, r, every], prim_v[2, r, every] = inv, pressure, sound
        scale = rate_row(v, pressure, sound, inv)
        rate[r, every] = scale
        new = []
        for c in range(5):
            total = (2.0 / area) * pltpu.roll(v[c], LANES - half, 1)
            force[c, r, every] = total
            new.append(v[c] - SEGMENT_WEIGHTS[0] * scale * total)
        store_row(wa, prim_a, r, every, new)

    def force_sink(r, v, total, band):
        for c in range(5):
            force[c, r, band.cols] = force[c, r, band.cols] - total[c]

    for begins, count, band, unroll in plan[0]:
        level.rows(v0, prim_v, begins, count, band, force_sink, unroll)
    source, source_prim = wa, prim_a
    for k in (1, 2, 3):
        target = (wb, wa, wb)[k - 1]
        target_prim = (prim_b, prim_v, prim_a)[k - 1]

        def sink(r, v, total, band, k=k, target=target, prim=target_prim):
            cols = band.cols
            scale = SEGMENT_WEIGHTS[k] * rate[r, cols]
            new = [v0[c, r, cols] - scale * (total[c] + force[c, r, cols]) for c in range(5)]
            store_row(target, prim, r, cols, new)

        for begins, count, band, unroll in plan[k - 1]:
            level.rows(source, source_prim, begins, count, band, sink, unroll)
        source, source_prim = target, target_prim


def middle(ends, pos, pieces, left, right, fields):
    cols = MIDDLE_COLS
    scratch = [vmem(5, 20, cols, LANES)] * 4 + [vmem(3, 20, cols, LANES)] * 3
    scratch += [vmem(20, cols, LANES), vmem(10, 4, 8, LANES), vmem(2, 12, 24, LANES)]
    scratch += [vmem(4, 12, 32, LANES), MATRIX, vmem(8, LANES)]
    return call(
        functools.partial(middle_kernel, ends),
        [(ends[0], 5, 4, LANES), (5, 4, 8, LANES)],
        scratch,
        60_000_000,
        pos,
        *pieces,
        left,
        right,
        fields,
    )


def coarse_kernel(
    ends, pos, own, left1, left2, right1, right2, fields, diff, smoothed, out,
    raw, v0, wa, wb, force, prim_v, prim_a, prim_b, rate, carry, shift, matrix, tall,
    wide,
):
    raw[...] = jnp.zeros_like(raw)
    for k, ref in enumerate((left2, left1, own, right1, right2)):
        for c in range(5):
            for b in range(7):
                at = (c * 7 + b) * LANES
                raw[4 * k : 4 * k + 4, at : at + LANES] = ref[c, b]
    first = 4 * pos[1] - 6
    extent = 4 * ends[1]
    j = lax.broadcasted_iota(jnp.int32, (16, 24), 0)
    s = lax.broadcasted_iota(jnp.int32, (16, 24), 1)
    cell = mirror(first + j, extent)
    moved = jnp.where(s == cell - first + 2, 1.0, 0.0)
    raw[0:16] = matmul(moved, raw[...])
    row = lax.broadcasted_iota(jnp.int32, (16, LANES), 0) + first
    cross_sign = jnp.where((row < 0) | (row >= extent), -1.0, 1.0)
    begin = 2 * pos[0] - 6
    ax_extent = 2 * ends[0]
    origin = 2 * jnp.clip(pos[0] - 3, 0, ends[0] - 7)

    @pl.loop(0, 14)
    def _(r):
        g = begin + r
        at = mirror(g, ax_extent)
        sign = jnp.where(at == g, 1.0, -1.0)
        block = (at - origin) // 2
        odd = (at - origin) % 2
        for c in range(5):
            x = raw[0:16, pl.ds(pl.multiple_of((c * 7 + block) * LANES, LANES), LANES)]
            x = jnp.where(odd == 1, pltpu.roll(x, 64, 1), x)
            if c == 1:
                x = x * sign
            if c == 2:
                x = x * cross_sign
            v0[c, r, 0:16] = x

    level = Level(32, fields, carry, shift, matrix)
    chain(level, COARSE_PLAN, 16.0, 14, 16, v0, wa, wb, force, prim_v, prim_a, prim_b, rate, 32)
    lane = lax.broadcasted_iota(jnp.int32, (16, LANES), 1)
    sub = lax.broadcasted_iota(jnp.int32, (16, LANES), 0)
    valid = (lane < 32) & (sub >= 6) & (sub < 10)
    parts = []
    for c in range(5):
        for r in range(2):
            parts.append(jnp.where(valid, wb[c, 6 + r, 0:16] - v0[c, 6 + r, 0:16], 0.0))
    wide[...] = matmul(
        jnp.concatenate(parts, axis=0), pick((LANES, LANES), lambda a, b: a == b // 4)
    )
    parts = [diff[c, r] for c in range(5) for r in range(4)]
    tall[...] = matmul(
        jnp.concatenate(parts, axis=0), pick((LANES, LANES), lambda a, b: a == b // 2)
    )
    four = pick((16, 16), lambda a, b: b == 6 + a // 4)
    two = pick((16, 8), lambda a, b: b == a // 2)
    for c in range(5):
        for r in range(2):
            at = (c * 2 + r) * 16
            big = matmul(four, wide[at : at + 16])
            for m in range(2):
                at = (c * 4 + 2 * r + m) * 8
                step = big + matmul(two, tall[at : at + 8])
                for n in range(2):
                    row = 4 * r + 2 * m + n
                    out[c, row] = smoothed[c, row] + step


def coarse(ends, pos, own, neighbours, fields, diff, smoothed):
    scratch = [vmem(24, 35 * LANES)]
    cols = COARSE_COLS
    scratch += [vmem(5, 14, cols, LANES)] * 4 + [vmem(3, 14, cols, LANES)] * 3
    scratch += [vmem(14, cols, LANES), vmem(2, 12, 16, LANES), vmem(4, 12, 24, LANES), MATRIX]
    scratch += [vmem(160, LANES), vmem(160, LANES)]
    return call(
        functools.partial(coarse_kernel, ends),
        [smoothed.shape],
        scratch,
        20_000_000,
        pos,
        own,
        *neighbours,
        fields,
        diff,
        smoothed,
    )


def shifted(x, axis, by):
    size = lax.axis_size(axis)
    return lax.ppermute(x, axis, [(i, i + by) for i in range(size) if 0 <= i + by < size])


def wide_halos(own):
    before = shifted(own, "ax", 1)
    after = shifted(own, "ax", -1)

    def slab(cols):
        return jnp.concatenate([before[:, 2:, cols], own[:, :, cols], after[:, :6, cols]], axis=1)

    left = shifted(slab(slice(8, 16)), "xs", 1)
    right = shifted(slab(slice(0, 8)), "xs", -1)
    return before, after, left, right


def wall_terms_kernel(factor, rows, count, origin, ends, pos, code, out, sides):
    extent = 8 * ends[0] // factor
    depth = 16 * ends[1] // factor
    scale = 1.0 / (factor * factor)
    begin = (8 // factor) * pos[0] - origin[0]
    first = (16 // factor) * pos[1] - origin[1]
    lane = lax.broadcasted_iota(jnp.int32, (count, LANES), 1)
    cell = mirror(lax.broadcasted_iota(jnp.int32, (count, LANES), 0) + first, depth)
    kinds = (1, 2, 0)

    def counts(r, kind, side):
        g = mirror(begin + r, extent)
        total = None
        for k in range(factor):
            hit = jnp.where(code[g * factor + k, side : side + 1] == kind, 1.0, 0.0)
            total = hit if total is None else total + hit
        return total

    if factor > 1:

        @pl.loop(0, rows, unroll=2)
        def _(r):
            for t, kind in enumerate(kinds):
                for side in range(2):
                    sides[pl.ds(r * 8 + 2 * t + side, 1)] = counts(r, kind, side)
            sides[pl.ds(r * 8 + 6, 2)] = jnp.zeros((2, LANES), jnp.float32)

        gather = pick((LANES, LANES), lambda a, b: a // factor == b)
        sides[...] = matmul(sides[...], gather)

    inside = cell == lane // factor

    @pl.loop(0, rows, unroll=2)
    def _(r):
        for t, kind in enumerate(kinds):
            edge = []
            for side in range(2):
                if factor > 1:
                    edge.append(sides[pl.ds(r * 8 + 2 * t + side, 1)])
                else:
                    edge.append(counts(r, kind, side))
            for side in (2, 3):
                line = jnp.broadcast_to(counts(r, kind, side), (count, LANES))
                edge.append(jnp.sum(jnp.where(inside, line, 0.0), axis=1, keepdims=True))
            total = jnp.where(cell == 0, edge[0], 0.0) + jnp.where(cell == depth - 1, edge[1], 0.0)
            total = total + jnp.where(lane == 0, edge[2], 0.0)
            total = total + jnp.where(lane == depth - 1, edge[3], 0.0)
            out[t, r] = scale * total


def wall_terms(ends, pos, code, factor, rows, count, origin):
    return call(
        functools.partial(wall_terms_kernel, factor, rows, count, origin, ends),
        [(3, rows, count, LANES)],
        [vmem(rows * 8, LANES)],
        1_000_000,
        pos,
        code,
    )


def per_device(state, wall_code):
    ends = (lax.axis_size("ax"), lax.axis_size("xs"))
    ax, xs = lax.axis_index("ax"), lax.axis_index("xs")
    pos = jnp.stack([ax, xs]).astype(jnp.int32)
    fine_fields = wall_terms(ends, pos, wall_code, 1, 24, FINE_COLS, (8, 8))
    middle_fields = wall_terms(ends, pos, wall_code, 2, 20, MIDDLE_COLS, (8, 8))
    coarse_fields = wall_terms(ends, pos, wall_code, 4, 14, COARSE_COLS, (6, 6))

    smoothed, high, low, last, first = fine_relax(
        ends, pos, state, wide_halos(state), fine_fields, True
    )
    halos = (
        shifted(high, "ax", 1),
        shifted(low, "ax", -1),
        shifted(last, "xs", 1),
        shifted(first, "xs", -1),
    )
    packed = fine_residual(ends, pos, smoothed, halos, fine_fields)

    pieces = [shifted(packed, "ax", by) for by in (2, 1)] + [packed]
    pieces += [shifted(packed, "ax", by) for by in (-1, -2)]
    slab = jnp.concatenate(
        [pieces[0][:, 2:], pieces[1], pieces[2], pieces[3], pieces[4][:, :2]], axis=1
    )
    block, diff = middle(
        ends, pos, pieces, shifted(slab, "xs", 1), shifted(slab, "xs", -1), middle_fields
    )

    column = lax.all_to_all(block, "ax", 0, 0)
    start = jnp.clip(ax - 3, 0, ends[0] - 7)
    column = lax.dynamic_slice_in_dim(column, start, 7, axis=0)
    column = jnp.transpose(column, (1, 0, 2, 3))
    neighbours = [shifted(column, "xs", by) for by in (1, 2, -1, -2)]
    fine_new = coarse(ends, pos, column, neighbours, coarse_fields, diff, smoothed)

    return fine_relax(ends, pos, fine_new, wide_halos(fine_new), fine_fields, False)


def solution(mesh):
    in_specs = (P(None, "ax", "xs", None), P())
    out_specs = P(None, "ax", "xs", None)
    return jax.shard_map(
        per_device, mesh=mesh, in_specs=in_specs, out_specs=out_specs, check_vma=False
    )
```

profile of v0, /device:TPU:3, one launch (start us, length us, event | category | flops | bytes accessed | tf_op | source)
XLA Modules:
  0.0 187.2 jit_solution(10213905602852297768)
XLA Ops:
  0.0 3.2 %collective-permute-start = (f32[5,8,16,128]{3,2,1,0:T(8,128)}, f32[5,8,16,128]{3,2,1,0:T(8,128)S(1)}, u32[]{:S(2)}, u32[]{:S(2)}) collective-permute-start(f32[5,8,16,128]{3,2,1,0:T(8,128)} %own.1), channel_id=1, source_target_pairs={{0,8},{8,16},{16,24},{24,32},{32,40},{40,48},{48,56},{56,64},{64,7... | collective-permute-start | bytes 983048 | tf_op jit(solution)/shard_map/ppermute | solution.py:716
  3.2 4.2 %collective-permute-start.1 = (f32[5,8,16,128]{3,2,1,0:T(8,128)}, f32[5,8,16,128]{3,2,1,0:T(8,128)S(1)}, u32[]{:S(2)}, u32[]{:S(2)}) collective-permute-start(f32[5,8,16,128]{3,2,1,0:T(8,128)} %own.1), channel_id=1, source_target_pairs={{8,0},{16,8},{24,16},{32,24},{40,32},{48,40},{56,48},{64,56},{72,6... | collective-permute-start | bytes 983048 | tf_op jit(solution)/shard_map/ppermute | solution.py:716
  7.4 1.0 fusion.4
  8.4 4.4 %collective-permute-done.before = f32[5,8,16,128]{3,2,1,0:T(8,128)S(1)} collective-permute-done((f32[5,8,16,128]{3,2,1,0:T(8,128)}, f32[5,8,16,128]{3,2,1,0:T(8,128)S(1)}, u32[]{:S(2)}, u32[]{:S(2)}) %collective-permute-start) | collective-permute-done | bytes 327712 | tf_op jit(solution)/shard_map/ppermute | solution.py:716
  12.8 1.0 collective-permute-done.1.after
  13.9 5.2 %collective-permute-start.2 = (f32[5,20,8,128]{3,2,1,0:T(8,128)S(1)}, f32[5,20,8,128]{3,2,1,0:T(8,128)S(1)}, u32[]{:S(2)}, u32[]{:S(2)}) collective-permute-start(f32[5,20,8,128]{3,2,1,0:T(8,128)S(1)} %pad_maximum_fusion), channel_id=1, source_target_pairs={{0,1},{1,2},{2,3},{3,4},{4,5},{5,6},{6,7},{8,9},{9,10},{10,11},{11... | collective-permute-start | bytes 1228808 | tf_op jit(solution)/shard_map/ppermute | solution.py:716
  19.2 1.9 %collective-permute-start.3 = (f32[5,20,8,128]{3,2,1,0:T(8,128)S(1)}, f32[5,20,8,128]{3,2,1,0:T(8,128)S(1)}, u32[]{:S(2)}, u32[]{:S(2)}) collective-permute-start(f32[5,20,8,128]{3,2,1,0:T(8,128)S(1)} %pad_maximum_fusion.1), channel_id=1, source_target_pairs={{1,0},{2,1},{3,2},{4,3},{5,4},{6,5},{7,6},{9,8},{10,9},{11,10},{12... | collective-permute-start | bytes 1228808 | tf_op jit(solution)/shard_map/ppermute | solution.py:716
  21.1 0.6 pad_add_fusion.pos
  21.7 3.8 %shard_map.28.fields = f32[3,24,40,128]{3,2,1,0:T(8,128)} custom-call(s32[2]{0:T(128)} %pad_add_fusion.pos, s32[128,4,128]{2,1,0:T(4,128)} %code.5), custom_call_target="tpu_custom_call" | custom-call | flops 1000000 | bytes 1736712 | tf_op jit(solution)/shard_map/pallas_call | solution.py:364
  25.5 0.0 collective-permute-done.2.left
  25.5 2.9 %collective-permute-done.3.right = f32[5,20,8,128]{3,2,1,0:T(8,128)S(1)} collective-permute-done((f32[5,20,8,128]{3,2,1,0:T(8,128)S(1)}, f32[5,20,8,128]{3,2,1,0:T(8,128)S(1)}, u32[]{:S(2)}, u32[]{:S(2)}) %collective-permute-start.3) | collective-permute-done | bytes 409632 | tf_op jit(solution)/shard_map/ppermute | solution.py:716
  28.4 0.8 copy-done.5
  29.2 15.9 %shard_map.29 = (f32[5,8,16,128]{3,2,1,0:T(8,128)}, f32[5,2,16,128]{3,2,1,0:T(8,128)}, f32[5,2,16,128]{3,2,1,0:T(8,128)}, f32[5,8,2,128]{3,2,1,0:T(2,128)}, f32[5,8,2,128]{3,2,1,0:T(2,128)}) custom-call(s32[2]{0:T(128)} %pad_add_fusion.pos, f32[5,8,16,128]{3,2,1,0:T(8,128)} %own.1, f32[5,8,16,128]{3,2,1,0:T(8,128)} %copy-done, f32[5,8,16,128]{3,2,1,0:T(8,128)} %copy-done.1, ...), custom_call_target="tpu_custom_call" | custom-call | flops 80000000 | bytes 3850248 | tf_op jit(solution)/shard_map/pallas_call | solution.py:364
  45.1 3.0 %collective-permute-start.4 = (f32[5,2,16,128]{3,2,1,0:T(8,128)}, f32[5,2,16,128]{3,2,1,0:T(8,128)S(1)}, u32[]{:S(2)}, u32[]{:S(2)}) collective-permute-start(f32[5,2,16,128]{3,2,1,0:T(8,128)} %get-tuple-element.13), channel_id=1, source_target_pairs={{0,8},{8,16},{16,24},{24,32},{32,40},{40,48},{48,56},{56,64},{64,7... | collective-permute-start | bytes 245768 | tf_op jit(solution)/shard_map/ppermute | solution.py:716
  48.1 5.0 %collective-permute-start.5 = (f32[5,2,16,128]{3,2,1,0:T(8,128)}, f32[5,2,16,128]{3,2,1,0:T(8,128)S(1)}, u32[]{:S(2)}, u32[]{:S(2)}) collective-permute-start(f32[5,2,16,128]{3,2,1,0:T(8,128)} %get-tuple-element.14), channel_id=1, source_target_pairs={{8,0},{16,8},{24,16},{32,24},{40,32},{48,40},{56,48},{64,56},{72,6... | collective-permute-start | bytes 245768 | tf_op jit(solution)/shard_map/ppermute | solution.py:716
  53.2 2.0 %collective-permute-start.6 = (f32[5,8,2,128]{3,2,1,0:T(2,128)}, f32[5,8,2,128]{3,2,1,0:T(2,128)S(1)}, u32[]{:S(2)}, u32[]{:S(2)}) collective-permute-start(f32[5,8,2,128]{3,2,1,0:T(2,128)} %get-tuple-element.15), channel_id=1, source_target_pairs={{0,1},{1,2},{2,3},{3,4},{4,5},{5,6},{6,7},{8,9},{9,10},{10,11},{11... | collective-permute-start | bytes 122888 | tf_op jit(solution)/shard_map/ppermute | solution.py:716
  55.2 2.3 %collective-permute-start.7 = (f32[5,8,2,128]{3,2,1,0:T(2,128)}, f32[5,8,2,128]{3,2,1,0:T(2,128)S(1)}, u32[]{:S(2)}, u32[]{:S(2)}) collective-permute-start(f32[5,8,2,128]{3,2,1,0:T(2,128)} %get-tuple-element.16), channel_id=1, source_target_pairs={{1,0},{2,1},{3,2},{4,3},{5,4},{6,5},{7,6},{9,8},{10,9},{11,10},{12... | collective-permute-start | bytes 122888 | tf_op jit(solution)/shard_map/ppermute | solution.py:716
  57.5 0.0 collective-permute-done.6.left
  57.5 3.4 %collective-permute-done.7.right = f32[5,8,2,128]{3,2,1,0:T(2,128)S(1)} collective-permute-done((f32[5,8,2,128]{3,2,1,0:T(2,128)}, f32[5,8,2,128]{3,2,1,0:T(2,128)S(1)}, u32[]{:S(2)}, u32[]{:S(2)}) %collective-permute-start.7) | collective-permute-done | bytes 40992 | tf_op jit(solution)/shard_map/ppermute | solution.py:716
  60.9 0.0 collective-permute-done.4.before
  60.9 0.0 collective-permute-done.5.after
  60.9 0.6 copy-done.22
  61.5 0.0 copy-done.15
  61.5 0.0 copy-done.16
  61.6 4.4 %shard_map.30.own = f32[5,4,8,128]{3,2,1,0:T(8,128)} custom-call(s32[2]{0:T(128)} %pad_add_fusion.pos, f32[5,8,16,128]{3,2,1,0:T(8,128)} %get-tuple-element.12.own.smoothed, f32[5,2,16,128]{3,2,1,0:T(8,128)} %copy-done.15, f32[5,2,16,128]{3,2,1,0:T(8,128)} %copy-done.16, f32[5,8,2,128]{3,2,1,0:T(2,128)} %copy-done.21, f32[5,8,2,128]{3,2,1,0:T(2,128)} %copy-done.22, ...), custom_call_target="tpu_custom_call" | custom-call | flops 8000000 | bytes 2129928 | tf_op jit(solution)/shard_map/pallas_call | solution.py:364
  66.0 3.1 %collective-permute-start.8 = (f32[5,4,8,128]{3,2,1,0:T(8,128)}, f32[5,4,8,128]{3,2,1,0:T(8,128)S(1)}, u32[]{:S(2)}, u32[]{:S(2)}) collective-permute-start(f32[5,4,8,128]{3,2,1,0:T(8,128)} %shard_map.30.own), channel_id=1, source_target_pairs={{0,16},{8,24},{16,32},{24,40},{32,48},{40,56},{48,64},{56,72},{64,... | collective-permute-start | bytes 245768 | tf_op jit(solution)/shard_map/ppermute | solution.py:716
  69.1 2.9 %collective-permute-start.9 = (f32[5,4,8,128]{3,2,1,0:T(8,128)}, f32[5,4,8,128]{3,2,1,0:T(8,128)S(1)}, u32[]{:S(2)}, u32[]{:S(2)}) collective-permute-start(f32[5,4,8,128]{3,2,1,0:T(8,128)} %shard_map.30.own), channel_id=1, source_target_pairs={{0,8},{8,16},{16,24},{24,32},{32,40},{40,48},{48,56},{56,64},{64,7... | collective-permute-start | bytes 245768 | tf_op jit(solution)/shard_map/ppermute | solution.py:716
  72.0 4.5 %collective-permute-start.10 = (f32[5,4,8,128]{3,2,1,0:T(8,128)}, f32[5,4,8,128]{3,2,1,0:T(8,128)S(1)}, u32[]{:S(2)}, u32[]{:S(2)}) collective-permute-start(f32[5,4,8,128]{3,2,1,0:T(8,128)} %shard_map.30.own), channel_id=1, source_target_pairs={{8,0},{16,8},{24,16},{32,24},{40,32},{48,40},{56,48},{64,56},{72,6... | collective-permute-start | bytes 245768 | tf_op jit(solution)/shard_map/ppermute | solution.py:716
  76.5 2.5 %collective-permute-start.11 = (f32[5,4,8,128]{3,2,1,0:T(8,128)}, f32[5,4,8,128]{3,2,1,0:T(8,128)S(1)}, u32[]{:S(2)}, u32[]{:S(2)}) collective-permute-start(f32[5,4,8,128]{3,2,1,0:T(8,128)} %shard_map.30.own), channel_id=1, source_target_pairs={{16,0},{24,8},{32,16},{40,24},{48,32},{56,40},{64,48},{72,56},{80,... | collective-permute-start | bytes 245768 | tf_op jit(solution)/shard_map/ppermute | solution.py:716
  79.0 0.0 collective-permute-done.8.before2
  79.0 0.0 collective-permute-done.9.before
  79.0 0.9 constant_dynamic-update-slice_fusion.1
  80.0 0.0 collective-permute-done.10.after
  80.0 3.6 %collective-permute-done.11.after2 = f32[5,4,8,128]{3,2,1,0:T(8,128)S(1)} collective-permute-done((f32[5,4,8,128]{3,2,1,0:T(8,128)}, f32[5,4,8,128]{3,2,1,0:T(8,128)S(1)}, u32[]{:S(2)}, u32[]{:S(2)}) %collective-permute-start.11) | collective-permute-done | bytes 81952 | tf_op jit(solution)/shard_map/ppermute | solution.py:716
  83.6 4.6 %collective-permute-start.12 = (f32[5,16,8,128]{3,2,1,0:T(8,128)S(1)}, f32[5,16,8,128]{3,2,1,0:T(8,128)S(1)}, u32[]{:S(2)}, u32[]{:S(2)}) collective-permute-start(f32[5,16,8,128]{3,2,1,0:T(8,128)S(1)} %slice_dynamic-update-slice_fusion), channel_id=1, source_target_pairs={{0,1},{1,2},{2,3},{3,4},{4,5},{5,6},{6,7},{8,9},{9,10},{10,11},{11... | collective-permute-start | bytes 983048 | tf_op jit(solution)/shard_map/ppermute | solution.py:716
  88.2 1.9 %collective-permute-start.13 = (f32[5,16,8,128]{3,2,1,0:T(8,128)S(1)}, f32[5,16,8,128]{3,2,1,0:T(8,128)S(1)}, u32[]{:S(2)}, u32[]{:S(2)}) collective-permute-start(f32[5,16,8,128]{3,2,1,0:T(8,128)S(1)} %slice_dynamic-update-slice_fusion), channel_id=1, source_target_pairs={{1,0},{2,1},{3,2},{4,3},{5,4},{6,5},{7,6},{9,8},{10,9},{11,10},{12... | collective-permute-start | bytes 983048 | tf_op jit(solution)/shard_map/ppermute | solution.py:716
  90.2 3.6 %shard_map.31.fields = f32[3,20,32,128]{3,2,1,0:T(8,128)} custom-call(s32[2]{0:T(128)} %pad_add_fusion.pos, s32[128,4,128]{2,1,0:T(4,128)} %code.5), custom_call_target="tpu_custom_call" | custom-call | flops 1000000 | bytes 1245192 | tf_op jit(solution)/shard_map/pallas_call | solution.py:364
  93.8 2.9 %collective-permute-done.13.right = f32[5,16,8,128]{3,2,1,0:T(8,128)S(1)} collective-permute-done((f32[5,16,8,128]{3,2,1,0:T(8,128)S(1)}, f32[5,16,8,128]{3,2,1,0:T(8,128)S(1)}, u32[]{:S(2)}, u32[]{:S(2)}) %collective-permute-start.13) | collective-permute-done | bytes 327712 | tf_op jit(solution)/shard_map/ppermute | solution.py:716
  96.7 0.7 copy-done.11
  97.4 13.4 %shard_map.32 = (f32[16,5,4,128]{3,2,1,0:T(4,128)}, f32[5,4,8,128]{3,2,1,0:T(8,128)}) custom-call(s32[2]{0:T(128)} %pad_add_fusion.pos, f32[5,4,8,128]{3,2,1,0:T(8,128)} %copy-done.13, f32[5,4,8,128]{3,2,1,0:T(8,128)} %copy-done.8, f32[5,4,8,128]{3,2,1,0:T(8,128)} %shard_map.30.own, f32[5,4,8,128]{3,2,1,0:T(8,128)} %copy-done.9, ...), custom_call_target="tpu_custom_call" | custom-call | flops 60000000 | bytes 2293768 | tf_op jit(solution)/shard_map/pallas_call | solution.py:364
  110.8 5.2 %all-to-all-start = ((f32[16,5,4,128]{3,2,1,0:T(4,128)}), f32[16,5,4,128]{3,2,1,0:T(4,128)S(1)}, u32[]{:S(2)}, u32[]{:S(2)}) async-start(f32[16,5,4,128]{3,2,1,0:T(4,128)} %get-tuple-element.17), calls=%async_computation | async-start | bytes 327680 | tf_op jit(solution)/shard_map/all_to_all | solution.py:820
  116.0 5.6 %all-to-all-done = f32[16,5,4,128]{3,2,1,0:T(4,128)S(1)} async-done(((f32[16,5,4,128]{3,2,1,0:T(4,128)}), f32[16,5,4,128]{3,2,1,0:T(4,128)S(1)}, u32[]{:S(2)}, u32[]{:S(2)}) %all-to-all-start) | async-done | bytes 163872 | tf_op jit(solution)/shard_map/all_to_all | solution.py:820
  121.6 0.0 copy-start.12
  121.6 3.3 %collective-permute-start.14 = (f32[5,7,4,128]{3,2,1,0:T(4,128)S(1)}, f32[5,7,4,128]{3,2,1,0:T(4,128)S(1)}, u32[]{:S(2)}, u32[]{:S(2)}) collective-permute-start(f32[5,7,4,128]{3,2,1,0:T(4,128)S(1)} %copy_bitcast_fusion.own), channel_id=1, source_target_pairs={{0,1},{1,2},{2,3},{3,4},{4,5},{5,6},{6,7},{8,9},{9,10},{10,11},{11... | collective-permute-start | bytes 215048 | tf_op jit(solution)/shard_map/ppermute | solution.py:716
  124.9 3.7 %collective-permute-start.15 = (f32[5,7,4,128]{3,2,1,0:T(4,128)S(1)}, f32[5,7,4,128]{3,2,1,0:T(4,128)S(1)}, u32[]{:S(2)}, u32[]{:S(2)}) collective-permute-start(f32[5,7,4,128]{3,2,1,0:T(4,128)S(1)} %copy_bitcast_fusion.own), channel_id=1, source_target_pairs={{0,2},{1,3},{2,4},{3,5},{4,6},{5,7},{8,10},{9,11},{10,12},{11,13},... | collective-permute-start | bytes 215048 | tf_op jit(solution)/shard_map/ppermute | solution.py:716
  128.6 1.9 %collective-permute-start.16 = (f32[5,7,4,128]{3,2,1,0:T(4,128)S(1)}, f32[5,7,4,128]{3,2,1,0:T(4,128)S(1)}, u32[]{:S(2)}, u32[]{:S(2)}) collective-permute-start(f32[5,7,4,128]{3,2,1,0:T(4,128)S(1)} %copy_bitcast_fusion.own), channel_id=1, source_target_pairs={{1,0},{2,1},{3,2},{4,3},{5,4},{6,5},{7,6},{9,8},{10,9},{11,10},{12... | collective-permute-start | bytes 215048 | tf_op jit(solution)/shard_map/ppermute | solution.py:716
  130.5 1.5 collective-permute-start.17
  132.0 3.0 %shard_map.33.fields = f32[3,14,24,128]{3,2,1,0:T(8,128)} custom-call(s32[2]{0:T(128)} %pad_add_fusion.pos, s32[128,4,128]{2,1,0:T(4,128)} %code.5), custom_call_target="tpu_custom_call" | custom-call | flops 1000000 | bytes 778248 | tf_op jit(solution)/shard_map/pallas_call | solution.py:364
  135.0 0.0 collective-permute-done.14.left1
  135.0 0.0 collective-permute-done.15.left2
  135.1 1.0 collective-permute-done.17.right2
  136.1 0.6 copy-done.20
  136.7 8.5 %shard_map.34.own = f32[5,8,16,128]{3,2,1,0:T(8,128)} custom-call(s32[2]{0:T(128)} %pad_add_fusion.pos, f32[5,7,4,128]{3,2,1,0:T(4,128)} %copy-done.12, f32[5,7,4,128]{3,2,1,0:T(4,128)} %copy-done.17, f32[5,7,4,128]{3,2,1,0:T(4,128)} %copy-done.18, f32[5,7,4,128]{3,2,1,0:T(4,128)} %copy-done.19, f32[5,7,4,128]{3,2,1,0:T(4,128)} %copy-done.20, ...), custom_call_target="tpu_custom_call" | custom-call | flops 20000000 | bytes 1611784 | tf_op jit(solution)/shard_map/pallas_call | solution.py:364
  145.2 2.1 %collective-permute-start.18 = (f32[5,8,16,128]{3,2,1,0:T(8,128)}, f32[5,8,16,128]{3,2,1,0:T(8,128)S(1)}, u32[]{:S(2)}, u32[]{:S(2)}) collective-permute-start(f32[5,8,16,128]{3,2,1,0:T(8,128)} %shard_map.34.own), channel_id=1, source_target_pairs={{0,8},{8,16},{16,24},{24,32},{32,40},{40,48},{48,56},{56,64},{64,7... | collective-permute-start | bytes 983048 | tf_op jit(solution)/shard_map/ppermute | solution.py:716
  147.2 5.3 %collective-permute-start.19 = (f32[5,8,16,128]{3,2,1,0:T(8,128)}, f32[5,8,16,128]{3,2,1,0:T(8,128)S(1)}, u32[]{:S(2)}, u32[]{:S(2)}) collective-permute-start(f32[5,8,16,128]{3,2,1,0:T(8,128)} %shard_map.34.own), channel_id=1, source_target_pairs={{8,0},{16,8},{24,16},{32,24},{40,32},{48,40},{56,48},{64,56},{72,6... | collective-permute-start | bytes 983048 | tf_op jit(solution)/shard_map/ppermute | solution.py:716
  152.6 1.0 fusion.1
  153.6 4.1 %collective-permute-done.18.before = f32[5,8,16,128]{3,2,1,0:T(8,128)S(1)} collective-permute-done((f32[5,8,16,128]{3,2,1,0:T(8,128)}, f32[5,8,16,128]{3,2,1,0:T(8,128)S(1)}, u32[]{:S(2)}, u32[]{:S(2)}) %collective-permute-start.18) | collective-permute-done | bytes 327712 | tf_op jit(solution)/shard_map/ppermute | solution.py:716
  157.7 1.0 collective-permute-done.19.after
  158.7 4.0 %collective-permute-start.21 = (f32[5,20,8,128]{3,2,1,0:T(8,128)S(1)}, f32[5,20,8,128]{3,2,1,0:T(8,128)S(1)}, u32[]{:S(2)}, u32[]{:S(2)}) collective-permute-start(f32[5,20,8,128]{3,2,1,0:T(8,128)S(1)} %pad_maximum_fusion.3), channel_id=1, source_target_pairs={{1,0},{2,1},{3,2},{4,3},{5,4},{6,5},{7,6},{9,8},{10,9},{11,10},{12... | collective-permute-start | bytes 1228808 | tf_op jit(solution)/shard_map/ppermute | solution.py:716
  162.8 2.9 %collective-permute-start.20 = (f32[5,20,8,128]{3,2,1,0:T(8,128)S(1)}, f32[5,20,8,128]{3,2,1,0:T(8,128)S(1)}, u32[]{:S(2)}, u32[]{:S(2)}) collective-permute-start(f32[5,20,8,128]{3,2,1,0:T(8,128)S(1)} %pad_maximum_fusion.2), channel_id=1, source_target_pairs={{0,1},{1,2},{2,3},{3,4},{4,5},{5,6},{6,7},{8,9},{9,10},{10,11},{11... | collective-permute-start | bytes 1228808 | tf_op jit(solution)/shard_map/ppermute | solution.py:716
  165.7 3.7 %collective-permute-done.21.right = f32[5,20,8,128]{3,2,1,0:T(8,128)S(1)} collective-permute-done((f32[5,20,8,128]{3,2,1,0:T(8,128)S(1)}, f32[5,20,8,128]{3,2,1,0:T(8,128)S(1)}, u32[]{:S(2)}, u32[]{:S(2)}) %collective-permute-start.21) | collective-permute-done | bytes 409632 | tf_op jit(solution)/shard_map/ppermute | solution.py:716
  169.4 1.2 collective-permute-done.20.left
  170.6 0.7 copy-done.7
  171.3 15.8 %shard_map.35 = f32[5,8,16,128]{3,2,1,0:T(8,128)} custom-call(s32[2]{0:T(128)} %pad_add_fusion.pos, f32[5,8,16,128]{3,2,1,0:T(8,128)} %shard_map.34.own, f32[5,8,16,128]{3,2,1,0:T(8,128)} %copy-done.2, f32[5,8,16,128]{3,2,1,0:T(8,128)} %copy-done.3, f32[5,20,8,128]{3,2,1,0:T(8,128)} %copy-done.7, f32[5,20,8,128]{3,2,1,0:T(8,128)} %copy-done.6, ...), custom_call_target="tpu_custom_call" | custom-call | flops 80000000 | bytes 3604488 | tf_op jit(solution)/shard_map/pallas_call | solution.py:364
  (53 shorter events, 0.3 us)
Async XLA Ops:
  0.0 12.8 %collective-permute-start = (f32[5,8,16,128]{3,2,1,0:T(8,128)}, f32[5,8,16,128]{3,2,1,0:T(8,128)S(1)}, u32[]{:S(2)}, u32[]{:S(2)}) collective-permute-start(f32[5,8,16,128]{3,2,1,0:T(8,128)} %own.1), channel_id=1, source_target_pairs={{0,8},{8,16},{16,24},{24,32},{32,40},{40,48},{48,56},{56,64},{64,7... | collective-permute-start | bytes 983048 | tf_op jit(solution)/shard_map/ppermute | solution.py:716
  3.2 10.6 %collective-permute-start.1 = (f32[5,8,16,128]{3,2,1,0:T(8,128)}, f32[5,8,16,128]{3,2,1,0:T(8,128)S(1)}, u32[]{:S(2)}, u32[]{:S(2)}) collective-permute-start(f32[5,8,16,128]{3,2,1,0:T(8,128)} %own.1), channel_id=1, source_target_pairs={{8,0},{16,8},{24,16},{32,24},{40,32},{48,40},{56,48},{64,56},{72,6... | collective-permute-start | bytes 983048 | tf_op jit(solution)/shard_map/ppermute | solution.py:716
  12.8 12.7 %copy-start = (f32[5,8,16,128]{3,2,1,0:T(8,128)}, f32[5,8,16,128]{3,2,1,0:T(8,128)S(1)}, u32[]{:S(2)}) copy-start(f32[5,8,16,128]{3,2,1,0:T(8,128)S(1)} %collective-permute-done.before) | copy-start | bytes 983044
  13.8 11.7 %copy-start.1 = (f32[5,8,16,128]{3,2,1,0:T(8,128)}, f32[5,8,16,128]{3,2,1,0:T(8,128)S(1)}, u32[]{:S(2)}) copy-start(f32[5,8,16,128]{3,2,1,0:T(8,128)S(1)} %collective-permute-done.1.after) | copy-start | bytes 983044
  13.9 11.6 %collective-permute-start.2 = (f32[5,20,8,128]{3,2,1,0:T(8,128)S(1)}, f32[5,20,8,128]{3,2,1,0:T(8,128)S(1)}, u32[]{:S(2)}, u32[]{:S(2)}) collective-permute-start(f32[5,20,8,128]{3,2,1,0:T(8,128)S(1)} %pad_maximum_fusion), channel_id=1, source_target_pairs={{0,1},{1,2},{2,3},{3,4},{4,5},{5,6},{6,7},{8,9},{9,10},{10,11},{11... | collective-permute-start | bytes 1228808 | tf_op jit(solution)/shard_map/ppermute | solution.py:716
  19.2 9.3 %collective-permute-start.3 = (f32[5,20,8,128]{3,2,1,0:T(8,128)S(1)}, f32[5,20,8,128]{3,2,1,0:T(8,128)S(1)}, u32[]{:S(2)}, u32[]{:S(2)}) collective-permute-start(f32[5,20,8,128]{3,2,1,0:T(8,128)S(1)} %pad_maximum_fusion.1), channel_id=1, source_target_pairs={{1,0},{2,1},{3,2},{4,3},{5,4},{6,5},{7,6},{9,8},{10,9},{11,10},{12... | collective-permute-start | bytes 1228808 | tf_op jit(solution)/shard_map/ppermute | solution.py:716
  25.5 2.9 %copy-start.4 = (f32[5,20,8,128]{3,2,1,0:T(8,128)}, f32[5,20,8,128]{3,2,1,0:T(8,128)S(1)}, u32[]{:S(2)}) copy-start(f32[5,20,8,128]{3,2,1,0:T(8,128)S(1)} %collective-permute-done.2.left) | copy-start | bytes 1228804
  28.4 0.8 copy-start.5
  45.1 15.8 %collective-permute-start.4 = (f32[5,2,16,128]{3,2,1,0:T(8,128)}, f32[5,2,16,128]{3,2,1,0:T(8,128)S(1)}, u32[]{:S(2)}, u32[]{:S(2)}) collective-permute-start(f32[5,2,16,128]{3,2,1,0:T(8,128)} %get-tuple-element.13), channel_id=1, source_target_pairs={{0,8},{8,16},{16,24},{24,32},{32,40},{40,48},{48,56},{56,64},{64,7... | collective-permute-start | bytes 245768 | tf_op jit(solution)/shard_map/ppermute | solution.py:716
  48.1 12.8 %collective-permute-start.5 = (f32[5,2,16,128]{3,2,1,0:T(8,128)}, f32[5,2,16,128]{3,2,1,0:T(8,128)S(1)}, u32[]{:S(2)}, u32[]{:S(2)}) collective-permute-start(f32[5,2,16,128]{3,2,1,0:T(8,128)} %get-tuple-element.14), channel_id=1, source_target_pairs={{8,0},{16,8},{24,16},{32,24},{40,32},{48,40},{56,48},{64,56},{72,6... | collective-permute-start | bytes 245768 | tf_op jit(solution)/shard_map/ppermute | solution.py:716
  53.2 4.3 %collective-permute-start.6 = (f32[5,8,2,128]{3,2,1,0:T(2,128)}, f32[5,8,2,128]{3,2,1,0:T(2,128)S(1)}, u32[]{:S(2)}, u32[]{:S(2)}) collective-permute-start(f32[5,8,2,128]{3,2,1,0:T(2,128)} %get-tuple-element.15), channel_id=1, source_target_pairs={{0,1},{1,2},{2,3},{3,4},{4,5},{5,6},{6,7},{8,9},{9,10},{10,11},{11... | collective-permute-start | bytes 122888 | tf_op jit(solution)/shard_map/ppermute | solution.py:716
  55.2 5.7 %collective-permute-start.7 = (f32[5,8,2,128]{3,2,1,0:T(2,128)}, f32[5,8,2,128]{3,2,1,0:T(2,128)S(1)}, u32[]{:S(2)}, u32[]{:S(2)}) collective-permute-start(f32[5,8,2,128]{3,2,1,0:T(2,128)} %get-tuple-element.16), channel_id=1, source_target_pairs={{1,0},{2,1},{3,2},{4,3},{5,4},{6,5},{7,6},{9,8},{10,9},{11,10},{12... | collective-permute-start | bytes 122888 | tf_op jit(solution)/shard_map/ppermute | solution.py:716
  57.5 3.4 %copy-start.21 = (f32[5,8,2,128]{3,2,1,0:T(2,128)}, f32[5,8,2,128]{3,2,1,0:T(2,128)S(1)}, u32[]{:S(2)}) copy-start(f32[5,8,2,128]{3,2,1,0:T(2,128)S(1)} %collective-permute-done.6.left) | copy-start | bytes 122884
  60.9 0.6 copy-start.22
  60.9 0.6 copy-start.15
  60.9 0.7 copy-start.16
  66.0 13.0 %collective-permute-start.8 = (f32[5,4,8,128]{3,2,1,0:T(8,128)}, f32[5,4,8,128]{3,2,1,0:T(8,128)S(1)}, u32[]{:S(2)}, u32[]{:S(2)}) collective-permute-start(f32[5,4,8,128]{3,2,1,0:T(8,128)} %shard_map.30.own), channel_id=1, source_target_pairs={{0,16},{8,24},{16,32},{24,40},{32,48},{40,56},{48,64},{56,72},{64,... | collective-permute-start | bytes 245768 | tf_op jit(solution)/shard_map/ppermute | solution.py:716
  69.1 9.9 %collective-permute-start.9 = (f32[5,4,8,128]{3,2,1,0:T(8,128)}, f32[5,4,8,128]{3,2,1,0:T(8,128)S(1)}, u32[]{:S(2)}, u32[]{:S(2)}) collective-permute-start(f32[5,4,8,128]{3,2,1,0:T(8,128)} %shard_map.30.own), channel_id=1, source_target_pairs={{0,8},{8,16},{16,24},{24,32},{32,40},{40,48},{48,56},{56,64},{64,7... | collective-permute-start | bytes 245768 | tf_op jit(solution)/shard_map/ppermute | solution.py:716
  72.0 8.0 %collective-permute-start.10 = (f32[5,4,8,128]{3,2,1,0:T(8,128)}, f32[5,4,8,128]{3,2,1,0:T(8,128)S(1)}, u32[]{:S(2)}, u32[]{:S(2)}) collective-permute-start(f32[5,4,8,128]{3,2,1,0:T(8,128)} %shard_map.30.own), channel_id=1, source_target_pairs={{8,0},{16,8},{24,16},{32,24},{40,32},{48,40},{56,48},{64,56},{72,6... | collective-permute-start | bytes 245768 | tf_op jit(solution)/shard_map/ppermute | solution.py:716
  76.5 7.1 %collective-permute-start.11 = (f32[5,4,8,128]{3,2,1,0:T(8,128)}, f32[5,4,8,128]{3,2,1,0:T(8,128)S(1)}, u32[]{:S(2)}, u32[]{:S(2)}) collective-permute-start(f32[5,4,8,128]{3,2,1,0:T(8,128)} %shard_map.30.own), channel_id=1, source_target_pairs={{16,0},{24,8},{32,16},{40,24},{48,32},{56,40},{64,48},{72,56},{80,... | collective-permute-start | bytes 245768 | tf_op jit(solution)/shard_map/ppermute | solution.py:716
  79.0 17.6 %copy-start.13 = (f32[5,4,8,128]{3,2,1,0:T(8,128)}, f32[5,4,8,128]{3,2,1,0:T(8,128)S(1)}, u32[]{:S(2)}) copy-start(f32[5,4,8,128]{3,2,1,0:T(8,128)S(1)} %collective-permute-done.8.before2) | copy-start | bytes 245764
  79.0 17.6 %copy-start.8 = (f32[5,4,8,128]{3,2,1,0:T(8,128)}, f32[5,4,8,128]{3,2,1,0:T(8,128)S(1)}, u32[]{:S(2)}) copy-start(f32[5,4,8,128]{3,2,1,0:T(8,128)S(1)} %collective-permute-done.9.before) | copy-start | bytes 245764
  80.0 16.7 %copy-start.9 = (f32[5,4,8,128]{3,2,1,0:T(8,128)}, f32[5,4,8,128]{3,2,1,0:T(8,128)S(1)}, u32[]{:S(2)}) copy-start(f32[5,4,8,128]{3,2,1,0:T(8,128)S(1)} %collective-permute-done.10.after) | copy-start | bytes 245764
  83.6 13.0 %copy-start.14 = (f32[5,4,8,128]{3,2,1,0:T(8,128)}, f32[5,4,8,128]{3,2,1,0:T(8,128)S(1)}, u32[]{:S(2)}) copy-start(f32[5,4,8,128]{3,2,1,0:T(8,128)S(1)} %collective-permute-done.11.after2) | copy-start | bytes 245764
  83.6 10.1 %collective-permute-start.12 = (f32[5,16,8,128]{3,2,1,0:T(8,128)S(1)}, f32[5,16,8,128]{3,2,1,0:T(8,128)S(1)}, u32[]{:S(2)}, u32[]{:S(2)}) collective-permute-start(f32[5,16,8,128]{3,2,1,0:T(8,128)S(1)} %slice_dynamic-update-slice_fusion), channel_id=1, source_target_pairs={{0,1},{1,2},{2,3},{3,4},{4,5},{5,6},{6,7},{8,9},{9,10},{10,11},{11... | collective-permute-start | bytes 983048 | tf_op jit(solution)/shard_map/ppermute | solution.py:716
  88.2 8.4 %collective-permute-start.13 = (f32[5,16,8,128]{3,2,1,0:T(8,128)S(1)}, f32[5,16,8,128]{3,2,1,0:T(8,128)S(1)}, u32[]{:S(2)}, u32[]{:S(2)}) collective-permute-start(f32[5,16,8,128]{3,2,1,0:T(8,128)S(1)} %slice_dynamic-update-slice_fusion), channel_id=1, source_target_pairs={{1,0},{2,1},{3,2},{4,3},{5,4},{6,5},{7,6},{9,8},{10,9},{11,10},{12... | collective-permute-start | bytes 983048 | tf_op jit(solution)/shard_map/ppermute | solution.py:716
  93.8 2.9 %copy-start.10 = (f32[5,16,8,128]{3,2,1,0:T(8,128)}, f32[5,16,8,128]{3,2,1,0:T(8,128)S(1)}, u32[]{:S(2)}) copy-start(f32[5,16,8,128]{3,2,1,0:T(8,128)S(1)} %collective-permute-done.12.left) | copy-start | bytes 983044
  96.7 0.7 copy-start.11
  110.8 10.8 %all-to-all-start = ((f32[16,5,4,128]{3,2,1,0:T(4,128)}), f32[16,5,4,128]{3,2,1,0:T(4,128)S(1)}, u32[]{:S(2)}, u32[]{:S(2)}) async-start(f32[16,5,4,128]{3,2,1,0:T(4,128)} %get-tuple-element.17), calls=%async_computation | async-start | bytes 327680 | tf_op jit(solution)/shard_map/all_to_all | solution.py:820
  121.6 14.5 %copy-start.12 = (f32[5,7,4,128]{3,2,1,0:T(4,128)}, f32[5,7,4,128]{3,2,1,0:T(4,128)S(1)}, u32[]{:S(2)}) copy-start(f32[5,7,4,128]{3,2,1,0:T(4,128)S(1)} %copy_bitcast_fusion.own) | copy-start | bytes 215044
  121.6 13.4 %collective-permute-start.14 = (f32[5,7,4,128]{3,2,1,0:T(4,128)S(1)}, f32[5,7,4,128]{3,2,1,0:T(4,128)S(1)}, u32[]{:S(2)}, u32[]{:S(2)}) collective-permute-start(f32[5,7,4,128]{3,2,1,0:T(4,128)S(1)} %copy_bitcast_fusion.own), channel_id=1, source_target_pairs={{0,1},{1,2},{2,3},{3,4},{4,5},{5,6},{6,7},{8,9},{9,10},{10,11},{11... | collective-permute-start | bytes 215048 | tf_op jit(solution)/shard_map/ppermute | solution.py:716
  124.9 10.1 %collective-permute-start.15 = (f32[5,7,4,128]{3,2,1,0:T(4,128)S(1)}, f32[5,7,4,128]{3,2,1,0:T(4,128)S(1)}, u32[]{:S(2)}, u32[]{:S(2)}) collective-permute-start(f32[5,7,4,128]{3,2,1,0:T(4,128)S(1)} %copy_bitcast_fusion.own), channel_id=1, source_target_pairs={{0,2},{1,3},{2,4},{3,5},{4,6},{5,7},{8,10},{9,11},{10,12},{11,13},... | collective-permute-start | bytes 215048 | tf_op jit(solution)/shard_map/ppermute | solution.py:716
  128.6 6.4 %collective-permute-start.16 = (f32[5,7,4,128]{3,2,1,0:T(4,128)S(1)}, f32[5,7,4,128]{3,2,1,0:T(4,128)S(1)}, u32[]{:S(2)}, u32[]{:S(2)}) collective-permute-start(f32[5,7,4,128]{3,2,1,0:T(4,128)S(1)} %copy_bitcast_fusion.own), channel_id=1, source_target_pairs={{1,0},{2,1},{3,2},{4,3},{5,4},{6,5},{7,6},{9,8},{10,9},{11,10},{12... | collective-permute-start | bytes 215048 | tf_op jit(solution)/shard_map/ppermute | solution.py:716
  130.5 5.6 %collective-permute-start.17 = (f32[5,7,4,128]{3,2,1,0:T(4,128)S(1)}, f32[5,7,4,128]{3,2,1,0:T(4,128)S(1)}, u32[]{:S(2)}, u32[]{:S(2)}) collective-permute-start(f32[5,7,4,128]{3,2,1,0:T(4,128)S(1)} %copy_bitcast_fusion.own), channel_id=1, source_target_pairs={{2,0},{3,1},{4,2},{5,3},{6,4},{7,5},{10,8},{11,9},{12,10},{13,11},... | collective-permute-start | bytes 215048 | tf_op jit(solution)/shard_map/ppermute | solution.py:716
  135.0 1.1 copy-start.17
  135.0 1.1 copy-start.18
  135.0 1.1 copy-start.19
  136.1 0.6 copy-start.20
  145.2 12.5 %collective-permute-start.18 = (f32[5,8,16,128]{3,2,1,0:T(8,128)}, f32[5,8,16,128]{3,2,1,0:T(8,128)S(1)}, u32[]{:S(2)}, u32[]{:S(2)}) collective-permute-start(f32[5,8,16,128]{3,2,1,0:T(8,128)} %shard_map.34.own), channel_id=1, source_target_pairs={{0,8},{8,16},{16,24},{24,32},{32,40},{40,48},{48,56},{56,64},{64,7... | collective-permute-start | bytes 983048 | tf_op jit(solution)/shard_map/ppermute | solution.py:716
  147.2 11.4 %collective-permute-start.19 = (f32[5,8,16,128]{3,2,1,0:T(8,128)}, f32[5,8,16,128]{3,2,1,0:T(8,128)S(1)}, u32[]{:S(2)}, u32[]{:S(2)}) collective-permute-start(f32[5,8,16,128]{3,2,1,0:T(8,128)} %shard_map.34.own), channel_id=1, source_target_pairs={{8,0},{16,8},{24,16},{32,24},{40,32},{48,40},{56,48},{64,56},{72,6... | collective-permute-start | bytes 983048 | tf_op jit(solution)/shard_map/ppermute | solution.py:716
  157.7 12.9 %copy-start.2 = (f32[5,8,16,128]{3,2,1,0:T(8,128)}, f32[5,8,16,128]{3,2,1,0:T(8,128)S(1)}, u32[]{:S(2)}) copy-start(f32[5,8,16,128]{3,2,1,0:T(8,128)S(1)} %collective-permute-done.18.before) | copy-start | bytes 983044
  158.7 11.9 %copy-start.3 = (f32[5,8,16,128]{3,2,1,0:T(8,128)}, f32[5,8,16,128]{3,2,1,0:T(8,128)S(1)}, u32[]{:S(2)}) copy-start(f32[5,8,16,128]{3,2,1,0:T(8,128)S(1)} %collective-permute-done.19.after) | copy-start | bytes 983044
  158.7 10.6 %collective-permute-start.21 = (f32[5,20,8,128]{3,2,1,0:T(8,128)S(1)}, f32[5,20,8,128]{3,2,1,0:T(8,128)S(1)}, u32[]{:S(2)}, u32[]{:S(2)}) collective-permute-start(f32[5,20,8,128]{3,2,1,0:T(8,128)S(1)} %pad_maximum_fusion.3), channel_id=1, source_target_pairs={{1,0},{2,1},{3,2},{4,3},{5,4},{6,5},{7,6},{9,8},{10,9},{11,10},{12... | collective-permute-start | bytes 1228808 | tf_op jit(solution)/shard_map/ppermute | solution.py:716
  162.8 7.8 %collective-permute-start.20 = (f32[5,20,8,128]{3,2,1,0:T(8,128)S(1)}, f32[5,20,8,128]{3,2,1,0:T(8,128)S(1)}, u32[]{:S(2)}, u32[]{:S(2)}) collective-permute-start(f32[5,20,8,128]{3,2,1,0:T(8,128)S(1)} %pad_maximum_fusion.2), channel_id=1, source_target_pairs={{0,1},{1,2},{2,3},{3,4},{4,5},{5,6},{6,7},{8,9},{9,10},{10,11},{11... | collective-permute-start | bytes 1228808 | tf_op jit(solution)/shard_map/ppermute | solution.py:716
  169.4 1.2 copy-start.6
  170.6 0.7 copy-start.7
where the time goes:
time: 190 us; the launch traced here: 187 us
  starting transfers between devices  76.2 us (40%)
  Pallas kernels  68.5 us (36%)
  waiting for transfers between devices  34.7 us (18%)
  local copies, waits for them, and re-layouts  6.58 us (3%)
    ppermute x22, starting transfers between devices, shifted(): lax.ppermute(x, axis, [(i, i + by) for i in range(size) if 0 <= i + by <...  71.1 us
    pallas_call x8, Pallas kernels, call(): pl.pallas_call(kernel, out_shape=outs[0] if single else outs, in_specs=sp...  68.5 us
    ppermute x22, waiting for transfers between devices, shifted(): lax.ppermute(x, axis, [(i, i + by) for i in range(size) if 0 <= i + by <...  29.1 us
    all_to_all x1, waiting for transfers between devices, per_device(): column = lax.all_to_all(block, 'ax', 0, 0)  5.6 us
    all_to_all x1, starting transfers between devices, per_device(): column = lax.all_to_all(block, 'ax', 0, 0)  5.18 us
    unnamed x50, local copies, waits for them, and re-layouts  4.45 us
  transfers between devices with their start and end apart: 23, of which 12 were waited for; matrix products, arithmetic and copies ran while one was open for 2% of the time, Pallas kernels for 6%

commit v1 on v0

--- a/solution.py
+++ b/solution.py
@@ -268,13 +268,24 @@
     return jnp.dot(a, b, precision=EXACT, preferred_element_type=jnp.float32)
 
 
-def fine_window(pos, own, before, after, left, right, w, ends):
-    for c in range(5):
-        w[c, 0:8, 8:24] = before[c]
+def odd(index, by):
+    return (index // by) % 2
+
+
+def aligned(index):
+    return pl.multiple_of(index, 8)
+
+
+def fine_window(pos, own, ax0, ax1, xs0, xs1, w, ends):
+    a, x = odd(pos[0], 1), odd(pos[1], 1)
+    for c in range(5):
         w[c, 8:16, 8:24] = own[c]
-        w[c, 16:24, 8:24] = after[c]
-        w[c, 2:22, 0:8] = left[c]
-        w[c, 2:22, 24:32] = right[c]
+        w[c, pl.ds(16 * (1 - a), 8), 8:24] = ax0[c]
+        w[c, pl.ds(16 * a, 8), 8:24] = ax1[c]
+        for slab, at in ((xs0, aligned(24 * (1 - x))), (xs1, aligned(24 * x))):
+            w[c, pl.ds(16 - 14 * a, 6), pl.ds(at, 8)] = slab[c, 0:6]
+            w[c, 8:16, pl.ds(at, 8)] = slab[c, 6:14]
+            w[c, pl.ds(2 + 14 * a, 6), pl.ds(at, 8)] = slab[c, 14:20]
 
     def cross(at, to, source):
         @pl.when(pos[1] == at)
@@ -310,10 +321,11 @@
 
 
 def fine_relax_kernel(
-    ends, pos, own, before, after, left, right, fields, out, *rest
+    ends, pos, own, ax0, ax1, xs0, xs1, fields, out, *rest
 ):
     slabs, (wa, wb, wc, prim_a, prim_b, rate, carry, shift, matrix) = rest[:-9], rest[-9:]
-    fine_window(pos, own, before, after, left, right, wa, ends)
+    fine_window(pos, own, ax0, ax1, xs0, xs1, wa, ends)
+    a, x = odd(pos[0], 1), odd(pos[1], 1)
     fill_prim(wa, prim_a, 0, 24)
 
     @pl.loop(2, 22, unroll=4)
@@ -335,8 +347,9 @@
                 for c in range(5):
                     out[c, r - 8] = new[c]
                     if slabs:
-                        slabs[2][c, r - 8] = new[c][14:16]
-                        slabs[3][c, r - 8] = new[c][0:2]
+                        first, final = new[c][0:2], new[c][14:16]
+                        slabs[2][c, r - 8] = jnp.where(x == 0, final, first)
+                        slabs[3][c, r - 8] = jnp.where(x == 0, first, final)
             else:
                 store_row(target, prim, r, cols, new)
 
@@ -346,8 +359,8 @@
     if slabs:
         for c in range(5):
             for k in range(2):
-                slabs[0][c, k] = out[c, 6 + k]
-                slabs[1][c, k] = out[c, k]
+                slabs[0][c, k] = out[c, 6 * (1 - a) + k]
+                slabs[1][c, k] = out[c, 6 * a + k]
 
 
 def vmem(*shape):
@@ -408,15 +421,16 @@
 
 
 def fine_residual_kernel(
-    ends, pos, own, before, after, left, right, fields, out, w, prim, res, carry, shift, matrix,
+    ends, pos, own, ax0, ax1, xs0, xs1, fields, out, w, prim, res, carry, shift, matrix,
     pair,
 ):
-    for c in range(5):
-        w[c, 0:2, 8:24] = before[c]
+    a, x = odd(pos[0], 1), odd(pos[1], 1)
+    for c in range(5):
         w[c, 2:10, 8:24] = own[c]
-        w[c, 10:12, 8:24] = after[c]
-        w[c, 2:10, 6:8] = left[c]
-        w[c, 2:10, 24:26] = right[c]
+        w[c, pl.ds(10 * (1 - a), 2), 8:24] = ax0[c]
+        w[c, pl.ds(10 * a, 2), 8:24] = ax1[c]
+        w[c, 2:10, 6:8] = jnp.where(x == 1, xs0[c], xs1[c])
+        w[c, 2:10, 24:26] = jnp.where(x == 1, xs1[c], xs0[c])
 
     def cross(at, to, source, step):
         @pl.when(pos[1] == at)
@@ -483,15 +497,22 @@
 
 
 def middle_kernel(
-    ends, pos, before2, before, own, after, after2, left, right, fields, out, diff,
+    ends, pos, two0, one0, own, one1, two1, xs0, xs1, fields, out, diff,
     v0, wa, wb, force, prim_v, prim_a, prim_b, rate, res, carry, shift, matrix, pair,
 ):
-    for k, ref in enumerate((before2, before, own, after, after2)):
-        for c in range(5):
-            v0[c, 4 * k : 4 * k + 4, 8:16] = ref[c]
-    for c in range(5):
-        v0[c, 2:18, 0:8] = left[c]
-        v0[c, 2:18, 16:24] = right[c]
+    a, b, x = odd(pos[0], 1), odd(pos[0], 2), odd(pos[1], 1)
+    for c in range(5):
+        v0[c, 8:12, 8:16] = own[c]
+        for ref, at in (
+            (two0, 16 - 16 * b), (one0, 12 - 8 * a), (one1, 4 + 8 * a), (two1, 16 * b)
+        ):
+            v0[c, pl.ds(at, 4), 8:16] = ref[c]
+        for slab, at in ((xs0, aligned(16 * (1 - x))), (xs1, aligned(16 * x))):
+            v0[c, pl.ds(16 - 14 * b, 2), pl.ds(at, 8)] = slab[c, 0:2]
+            v0[c, pl.ds(12 - 8 * a, 4), pl.ds(at, 8)] = slab[c, 2:6]
+            v0[c, 8:12, pl.ds(at, 8)] = slab[c, 6:10]
+            v0[c, pl.ds(4 + 8 * a, 4), pl.ds(at, 8)] = slab[c, 10:14]
+            v0[c, pl.ds(2 + 14 * b, 2), pl.ds(at, 8)] = slab[c, 14:16]
     begin = 4 * pos[0] - 8
     extent = 4 * ends[0]
 
@@ -622,16 +643,20 @@
 
 
 def coarse_kernel(
-    ends, pos, own, left1, left2, right1, right2, fields, diff, smoothed, out,
+    ends, pos, own, two0, one0, one1, two1, fields, diff, smoothed, out,
     raw, v0, wa, wb, force, prim_v, prim_a, prim_b, rate, carry, shift, matrix, tall,
     wide,
 ):
     raw[...] = jnp.zeros_like(raw)
-    for k, ref in enumerate((left2, left1, own, right1, right2)):
-        for c in range(5):
-            for b in range(7):
-                at = (c * 7 + b) * LANES
-                raw[4 * k : 4 * k + 4, at : at + LANES] = ref[c, b]
+    one, two = odd(pos[1], 1) == 1, odd(pos[1], 2) == 1
+    for c in range(5):
+        for b in range(7):
+            at = pl.ds((c * 7 + b) * LANES, LANES)
+            raw[0:4, at] = jnp.where(two, two0[c, b], two1[c, b])
+            raw[4:8, at] = jnp.where(one, one0[c, b], one1[c, b])
+            raw[8:12, at] = own[c, b]
+            raw[12:16, at] = jnp.where(one, one1[c, b], one0[c, b])
+            raw[16:20, at] = jnp.where(two, two1[c, b], two0[c, b])
     first = 4 * pos[1] - 6
     extent = 4 * ends[1]
     j = lax.broadcasted_iota(jnp.int32, (16, 24), 0)
@@ -651,10 +676,10 @@
         at = mirror(g, ax_extent)
         sign = jnp.where(at == g, 1.0, -1.0)
         block = (at - origin) // 2
-        odd = (at - origin) % 2
+        half = (at - origin) % 2
         for c in range(5):
             x = raw[0:16, pl.ds(pl.multiple_of((c * 7 + block) * LANES, LANES), LANES)]
-            x = jnp.where(odd == 1, pltpu.roll(x, 64, 1), x)
+            x = jnp.where(half == 1, pltpu.roll(x, 64, 1), x)
             if c == 1:
                 x = x * sign
             if c == 2:
@@ -711,21 +736,29 @@
     )
 
 
-def shifted(x, axis, by):
+def swapped(x, axis, by, phase):
     size = lax.axis_size(axis)
-    return lax.ppermute(x, axis, [(i, i + by) for i in range(size) if 0 <= i + by < size])
+    low = [i for i in range(size - by) if (i // by) % 2 == phase]
+    pairs = [(i, i + by) for i in low] + [(i + by, i) for i in low]
+    return lax.ppermute(x, axis, sorted(pairs))
 
 
 def wide_halos(own):
-    before = shifted(own, "ax", 1)
-    after = shifted(own, "ax", -1)
-
-    def slab(cols):
-        return jnp.concatenate([before[:, 2:, cols], own[:, :, cols], after[:, :6, cols]], axis=1)
-
-    left = shifted(slab(slice(8, 16)), "xs", 1)
-    right = shifted(slab(slice(0, 8)), "xs", -1)
-    return before, after, left, right
+    a, x = odd(lax.axis_index("ax"), 1), odd(lax.axis_index("xs"), 1)
+    ax1 = swapped(own, "ax", 1, 1)
+    ax0 = swapped(own, "ax", 1, 0)
+
+    def slab(phase):
+        col = 8 * jnp.where(phase == 0, 1 - x, x)
+        parts = [(ax0, 2 * a, 6), (own, 0, 8), (ax1, 2 * (1 - a), 6)]
+        return jnp.concatenate(
+            [lax.dynamic_slice(y, (0, row, col, 0), (5, n, 8, LANES)) for y, row, n in parts],
+            axis=1,
+        )
+
+    xs1 = swapped(slab(1), "xs", 1, 1)
+    xs0 = swapped(slab(0), "xs", 1, 0)
+    return ax0, ax1, xs0, xs1
 
 
 def wall_terms_kernel(factor, rows, count, origin, ends, pos, code, out, sides):
@@ -797,31 +830,36 @@
     middle_fields = wall_terms(ends, pos, wall_code, 2, 20, MIDDLE_COLS, (8, 8))
     coarse_fields = wall_terms(ends, pos, wall_code, 4, 14, COARSE_COLS, (6, 6))
 
-    smoothed, high, low, last, first = fine_relax(
-        ends, pos, state, wide_halos(state), fine_fields, True
-    )
-    halos = (
-        shifted(high, "ax", 1),
-        shifted(low, "ax", -1),
-        shifted(last, "xs", 1),
-        shifted(first, "xs", -1),
-    )
+    smoothed, *slabs = fine_relax(ends, pos, state, wide_halos(state), fine_fields, True)
+    halos = [
+        swapped(slab, axis, 1, phase)
+        for slab, (axis, phase) in zip(slabs, (("ax", 0), ("ax", 1), ("xs", 0), ("xs", 1)))
+    ]
     packed = fine_residual(ends, pos, smoothed, halos, fine_fields)
 
-    pieces = [shifted(packed, "ax", by) for by in (2, 1)] + [packed]
-    pieces += [shifted(packed, "ax", by) for by in (-1, -2)]
+    two0, two1 = [swapped(packed, "ax", 2, phase) for phase in (0, 1)]
+    one0, one1 = [swapped(packed, "ax", 1, phase) for phase in (0, 1)]
+    b = odd(ax, 2)
     slab = jnp.concatenate(
-        [pieces[0][:, 2:], pieces[1], pieces[2], pieces[3], pieces[4][:, :2]], axis=1
-    )
-    block, diff = middle(
-        ends, pos, pieces, shifted(slab, "xs", 1), shifted(slab, "xs", -1), middle_fields
-    )
+        [
+            lax.dynamic_slice_in_dim(two0, 2 * b, 2, axis=1),
+            one0,
+            packed,
+            one1,
+            lax.dynamic_slice_in_dim(two1, 2 * (1 - b), 2, axis=1),
+        ],
+        axis=1,
+    )
+    xs0, xs1 = [swapped(slab, "xs", 1, phase) for phase in (0, 1)]
+    block, diff = middle(ends, pos, (two0, one0, packed, one1, two1), xs0, xs1, middle_fields)
 
     column = lax.all_to_all(block, "ax", 0, 0)
     start = jnp.clip(ax - 3, 0, ends[0] - 7)
     column = lax.dynamic_slice_in_dim(column, start, 7, axis=0)
     column = jnp.transpose(column, (1, 0, 2, 3))
-    neighbours = [shifted(column, "xs", by) for by in (1, 2, -1, -2)]
+    neighbours = [
+        swapped(column, "xs", by, phase) for by, phase in ((2, 0), (1, 0), (1, 1), (2, 1))
+    ]
     fine_new = coarse(ends, pos, column, neighbours, coarse_fields, diff, smoothed)
 
     return fine_relax(ends, pos, fine_new, wide_halos(fine_new), fine_fields, False)

time: 190 us -> 169 us (0.89); the launches traced: 187 us -> 168 us
  starting transfers between devices: 76.2 us -> 55.9 us
    ppermute x22, starting transfers between devices: 71.1 us -> 50.3 us  [swapped(): return lax.ppermute(x, axis, sorted(pairs))]
    dynamic_slice x0 -> x6, local copies, waits for them, and re-layouts: none -> 2.12 us  [slab(): lax.dynamic_slice(y, (0, row, col, 0), (5, n, 8, LANES))]
    slice x6 -> x0, local copies, waits for them, and re-layouts: 2.11 us -> none  [the longest x2 2.04 us: slab(): own[:, :, cols]]
  transfers between devices with their start and end apart: 23 -> 23, of which waited for: 12 -> 11; matrix products, arithmetic and copies ran while one was open for 2% -> 2% of each run, Pallas kernels for 6% -> 6%
where the time goes in v1:
time: 169 us; the launch traced here: 168 us
  Pallas kernels  68.5 us (41%)
  starting transfers between devices  55.9 us (33%)
  waiting for transfers between devices  34.5 us (20%)
  local copies, waits for them, and re-layouts  8.11 us (5%)
    pallas_call x8, Pallas kernels, call(): pl.pallas_call(kernel, out_shape=outs[0] if single else outs, in_specs=sp...  68.5 us
    ppermute x22, starting transfers between devices, swapped(): return lax.ppermute(x, axis, sorted(pairs))  50.3 us
    ppermute x22, waiting for transfers between devices, swapped(): return lax.ppermute(x, axis, sorted(pairs))  28.9 us
    unnamed x50, local copies, waits for them, and re-layouts  5.98 us
    all_to_all x1, starting transfers between devices, per_device(): column = lax.all_to_all(block, 'ax', 0, 0)  5.66 us
    all_to_all x1, waiting for transfers between devices, per_device(): column = lax.all_to_all(block, 'ax', 0, 0)  5.6 us
  transfers between devices with their start and end apart: 23, of which 11 were waited for; matrix products, arithmetic and copies ran while one was open for 2% of the time, Pallas kernels for 6%

profile of v1, /device:TPU:3, one launch (start us, length us, event | category | flops | bytes accessed | tf_op | source)
XLA Modules:
  0.0 168.2 jit_solution(16680693339251807288)
XLA Ops:
  0.0 1.3 collective-permute-start
  1.3 3.8 %collective-permute-start.1 = (f32[5,8,16,128]{3,2,1,0:T(8,128)}, f32[5,8,16,128]{3,2,1,0:T(8,128)S(1)}, u32[]{:S(2)}, u32[]{:S(2)}) collective-permute-start(f32[5,8,16,128]{3,2,1,0:T(8,128)} %own.1), channel_id=1, source_target_pairs={{8,16},{16,8},{24,32},{32,24},{40,48},{48,40},{56,64},{64,56},{72,... | collective-permute-start | bytes 983048 | tf_op jit(solution)/shard_map/ppermute | solution.py:743
  5.1 1.0 constant_dynamic-slice_fusion.8
  6.1 2.7 %collective-permute-done.ax0 = f32[5,8,16,128]{3,2,1,0:T(8,128)S(1)} collective-permute-done((f32[5,8,16,128]{3,2,1,0:T(8,128)}, f32[5,8,16,128]{3,2,1,0:T(8,128)S(1)}, u32[]{:S(2)}, u32[]{:S(2)}) %collective-permute-start) | collective-permute-done | bytes 327712 | tf_op jit(solution)/shard_map/ppermute | solution.py:743
  8.8 5.0 %collective-permute-done.1.ax1 = f32[5,8,16,128]{3,2,1,0:T(8,128)S(1)} collective-permute-done((f32[5,8,16,128]{3,2,1,0:T(8,128)}, f32[5,8,16,128]{3,2,1,0:T(8,128)S(1)}, u32[]{:S(2)}, u32[]{:S(2)}) %collective-permute-start.1) | collective-permute-done | bytes 327712 | tf_op jit(solution)/shard_map/ppermute | solution.py:743
  13.9 5.2 %collective-permute-start.3 = (f32[5,20,8,128]{3,2,1,0:T(8,128)S(1)}, f32[5,20,8,128]{3,2,1,0:T(8,128)S(1)}, u32[]{:S(2)}, u32[]{:S(2)}) collective-permute-start(f32[5,20,8,128]{3,2,1,0:T(8,128)S(1)} %pad_maximum_fusion.1), channel_id=1, source_target_pairs={{1,2},{2,1},{3,4},{4,3},{5,6},{6,5},{9,10},{10,9},{11,12},{12,11},... | collective-permute-start | bytes 1228808 | tf_op jit(solution)/shard_map/ppermute | solution.py:743
  19.2 0.1 collective-permute-start.2
  19.3 0.6 pad_add_fusion.pos
  19.9 3.8 %shard_map.28.fields = f32[3,24,40,128]{3,2,1,0:T(8,128)} custom-call(s32[2]{0:T(128)} %pad_add_fusion.pos, s32[128,4,128]{2,1,0:T(4,128)} %code.5), custom_call_target="tpu_custom_call" | custom-call | flops 1000000 | bytes 1736712 | tf_op jit(solution)/shard_map/pallas_call | solution.py:377
  23.7 1.1 collective-permute-done.3.xs1
  24.7 0.0 collective-permute-done.2.xs0
  24.8 0.8 copy-done.4
  25.5 0.7 copy-done.6
  26.3 15.9 %shard_map.29 = (f32[5,8,16,128]{3,2,1,0:T(8,128)}, f32[5,2,16,128]{3,2,1,0:T(8,128)}, f32[5,2,16,128]{3,2,1,0:T(8,128)}, f32[5,8,2,128]{3,2,1,0:T(2,128)}, f32[5,8,2,128]{3,2,1,0:T(2,128)}) custom-call(s32[2]{0:T(128)} %pad_add_fusion.pos, f32[5,8,16,128]{3,2,1,0:T(8,128)} %own.1, f32[5,8,16,128]{3,2,1,0:T(8,128)} %copy-done, f32[5,8,16,128]{3,2,1,0:T(8,128)} %copy-done.1, ...), custom_call_target="tpu_custom_call" | custom-call | flops 80000000 | bytes 3850248 | tf_op jit(solution)/shard_map/pallas_call | solution.py:377
  42.2 0.0 collective-permute-start.4
  42.2 3.8 %collective-permute-start.5 = (f32[5,2,16,128]{3,2,1,0:T(8,128)}, f32[5,2,16,128]{3,2,1,0:T(8,128)S(1)}, u32[]{:S(2)}, u32[]{:S(2)}) collective-permute-start(f32[5,2,16,128]{3,2,1,0:T(8,128)} %get-tuple-element.14), channel_id=1, source_target_pairs={{8,16},{16,8},{24,32},{32,24},{40,48},{48,40},{56,64},{64,56},{72,... | collective-permute-start | bytes 245768 | tf_op jit(solution)/shard_map/ppermute | solution.py:743
  46.0 0.1 collective-permute-start.6
  46.1 3.9 %collective-permute-start.7 = (f32[5,8,2,128]{3,2,1,0:T(2,128)}, f32[5,8,2,128]{3,2,1,0:T(2,128)S(1)}, u32[]{:S(2)}, u32[]{:S(2)}) collective-permute-start(f32[5,8,2,128]{3,2,1,0:T(2,128)} %get-tuple-element.16), channel_id=1, source_target_pairs={{1,2},{2,1},{3,4},{4,3},{5,6},{6,5},{9,10},{10,9},{11,12},{12,11},... | collective-permute-start | bytes 122888 | tf_op jit(solution)/shard_map/ppermute | solution.py:743
  50.0 0.0 collective-permute-done.6.xs0
  50.0 1.9 %collective-permute-done.7.xs1 = f32[5,8,2,128]{3,2,1,0:T(2,128)S(1)} collective-permute-done((f32[5,8,2,128]{3,2,1,0:T(2,128)}, f32[5,8,2,128]{3,2,1,0:T(2,128)S(1)}, u32[]{:S(2)}, u32[]{:S(2)}) %collective-permute-start.7) | collective-permute-done | bytes 40992 | tf_op jit(solution)/shard_map/ppermute | solution.py:743
  51.9 0.6 copy-done.22
  52.5 0.0 copy-done.15
  52.5 0.0 copy-done.16
  52.6 4.4 %shard_map.30.own = f32[5,4,8,128]{3,2,1,0:T(8,128)} custom-call(s32[2]{0:T(128)} %pad_add_fusion.pos, f32[5,8,16,128]{3,2,1,0:T(8,128)} %get-tuple-element.12.own.smoothed, f32[5,2,16,128]{3,2,1,0:T(8,128)} %copy-done.15, f32[5,2,16,128]{3,2,1,0:T(8,128)} %copy-done.16, f32[5,8,2,128]{3,2,1,0:T(2,128)} %copy-done.21, f32[5,8,2,128]{3,2,1,0:T(2,128)} %copy-done.22, ...), custom_call_target="tpu_custom_call" | custom-call | flops 8000000 | bytes 2129928 | tf_op jit(solution)/shard_map/pallas_call | solution.py:377
  57.0 1.7 collective-permute-start.8
  58.6 0.7 collective-permute-start.9
  59.3 3.1 %collective-permute-start.10 = (f32[5,4,8,128]{3,2,1,0:T(8,128)}, f32[5,4,8,128]{3,2,1,0:T(8,128)S(1)}, u32[]{:S(2)}, u32[]{:S(2)}) collective-permute-start(f32[5,4,8,128]{3,2,1,0:T(8,128)} %shard_map.30.own), channel_id=1, source_target_pairs={{8,16},{16,8},{24,32},{32,24},{40,48},{48,40},{56,64},{64,56},{72,... | collective-permute-start | bytes 245768 | tf_op jit(solution)/shard_map/ppermute | solution.py:743
  62.4 3.1 %collective-permute-start.11 = (f32[5,4,8,128]{3,2,1,0:T(8,128)}, f32[5,4,8,128]{3,2,1,0:T(8,128)S(1)}, u32[]{:S(2)}, u32[]{:S(2)}) collective-permute-start(f32[5,4,8,128]{3,2,1,0:T(8,128)} %shard_map.30.own), channel_id=1, source_target_pairs={{16,32},{24,40},{32,16},{40,24},{48,64},{56,72},{64,48},{72,56},{8... | collective-permute-start | bytes 245768 | tf_op jit(solution)/shard_map/ppermute | solution.py:743
  65.5 0.0 collective-permute-done.8.two0
  65.6 0.0 collective-permute-done.9.one0
  65.6 0.9 constant_dynamic-update-slice_fusion.1
  66.5 0.9 collective-permute-done.10.one1
  67.4 3.0 %collective-permute-done.11.two1 = f32[5,4,8,128]{3,2,1,0:T(8,128)S(1)} collective-permute-done((f32[5,4,8,128]{3,2,1,0:T(8,128)}, f32[5,4,8,128]{3,2,1,0:T(8,128)S(1)}, u32[]{:S(2)}, u32[]{:S(2)}) %collective-permute-start.11) | collective-permute-done | bytes 81952 | tf_op jit(solution)/shard_map/ppermute | solution.py:743
  70.5 0.0 collective-permute-start.12
  70.5 5.1 %collective-permute-start.13 = (f32[5,16,8,128]{3,2,1,0:T(8,128)S(1)}, f32[5,16,8,128]{3,2,1,0:T(8,128)S(1)}, u32[]{:S(2)}, u32[]{:S(2)}) collective-permute-start(f32[5,16,8,128]{3,2,1,0:T(8,128)S(1)} %dynamic-slice_dynamic-update-slice_fusion), channel_id=1, source_target_pairs={{1,2},{2,1},{3,4},{4,3},{5,6},{6,5},{9,10},{10,9},{11,12},{12,11},... | collective-permute-start | bytes 983048 | tf_op jit(solution)/shard_map/ppermute | solution.py:743
  75.6 3.6 %shard_map.31.fields = f32[3,20,32,128]{3,2,1,0:T(8,128)} custom-call(s32[2]{0:T(128)} %pad_add_fusion.pos, s32[128,4,128]{2,1,0:T(4,128)} %code.5), custom_call_target="tpu_custom_call" | custom-call | flops 1000000 | bytes 1245192 | tf_op jit(solution)/shard_map/pallas_call | solution.py:377
  79.2 1.1 collective-permute-done.13.xs1
  80.4 0.7 copy-done.11
  81.1 13.4 %shard_map.32 = (f32[16,5,4,128]{3,2,1,0:T(4,128)}, f32[5,4,8,128]{3,2,1,0:T(8,128)}) custom-call(s32[2]{0:T(128)} %pad_add_fusion.pos, f32[5,4,8,128]{3,2,1,0:T(8,128)} %copy-done.13, f32[5,4,8,128]{3,2,1,0:T(8,128)} %copy-done.8, f32[5,4,8,128]{3,2,1,0:T(8,128)} %shard_map.30.own, f32[5,4,8,128]{3,2,1,0:T(8,128)} %copy-done.9, ...), custom_call_target="tpu_custom_call" | custom-call | flops 60000000 | bytes 2293768 | tf_op jit(solution)/shard_map/pallas_call | solution.py:377
  94.5 5.7 %all-to-all-start = ((f32[16,5,4,128]{3,2,1,0:T(4,128)}), f32[16,5,4,128]{3,2,1,0:T(4,128)S(1)}, u32[]{:S(2)}, u32[]{:S(2)}) async-start(f32[16,5,4,128]{3,2,1,0:T(4,128)} %get-tuple-element.17), calls=%async_computation | async-start | bytes 327680 | tf_op jit(solution)/shard_map/all_to_all | solution.py:856
  100.2 5.6 %all-to-all-done = f32[16,5,4,128]{3,2,1,0:T(4,128)S(1)} async-done(((f32[16,5,4,128]{3,2,1,0:T(4,128)}), f32[16,5,4,128]{3,2,1,0:T(4,128)S(1)}, u32[]{:S(2)}, u32[]{:S(2)}) %all-to-all-start) | async-done | bytes 163872 | tf_op jit(solution)/shard_map/all_to_all | solution.py:856
  105.8 0.0 copy-start.12
  105.8 2.4 %collective-permute-start.14 = (f32[5,7,4,128]{3,2,1,0:T(4,128)S(1)}, f32[5,7,4,128]{3,2,1,0:T(4,128)S(1)}, u32[]{:S(2)}, u32[]{:S(2)}) collective-permute-start(f32[5,7,4,128]{3,2,1,0:T(4,128)S(1)} %copy_bitcast_fusion.own), channel_id=1, source_target_pairs={{0,2},{1,3},{2,0},{3,1},{4,6},{5,7},{6,4},{7,5},{8,10},{9,11},{10,... | collective-permute-start | bytes 215048 | tf_op jit(solution)/shard_map/ppermute | solution.py:743
  108.2 1.6 collective-permute-start.15
  109.7 1.9 %collective-permute-start.16 = (f32[5,7,4,128]{3,2,1,0:T(4,128)S(1)}, f32[5,7,4,128]{3,2,1,0:T(4,128)S(1)}, u32[]{:S(2)}, u32[]{:S(2)}) collective-permute-start(f32[5,7,4,128]{3,2,1,0:T(4,128)S(1)} %copy_bitcast_fusion.own), channel_id=1, source_target_pairs={{1,2},{2,1},{3,4},{4,3},{5,6},{6,5},{9,10},{10,9},{11,12},{12,11},... | collective-permute-start | bytes 215048 | tf_op jit(solution)/shard_map/ppermute | solution.py:743
  111.6 0.7 collective-permute-start.17
  112.3 3.0 %shard_map.33.fields = f32[3,14,24,128]{3,2,1,0:T(8,128)} custom-call(s32[2]{0:T(128)} %pad_add_fusion.pos, s32[128,4,128]{2,1,0:T(4,128)} %code.5), custom_call_target="tpu_custom_call" | custom-call | flops 1000000 | bytes 778248 | tf_op jit(solution)/shard_map/pallas_call | solution.py:377
  115.3 0.0 collective-permute-done.16.one1
  115.4 0.6 copy-done.17
  116.0 0.0 copy-done.18
  116.0 0.0 copy-done.19
  116.0 0.0 copy-done.20
  116.0 8.5 %shard_map.34.own = f32[5,8,16,128]{3,2,1,0:T(8,128)} custom-call(s32[2]{0:T(128)} %pad_add_fusion.pos, f32[5,7,4,128]{3,2,1,0:T(4,128)} %copy-done.12, f32[5,7,4,128]{3,2,1,0:T(4,128)} %copy-done.17, f32[5,7,4,128]{3,2,1,0:T(4,128)} %copy-done.18, f32[5,7,4,128]{3,2,1,0:T(4,128)} %copy-done.19, f32[5,7,4,128]{3,2,1,0:T(4,128)} %copy-done.20, ...), custom_call_target="tpu_custom_call" | custom-call | flops 20000000 | bytes 1611784 | tf_op jit(solution)/shard_map/pallas_call | solution.py:377
  124.5 0.1 collective-permute-start.18
  124.6 4.4 %collective-permute-start.19 = (f32[5,8,16,128]{3,2,1,0:T(8,128)}, f32[5,8,16,128]{3,2,1,0:T(8,128)S(1)}, u32[]{:S(2)}, u32[]{:S(2)}) collective-permute-start(f32[5,8,16,128]{3,2,1,0:T(8,128)} %shard_map.34.own), channel_id=1, source_target_pairs={{8,16},{16,8},{24,32},{32,24},{40,48},{48,40},{56,64},{64,56},{72,... | collective-permute-start | bytes 983048 | tf_op jit(solution)/shard_map/ppermute | solution.py:743
  129.0 1.0 constant_dynamic-slice_fusion.1
  130.0 3.6 %collective-permute-done.18.ax0 = f32[5,8,16,128]{3,2,1,0:T(8,128)S(1)} collective-permute-done((f32[5,8,16,128]{3,2,1,0:T(8,128)}, f32[5,8,16,128]{3,2,1,0:T(8,128)S(1)}, u32[]{:S(2)}, u32[]{:S(2)}) %collective-permute-start.18) | collective-permute-done | bytes 327712 | tf_op jit(solution)/shard_map/ppermute | solution.py:743
  133.7 4.1 %collective-permute-done.19.ax1 = f32[5,8,16,128]{3,2,1,0:T(8,128)S(1)} collective-permute-done((f32[5,8,16,128]{3,2,1,0:T(8,128)}, f32[5,8,16,128]{3,2,1,0:T(8,128)S(1)}, u32[]{:S(2)}, u32[]{:S(2)}) %collective-permute-start.19) | collective-permute-done | bytes 327712 | tf_op jit(solution)/shard_map/ppermute | solution.py:743
  137.8 7.4 %collective-permute-start.21 = (f32[5,20,8,128]{3,2,1,0:T(8,128)S(1)}, f32[5,20,8,128]{3,2,1,0:T(8,128)S(1)}, u32[]{:S(2)}, u32[]{:S(2)}) collective-permute-start(f32[5,20,8,128]{3,2,1,0:T(8,128)S(1)} %pad_maximum_fusion.3), channel_id=1, source_target_pairs={{1,2},{2,1},{3,4},{4,3},{5,6},{6,5},{9,10},{10,9},{11,12},{12,11},... | collective-permute-start | bytes 1228808 | tf_op jit(solution)/shard_map/ppermute | solution.py:743
  145.2 0.1 collective-permute-start.20
  145.3 5.5 %collective-permute-done.21.xs1 = f32[5,20,8,128]{3,2,1,0:T(8,128)S(1)} collective-permute-done((f32[5,20,8,128]{3,2,1,0:T(8,128)S(1)}, f32[5,20,8,128]{3,2,1,0:T(8,128)S(1)}, u32[]{:S(2)}, u32[]{:S(2)}) %collective-permute-start.21) | collective-permute-done | bytes 409632 | tf_op jit(solution)/shard_map/ppermute | solution.py:743
  150.8 0.7 copy-done.5
  151.6 0.7 copy-done.7
  152.3 15.8 %shard_map.35 = f32[5,8,16,128]{3,2,1,0:T(8,128)} custom-call(s32[2]{0:T(128)} %pad_add_fusion.pos, f32[5,8,16,128]{3,2,1,0:T(8,128)} %shard_map.34.own, f32[5,8,16,128]{3,2,1,0:T(8,128)} %copy-done.2, f32[5,8,16,128]{3,2,1,0:T(8,128)} %copy-done.3, f32[5,20,8,128]{3,2,1,0:T(8,128)} %copy-done.7, f32[5,20,8,128]{3,2,1,0:T(8,128)} %copy-done.5, ...), custom_call_target="tpu_custom_call" | custom-call | flops 80000000 | bytes 3604488 | tf_op jit(solution)/shard_map/pallas_call | solution.py:377
  (53 shorter events, 0.3 us)
Async XLA Ops:
  0.0 8.8 %collective-permute-start = (f32[5,8,16,128]{3,2,1,0:T(8,128)}, f32[5,8,16,128]{3,2,1,0:T(8,128)S(1)}, u32[]{:S(2)}, u32[]{:S(2)}) collective-permute-start(f32[5,8,16,128]{3,2,1,0:T(8,128)} %own.1), channel_id=1, source_target_pairs={{0,8},{8,0},{16,24},{24,16},{32,40},{40,32},{48,56},{56,48},{64,72... | collective-permute-start | bytes 983048 | tf_op jit(solution)/shard_map/ppermute | solution.py:743
  1.3 12.5 %collective-permute-start.1 = (f32[5,8,16,128]{3,2,1,0:T(8,128)}, f32[5,8,16,128]{3,2,1,0:T(8,128)S(1)}, u32[]{:S(2)}, u32[]{:S(2)}) collective-permute-start(f32[5,8,16,128]{3,2,1,0:T(8,128)} %own.1), channel_id=1, source_target_pairs={{8,16},{16,8},{24,32},{32,24},{40,48},{48,40},{56,64},{64,56},{72,... | collective-permute-start | bytes 983048 | tf_op jit(solution)/shard_map/ppermute | solution.py:743
  8.8 14.9 %copy-start = (f32[5,8,16,128]{3,2,1,0:T(8,128)}, f32[5,8,16,128]{3,2,1,0:T(8,128)S(1)}, u32[]{:S(2)}) copy-start(f32[5,8,16,128]{3,2,1,0:T(8,128)S(1)} %collective-permute-done.ax0) | copy-start | bytes 983044
  13.8 9.9 %copy-start.1 = (f32[5,8,16,128]{3,2,1,0:T(8,128)}, f32[5,8,16,128]{3,2,1,0:T(8,128)S(1)}, u32[]{:S(2)}) copy-start(f32[5,8,16,128]{3,2,1,0:T(8,128)S(1)} %collective-permute-done.1.ax1) | copy-start | bytes 983044
  13.9 10.9 %collective-permute-start.3 = (f32[5,20,8,128]{3,2,1,0:T(8,128)S(1)}, f32[5,20,8,128]{3,2,1,0:T(8,128)S(1)}, u32[]{:S(2)}, u32[]{:S(2)}) collective-permute-start(f32[5,20,8,128]{3,2,1,0:T(8,128)S(1)} %pad_maximum_fusion.1), channel_id=1, source_target_pairs={{1,2},{2,1},{3,4},{4,3},{5,6},{6,5},{9,10},{10,9},{11,12},{12,11},... | collective-permute-start | bytes 1228808 | tf_op jit(solution)/shard_map/ppermute | solution.py:743
  19.2 5.6 %collective-permute-start.2 = (f32[5,20,8,128]{3,2,1,0:T(8,128)S(1)}, f32[5,20,8,128]{3,2,1,0:T(8,128)S(1)}, u32[]{:S(2)}, u32[]{:S(2)}) collective-permute-start(f32[5,20,8,128]{3,2,1,0:T(8,128)S(1)} %pad_maximum_fusion), channel_id=1, source_target_pairs={{0,1},{1,0},{2,3},{3,2},{4,5},{5,4},{6,7},{7,6},{8,9},{9,8},{10,11... | collective-permute-start | bytes 1228808 | tf_op jit(solution)/shard_map/ppermute | solution.py:743
  24.7 0.8 copy-start.4
  25.5 0.7 copy-start.6
  42.2 9.7 %collective-permute-start.4 = (f32[5,2,16,128]{3,2,1,0:T(8,128)}, f32[5,2,16,128]{3,2,1,0:T(8,128)S(1)}, u32[]{:S(2)}, u32[]{:S(2)}) collective-permute-start(f32[5,2,16,128]{3,2,1,0:T(8,128)} %get-tuple-element.13), channel_id=1, source_target_pairs={{0,8},{8,0},{16,24},{24,16},{32,40},{40,32},{48,56},{56,48},{64,72... | collective-permute-start | bytes 245768 | tf_op jit(solution)/shard_map/ppermute | solution.py:743
  42.2 9.7 %collective-permute-start.5 = (f32[5,2,16,128]{3,2,1,0:T(8,128)}, f32[5,2,16,128]{3,2,1,0:T(8,128)S(1)}, u32[]{:S(2)}, u32[]{:S(2)}) collective-permute-start(f32[5,2,16,128]{3,2,1,0:T(8,128)} %get-tuple-element.14), channel_id=1, source_target_pairs={{8,16},{16,8},{24,32},{32,24},{40,48},{48,40},{56,64},{64,56},{72,... | collective-permute-start | bytes 245768 | tf_op jit(solution)/shard_map/ppermute | solution.py:743
  46.0 4.0 %collective-permute-start.6 = (f32[5,8,2,128]{3,2,1,0:T(2,128)}, f32[5,8,2,128]{3,2,1,0:T(2,128)S(1)}, u32[]{:S(2)}, u32[]{:S(2)}) collective-permute-start(f32[5,8,2,128]{3,2,1,0:T(2,128)} %get-tuple-element.15), channel_id=1, source_target_pairs={{0,1},{1,0},{2,3},{3,2},{4,5},{5,4},{6,7},{7,6},{8,9},{9,8},{10,11... | collective-permute-start | bytes 122888 | tf_op jit(solution)/shard_map/ppermute | solution.py:743
  46.1 5.8 %collective-permute-start.7 = (f32[5,8,2,128]{3,2,1,0:T(2,128)}, f32[5,8,2,128]{3,2,1,0:T(2,128)S(1)}, u32[]{:S(2)}, u32[]{:S(2)}) collective-permute-start(f32[5,8,2,128]{3,2,1,0:T(2,128)} %get-tuple-element.16), channel_id=1, source_target_pairs={{1,2},{2,1},{3,4},{4,3},{5,6},{6,5},{9,10},{10,9},{11,12},{12,11},... | collective-permute-start | bytes 122888 | tf_op jit(solution)/shard_map/ppermute | solution.py:743
  50.0 1.9 %copy-start.21 = (f32[5,8,2,128]{3,2,1,0:T(2,128)}, f32[5,8,2,128]{3,2,1,0:T(2,128)S(1)}, u32[]{:S(2)}) copy-start(f32[5,8,2,128]{3,2,1,0:T(2,128)S(1)} %collective-permute-done.6.xs0) | copy-start | bytes 122884
  51.9 0.6 copy-start.22
  51.9 0.6 copy-start.15
  51.9 0.7 copy-start.16
  57.0 8.5 %collective-permute-start.8 = (f32[5,4,8,128]{3,2,1,0:T(8,128)}, f32[5,4,8,128]{3,2,1,0:T(8,128)S(1)}, u32[]{:S(2)}, u32[]{:S(2)}) collective-permute-start(f32[5,4,8,128]{3,2,1,0:T(8,128)} %shard_map.30.own), channel_id=1, source_target_pairs={{0,16},{8,24},{16,0},{24,8},{32,48},{40,56},{48,32},{56,40},{64,80... | collective-permute-start | bytes 245768 | tf_op jit(solution)/shard_map/ppermute | solution.py:743
  58.6 6.9 %collective-permute-start.9 = (f32[5,4,8,128]{3,2,1,0:T(8,128)}, f32[5,4,8,128]{3,2,1,0:T(8,128)S(1)}, u32[]{:S(2)}, u32[]{:S(2)}) collective-permute-start(f32[5,4,8,128]{3,2,1,0:T(8,128)} %shard_map.30.own), channel_id=1, source_target_pairs={{0,8},{8,0},{16,24},{24,16},{32,40},{40,32},{48,56},{56,48},{64,72... | collective-permute-start | bytes 245768 | tf_op jit(solution)/shard_map/ppermute | solution.py:743
  59.3 8.1 %collective-permute-start.10 = (f32[5,4,8,128]{3,2,1,0:T(8,128)}, f32[5,4,8,128]{3,2,1,0:T(8,128)S(1)}, u32[]{:S(2)}, u32[]{:S(2)}) collective-permute-start(f32[5,4,8,128]{3,2,1,0:T(8,128)} %shard_map.30.own), channel_id=1, source_target_pairs={{8,16},{16,8},{24,32},{32,24},{40,48},{48,40},{56,64},{64,56},{72,... | collective-permute-start | bytes 245768 | tf_op jit(solution)/shard_map/ppermute | solution.py:743
  62.4 8.0 %collective-permute-start.11 = (f32[5,4,8,128]{3,2,1,0:T(8,128)}, f32[5,4,8,128]{3,2,1,0:T(8,128)S(1)}, u32[]{:S(2)}, u32[]{:S(2)}) collective-permute-start(f32[5,4,8,128]{3,2,1,0:T(8,128)} %shard_map.30.own), channel_id=1, source_target_pairs={{16,32},{24,40},{32,16},{40,24},{48,64},{56,72},{64,48},{72,56},{8... | collective-permute-start | bytes 245768 | tf_op jit(solution)/shard_map/ppermute | solution.py:743
  65.5 14.8 %copy-start.13 = (f32[5,4,8,128]{3,2,1,0:T(8,128)}, f32[5,4,8,128]{3,2,1,0:T(8,128)S(1)}, u32[]{:S(2)}) copy-start(f32[5,4,8,128]{3,2,1,0:T(8,128)S(1)} %collective-permute-done.8.two0) | copy-start | bytes 245764
  65.6 14.8 %copy-start.8 = (f32[5,4,8,128]{3,2,1,0:T(8,128)}, f32[5,4,8,128]{3,2,1,0:T(8,128)S(1)}, u32[]{:S(2)}) copy-start(f32[5,4,8,128]{3,2,1,0:T(8,128)S(1)} %collective-permute-done.9.one0) | copy-start | bytes 245764
  67.4 12.9 %copy-start.9 = (f32[5,4,8,128]{3,2,1,0:T(8,128)}, f32[5,4,8,128]{3,2,1,0:T(8,128)S(1)}, u32[]{:S(2)}) copy-start(f32[5,4,8,128]{3,2,1,0:T(8,128)S(1)} %collective-permute-done.10.one1) | copy-start | bytes 245764
  70.5 9.9 %copy-start.14 = (f32[5,4,8,128]{3,2,1,0:T(8,128)}, f32[5,4,8,128]{3,2,1,0:T(8,128)S(1)}, u32[]{:S(2)}) copy-start(f32[5,4,8,128]{3,2,1,0:T(8,128)S(1)} %collective-permute-done.11.two1) | copy-start | bytes 245764
  70.5 8.7 %collective-permute-start.12 = (f32[5,16,8,128]{3,2,1,0:T(8,128)S(1)}, f32[5,16,8,128]{3,2,1,0:T(8,128)S(1)}, u32[]{:S(2)}, u32[]{:S(2)}) collective-permute-start(f32[5,16,8,128]{3,2,1,0:T(8,128)S(1)} %dynamic-slice_dynamic-update-slice_fusion), channel_id=1, source_target_pairs={{0,1},{1,0},{2,3},{3,2},{4,5},{5,4},{6,7},{7,6},{8,9},{9,8},{10,11... | collective-permute-start | bytes 983048 | tf_op jit(solution)/shard_map/ppermute | solution.py:743
  70.5 9.8 %collective-permute-start.13 = (f32[5,16,8,128]{3,2,1,0:T(8,128)S(1)}, f32[5,16,8,128]{3,2,1,0:T(8,128)S(1)}, u32[]{:S(2)}, u32[]{:S(2)}) collective-permute-start(f32[5,16,8,128]{3,2,1,0:T(8,128)S(1)} %dynamic-slice_dynamic-update-slice_fusion), channel_id=1, source_target_pairs={{1,2},{2,1},{3,4},{4,3},{5,6},{6,5},{9,10},{10,9},{11,12},{12,11},... | collective-permute-start | bytes 983048 | tf_op jit(solution)/shard_map/ppermute | solution.py:743
  79.2 1.2 copy-start.10
  80.4 0.7 copy-start.11
  94.5 11.3 %all-to-all-start = ((f32[16,5,4,128]{3,2,1,0:T(4,128)}), f32[16,5,4,128]{3,2,1,0:T(4,128)S(1)}, u32[]{:S(2)}, u32[]{:S(2)}) async-start(f32[16,5,4,128]{3,2,1,0:T(4,128)} %get-tuple-element.17), calls=%async_computation | async-start | bytes 327680 | tf_op jit(solution)/shard_map/all_to_all | solution.py:856
  105.8 9.6 %copy-start.12 = (f32[5,7,4,128]{3,2,1,0:T(4,128)}, f32[5,7,4,128]{3,2,1,0:T(4,128)S(1)}, u32[]{:S(2)}) copy-start(f32[5,7,4,128]{3,2,1,0:T(4,128)S(1)} %copy_bitcast_fusion.own) | copy-start | bytes 215044
  105.8 9.5 %collective-permute-start.14 = (f32[5,7,4,128]{3,2,1,0:T(4,128)S(1)}, f32[5,7,4,128]{3,2,1,0:T(4,128)S(1)}, u32[]{:S(2)}, u32[]{:S(2)}) collective-permute-start(f32[5,7,4,128]{3,2,1,0:T(4,128)S(1)} %copy_bitcast_fusion.own), channel_id=1, source_target_pairs={{0,2},{1,3},{2,0},{3,1},{4,6},{5,7},{6,4},{7,5},{8,10},{9,11},{10,... | collective-permute-start | bytes 215048 | tf_op jit(solution)/shard_map/ppermute | solution.py:743
  108.2 7.2 %collective-permute-start.15 = (f32[5,7,4,128]{3,2,1,0:T(4,128)S(1)}, f32[5,7,4,128]{3,2,1,0:T(4,128)S(1)}, u32[]{:S(2)}, u32[]{:S(2)}) collective-permute-start(f32[5,7,4,128]{3,2,1,0:T(4,128)S(1)} %copy_bitcast_fusion.own), channel_id=1, source_target_pairs={{0,1},{1,0},{2,3},{3,2},{4,5},{5,4},{6,7},{7,6},{8,9},{9,8},{10,11... | collective-permute-start | bytes 215048 | tf_op jit(solution)/shard_map/ppermute | solution.py:743
  109.7 5.6 %collective-permute-start.16 = (f32[5,7,4,128]{3,2,1,0:T(4,128)S(1)}, f32[5,7,4,128]{3,2,1,0:T(4,128)S(1)}, u32[]{:S(2)}, u32[]{:S(2)}) collective-permute-start(f32[5,7,4,128]{3,2,1,0:T(4,128)S(1)} %copy_bitcast_fusion.own), channel_id=1, source_target_pairs={{1,2},{2,1},{3,4},{4,3},{5,6},{6,5},{9,10},{10,9},{11,12},{12,11},... | collective-permute-start | bytes 215048 | tf_op jit(solution)/shard_map/ppermute | solution.py:743
  111.6 3.7 %collective-permute-start.17 = (f32[5,7,4,128]{3,2,1,0:T(4,128)S(1)}, f32[5,7,4,128]{3,2,1,0:T(4,128)S(1)}, u32[]{:S(2)}, u32[]{:S(2)}) collective-permute-start(f32[5,7,4,128]{3,2,1,0:T(4,128)S(1)} %copy_bitcast_fusion.own), channel_id=1, source_target_pairs={{2,4},{3,5},{4,2},{5,3},{10,12},{11,13},{12,10},{13,11},{18,20},{1... | collective-permute-start | bytes 215048 | tf_op jit(solution)/shard_map/ppermute | solution.py:743
  115.3 0.6 copy-start.17
  115.3 0.7 copy-start.18
  115.4 0.7 copy-start.19
  115.4 0.7 copy-start.20
  124.5 9.1 %collective-permute-start.18 = (f32[5,8,16,128]{3,2,1,0:T(8,128)}, f32[5,8,16,128]{3,2,1,0:T(8,128)S(1)}, u32[]{:S(2)}, u32[]{:S(2)}) collective-permute-start(f32[5,8,16,128]{3,2,1,0:T(8,128)} %shard_map.34.own), channel_id=1, source_target_pairs={{0,8},{8,0},{16,24},{24,16},{32,40},{40,32},{48,56},{56,48},{64,72... | collective-permute-start | bytes 983048 | tf_op jit(solution)/shard_map/ppermute | solution.py:743
  124.6 13.1 %collective-permute-start.19 = (f32[5,8,16,128]{3,2,1,0:T(8,128)}, f32[5,8,16,128]{3,2,1,0:T(8,128)S(1)}, u32[]{:S(2)}, u32[]{:S(2)}) collective-permute-start(f32[5,8,16,128]{3,2,1,0:T(8,128)} %shard_map.34.own), channel_id=1, source_target_pairs={{8,16},{16,8},{24,32},{32,24},{40,48},{48,40},{56,64},{64,56},{72,... | collective-permute-start | bytes 983048 | tf_op jit(solution)/shard_map/ppermute | solution.py:743
  133.7 17.2 %copy-start.2 = (f32[5,8,16,128]{3,2,1,0:T(8,128)}, f32[5,8,16,128]{3,2,1,0:T(8,128)S(1)}, u32[]{:S(2)}) copy-start(f32[5,8,16,128]{3,2,1,0:T(8,128)S(1)} %collective-permute-done.18.ax0) | copy-start | bytes 983044
  137.8 13.1 %copy-start.3 = (f32[5,8,16,128]{3,2,1,0:T(8,128)}, f32[5,8,16,128]{3,2,1,0:T(8,128)S(1)}, u32[]{:S(2)}) copy-start(f32[5,8,16,128]{3,2,1,0:T(8,128)S(1)} %collective-permute-done.19.ax1) | copy-start | bytes 983044
  137.8 13.0 %collective-permute-start.21 = (f32[5,20,8,128]{3,2,1,0:T(8,128)S(1)}, f32[5,20,8,128]{3,2,1,0:T(8,128)S(1)}, u32[]{:S(2)}, u32[]{:S(2)}) collective-permute-start(f32[5,20,8,128]{3,2,1,0:T(8,128)S(1)} %pad_maximum_fusion.3), channel_id=1, source_target_pairs={{1,2},{2,1},{3,4},{4,3},{5,6},{6,5},{9,10},{10,9},{11,12},{12,11},... | collective-permute-start | bytes 1228808 | tf_op jit(solution)/shard_map/ppermute | solution.py:743
  145.2 5.6 %collective-permute-start.20 = (f32[5,20,8,128]{3,2,1,0:T(8,128)S(1)}, f32[5,20,8,128]{3,2,1,0:T(8,128)S(1)}, u32[]{:S(2)}, u32[]{:S(2)}) collective-permute-start(f32[5,20,8,128]{3,2,1,0:T(8,128)S(1)} %pad_maximum_fusion.2), channel_id=1, source_target_pairs={{0,1},{1,0},{2,3},{3,2},{4,5},{5,4},{6,7},{7,6},{8,9},{9,8},{10,11... | collective-permute-start | bytes 1228808 | tf_op jit(solution)/shard_map/ppermute | solution.py:743
  150.8 0.8 copy-start.5
  151.6 0.7 copy-start.7

commit v2 on v1

--- a/solution.py
+++ b/solution.py
@@ -313,10 +313,10 @@
 
 
 FINE_PLAN = (
-    (((6,), 12, Band(2, 28)), ((2, 18), 4, Band(6, 20))),
-    (((6,), 12, Band(4, 24)), ((4, 18), 2, Band(8, 16))),
-    (((8,), 8, Band(6, 20)), ((6, 16), 2, Band(8, 16))),
-    (((8,), 8, Band(8, 16)),),
+    (((6,), 12, Band(2, 28), 3), ((2, 18), 4, Band(6, 20), 2)),
+    (((6,), 12, Band(4, 24), 2), ((4, 18), 2, Band(8, 16), 2)),
+    (((8,), 8, Band(6, 20), 4), ((6, 16), 2, Band(8, 16), 2)),
+    (((8,), 8, Band(8, 16), 4),),
 )
 
 
@@ -353,8 +353,8 @@
             else:
                 store_row(target, prim, r, cols, new)
 
-        for begins, count, band in FINE_PLAN[k]:
-            level.rows(source, source_prim, begins, count, band, sink)
+        for begins, count, band, unroll in FINE_PLAN[k]:
+            level.rows(source, source_prim, begins, count, band, sink, unroll)
         source, source_prim = target, target_prim
     if slabs:
         for c in range(5):
@@ -460,7 +460,7 @@
             res[c, r - 2] = 0.5 * total[c]
 
     level = Level(LANES, ShiftedRows(fields, 6), carry, shift, matrix)
-    level.rows(w, prim, (2,), 8, Band(8, 16), sink)
+    level.rows(w, prim, (2,), 8, Band(8, 16), sink, 4)
     low = pick((LANES, LANES), lambda a, b: a // 2 == b)
     high = pick((LANES, LANES), lambda a, b: a // 2 + 64 == b)
     packed = matmul(0.125 * restrict_rows(own, pair, 8, 16), low)
@@ -482,7 +482,7 @@
 
 def fine_residual(ends, pos, own, halos, fields):
     scratch = [vmem(5, 12, FINE_COLS, LANES), vmem(3, 12, FINE_COLS, LANES)]
-    scratch += [vmem(5, 8, 16, LANES), vmem(1, 12, 16, LANES), vmem(2, 12, 32, LANES), MATRIX]
+    scratch += [vmem(5, 8, 16, LANES), vmem(1, 12, 16, LANES), vmem(4, 12, 32, LANES), MATRIX]
     scratch += [vmem(16, LANES)]
     return call(
         functools.partial(fine_residual_kernel, ends),
@@ -575,13 +575,13 @@
 
 
 MIDDLE_PLAN = (
-    (((6,), 8, Band(2, 20), 2), ((2, 14), 4, Band(6, 12), 1)),
-    (((6,), 8, Band(4, 16), 2), ((4, 14), 2, Band(8, 8), 2)),
-    (((8,), 4, Band(6, 12), 2), ((6, 12), 2, Band(8, 8), 2)),
+    (((6,), 8, Band(2, 20), 4), ((2, 14), 4, Band(6, 12), 2)),
+    (((6,), 8, Band(4, 16), 4), ((4, 14), 2, Band(8, 8), 2)),
+    (((8,), 4, Band(6, 12), 4), ((6, 12), 2, Band(8, 8), 2)),
 )
 COARSE_PLAN = (
-    (((6,), 2, Band(2, 12), 2), ((2, 8), 4, Band(4, 8), 2)),
-    (((4,), 6, Band(4, 8), 3),),
+    (((6,), 2, Band(2, 12), 2), ((2, 8), 4, Band(4, 8), 4)),
+    (((4,), 6, Band(4, 8), 6),),
     (((6,), 2, Band(6, 4), 2),),
 )
 
@@ -670,7 +670,7 @@
     ax_extent = 2 * ends[0]
     origin = 2 * jnp.clip(pos[0] - 3, 0, ends[0] - 7)
 
-    @pl.loop(0, 14)
+    @pl.loop(0, 14, unroll=2)
     def _(r):
         g = begin + r
         at = mirror(g, ax_extent)
@@ -720,7 +720,7 @@
     scratch = [vmem(24, 35 * LANES)]
     cols = COARSE_COLS
     scratch += [vmem(5, 14, cols, LANES)] * 4 + [vmem(3, 14, cols, LANES)] * 3
-    scratch += [vmem(14, cols, LANES), vmem(2, 12, 16, LANES), vmem(4, 12, 24, LANES), MATRIX]
+    scratch += [vmem(14, cols, LANES), vmem(2, 12, 16, LANES), vmem(8, 12, 24, LANES), MATRIX]
     scratch += [vmem(160, LANES), vmem(160, LANES)]
     return call(
         functools.partial(coarse_kernel, ends),

time: 169 us -> 164 us (0.970)
  Pallas kernels: 68.5 us -> 64 us
    pallas_call x8, Pallas kernels: 68.5 us -> 64 us  [call(): pl.pallas_call(kernel, out_shape=outs[0] if single else outs, in_specs=sp...]
where the time goes in v2:
time: 164 us; the launch traced here: 163 us
  Pallas kernels  64 us (39%)
  starting transfers between devices  55.7 us (34%)
  waiting for transfers between devices  34.5 us (21%)
  local copies, waits for them, and re-layouts  8.11 us (5%)
    pallas_call x8, Pallas kernels, call(): pl.pallas_call(kernel, out_shape=outs[0] if single else outs, in_specs=sp...  64 us
    ppermute x22, starting transfers between devices, swapped(): return lax.ppermute(x, axis, sorted(pairs))  50.1 us
    ppermute x22, waiting for transfers between devices, swapped(): return lax.ppermute(x, axis, sorted(pairs))  28.9 us
    unnamed x50, local copies, waits for them, and re-layouts  5.98 us
    all_to_all x1, starting transfers between devices, per_device(): column = lax.all_to_all(block, 'ax', 0, 0)  5.66 us
    all_to_all x1, waiting for transfers between devices, per_device(): column = lax.all_to_all(block, 'ax', 0, 0)  5.6 us
  transfers between devices with their start and end apart: 23, of which 11 were waited for; matrix products, arithmetic and copies ran while one was open for 2% of the time, Pallas kernels for 6%

profile of v2, /device:TPU:3, one launch (start us, length us, event | category | flops | bytes accessed | tf_op | source)
XLA Modules:
  0.0 163.4 jit_solution(1712951700606520957)
XLA Ops:
  0.0 1.3 collective-permute-start
  1.3 3.8 %collective-permute-start.1 = (f32[5,8,16,128]{3,2,1,0:T(8,128)}, f32[5,8,16,128]{3,2,1,0:T(8,128)S(1)}, u32[]{:S(2)}, u32[]{:S(2)}) collective-permute-start(f32[5,8,16,128]{3,2,1,0:T(8,128)} %own.1), channel_id=1, source_target_pairs={{8,16},{16,8},{24,32},{32,24},{40,48},{48,40},{56,64},{64,56},{72,... | collective-permute-start | bytes 983048 | tf_op jit(solution)/shard_map/ppermute | solution.py:743
  5.1 1.0 constant_dynamic-slice_fusion.8
  6.1 2.7 %collective-permute-done.ax0 = f32[5,8,16,128]{3,2,1,0:T(8,128)S(1)} collective-permute-done((f32[5,8,16,128]{3,2,1,0:T(8,128)}, f32[5,8,16,128]{3,2,1,0:T(8,128)S(1)}, u32[]{:S(2)}, u32[]{:S(2)}) %collective-permute-start) | collective-permute-done | bytes 327712 | tf_op jit(solution)/shard_map/ppermute | solution.py:743
  8.8 5.0 %collective-permute-done.1.ax1 = f32[5,8,16,128]{3,2,1,0:T(8,128)S(1)} collective-permute-done((f32[5,8,16,128]{3,2,1,0:T(8,128)}, f32[5,8,16,128]{3,2,1,0:T(8,128)S(1)}, u32[]{:S(2)}, u32[]{:S(2)}) %collective-permute-start.1) | collective-permute-done | bytes 327712 | tf_op jit(solution)/shard_map/ppermute | solution.py:743
  13.9 5.2 %collective-permute-start.3 = (f32[5,20,8,128]{3,2,1,0:T(8,128)S(1)}, f32[5,20,8,128]{3,2,1,0:T(8,128)S(1)}, u32[]{:S(2)}, u32[]{:S(2)}) collective-permute-start(f32[5,20,8,128]{3,2,1,0:T(8,128)S(1)} %pad_maximum_fusion.1), channel_id=1, source_target_pairs={{1,2},{2,1},{3,4},{4,3},{5,6},{6,5},{9,10},{10,9},{11,12},{12,11},... | collective-permute-start | bytes 1228808 | tf_op jit(solution)/shard_map/ppermute | solution.py:743
  19.2 0.1 collective-permute-start.2
  19.3 0.6 pad_add_fusion.pos
  19.9 3.8 %shard_map.28.fields = f32[3,24,40,128]{3,2,1,0:T(8,128)} custom-call(s32[2]{0:T(128)} %pad_add_fusion.pos, s32[128,4,128]{2,1,0:T(4,128)} %code.5), custom_call_target="tpu_custom_call" | custom-call | flops 1000000 | bytes 1736712 | tf_op jit(solution)/shard_map/pallas_call | solution.py:377
  23.7 1.1 collective-permute-done.3.xs1
  24.8 0.8 copy-done.4
  25.5 0.7 copy-done.6
  26.3 15.1 %shard_map.29 = (f32[5,8,16,128]{3,2,1,0:T(8,128)}, f32[5,2,16,128]{3,2,1,0:T(8,128)}, f32[5,2,16,128]{3,2,1,0:T(8,128)}, f32[5,8,2,128]{3,2,1,0:T(2,128)}, f32[5,8,2,128]{3,2,1,0:T(2,128)}) custom-call(s32[2]{0:T(128)} %pad_add_fusion.pos, f32[5,8,16,128]{3,2,1,0:T(8,128)} %own.1, f32[5,8,16,128]{3,2,1,0:T(8,128)} %copy-done, f32[5,8,16,128]{3,2,1,0:T(8,128)} %copy-done.1, ...), custom_call_target="tpu_custom_call" | custom-call | flops 80000000 | bytes 3850248 | tf_op jit(solution)/shard_map/pallas_call | solution.py:377
  41.4 3.8 %collective-permute-start.5 = (f32[5,2,16,128]{3,2,1,0:T(8,128)}, f32[5,2,16,128]{3,2,1,0:T(8,128)S(1)}, u32[]{:S(2)}, u32[]{:S(2)}) collective-permute-start(f32[5,2,16,128]{3,2,1,0:T(8,128)} %get-tuple-element.14), channel_id=1, source_target_pairs={{8,16},{16,8},{24,32},{32,24},{40,48},{48,40},{56,64},{64,56},{72,... | collective-permute-start | bytes 245768 | tf_op jit(solution)/shard_map/ppermute | solution.py:743
  45.2 0.1 collective-permute-start.6
  45.2 3.9 %collective-permute-start.7 = (f32[5,8,2,128]{3,2,1,0:T(2,128)}, f32[5,8,2,128]{3,2,1,0:T(2,128)S(1)}, u32[]{:S(2)}, u32[]{:S(2)}) collective-permute-start(f32[5,8,2,128]{3,2,1,0:T(2,128)} %get-tuple-element.16), channel_id=1, source_target_pairs={{1,2},{2,1},{3,4},{4,3},{5,6},{6,5},{9,10},{10,9},{11,12},{12,11},... | collective-permute-start | bytes 122888 | tf_op jit(solution)/shard_map/ppermute | solution.py:743
  49.2 0.0 collective-permute-done.6.xs0
  49.2 1.9 %collective-permute-done.7.xs1 = f32[5,8,2,128]{3,2,1,0:T(2,128)S(1)} collective-permute-done((f32[5,8,2,128]{3,2,1,0:T(2,128)}, f32[5,8,2,128]{3,2,1,0:T(2,128)S(1)}, u32[]{:S(2)}, u32[]{:S(2)}) %collective-permute-start.7) | collective-permute-done | bytes 40992 | tf_op jit(solution)/shard_map/ppermute | solution.py:743
  51.1 0.6 copy-done.22
  51.7 0.0 copy-done.15
  51.7 0.0 copy-done.16
  51.7 4.1 %shard_map.30.own = f32[5,4,8,128]{3,2,1,0:T(8,128)} custom-call(s32[2]{0:T(128)} %pad_add_fusion.pos, f32[5,8,16,128]{3,2,1,0:T(8,128)} %get-tuple-element.12.own.smoothed, f32[5,2,16,128]{3,2,1,0:T(8,128)} %copy-done.15, f32[5,2,16,128]{3,2,1,0:T(8,128)} %copy-done.16, f32[5,8,2,128]{3,2,1,0:T(2,128)} %copy-done.21, f32[5,8,2,128]{3,2,1,0:T(2,128)} %copy-done.22, ...), custom_call_target="tpu_custom_call" | custom-call | flops 8000000 | bytes 2129928 | tf_op jit(solution)/shard_map/pallas_call | solution.py:377
  55.8 1.6 %collective-permute-start.8 = (f32[5,4,8,128]{3,2,1,0:T(8,128)}, f32[5,4,8,128]{3,2,1,0:T(8,128)S(1)}, u32[]{:S(2)}, u32[]{:S(2)}) collective-permute-start(f32[5,4,8,128]{3,2,1,0:T(8,128)} %shard_map.30.own), channel_id=1, source_target_pairs={{0,16},{8,24},{16,0},{24,8},{32,48},{40,56},{48,32},{56,40},{64,80... | collective-permute-start | bytes 245768 | tf_op jit(solution)/shard_map/ppermute | solution.py:743
  57.5 0.7 collective-permute-start.9
  58.2 3.1 %collective-permute-start.10 = (f32[5,4,8,128]{3,2,1,0:T(8,128)}, f32[5,4,8,128]{3,2,1,0:T(8,128)S(1)}, u32[]{:S(2)}, u32[]{:S(2)}) collective-permute-start(f32[5,4,8,128]{3,2,1,0:T(8,128)} %shard_map.30.own), channel_id=1, source_target_pairs={{8,16},{16,8},{24,32},{32,24},{40,48},{48,40},{56,64},{64,56},{72,... | collective-permute-start | bytes 245768 | tf_op jit(solution)/shard_map/ppermute | solution.py:743
  61.3 3.1 %collective-permute-start.11 = (f32[5,4,8,128]{3,2,1,0:T(8,128)}, f32[5,4,8,128]{3,2,1,0:T(8,128)S(1)}, u32[]{:S(2)}, u32[]{:S(2)}) collective-permute-start(f32[5,4,8,128]{3,2,1,0:T(8,128)} %shard_map.30.own), channel_id=1, source_target_pairs={{16,32},{24,40},{32,16},{40,24},{48,64},{56,72},{64,48},{72,56},{8... | collective-permute-start | bytes 245768 | tf_op jit(solution)/shard_map/ppermute | solution.py:743
  64.4 0.0 collective-permute-done.8.two0
  64.4 0.0 collective-permute-done.9.one0
  64.5 0.9 constant_dynamic-update-slice_fusion.1
  65.4 0.9 collective-permute-done.10.one1
  66.3 3.0 %collective-permute-done.11.two1 = f32[5,4,8,128]{3,2,1,0:T(8,128)S(1)} collective-permute-done((f32[5,4,8,128]{3,2,1,0:T(8,128)}, f32[5,4,8,128]{3,2,1,0:T(8,128)S(1)}, u32[]{:S(2)}, u32[]{:S(2)}) %collective-permute-start.11) | collective-permute-done | bytes 81952 | tf_op jit(solution)/shard_map/ppermute | solution.py:743
  69.3 0.0 collective-permute-start.12
  69.4 5.1 %collective-permute-start.13 = (f32[5,16,8,128]{3,2,1,0:T(8,128)S(1)}, f32[5,16,8,128]{3,2,1,0:T(8,128)S(1)}, u32[]{:S(2)}, u32[]{:S(2)}) collective-permute-start(f32[5,16,8,128]{3,2,1,0:T(8,128)S(1)} %dynamic-slice_dynamic-update-slice_fusion), channel_id=1, source_target_pairs={{1,2},{2,1},{3,4},{4,3},{5,6},{6,5},{9,10},{10,9},{11,12},{12,11},... | collective-permute-start | bytes 983048 | tf_op jit(solution)/shard_map/ppermute | solution.py:743
  74.4 3.6 %shard_map.31.fields = f32[3,20,32,128]{3,2,1,0:T(8,128)} custom-call(s32[2]{0:T(128)} %pad_add_fusion.pos, s32[128,4,128]{2,1,0:T(4,128)} %code.5), custom_call_target="tpu_custom_call" | custom-call | flops 1000000 | bytes 1245192 | tf_op jit(solution)/shard_map/pallas_call | solution.py:377
  78.1 1.1 collective-permute-done.13.xs1
  79.2 0.7 copy-done.11
  79.9 12.0 %shard_map.32 = (f32[16,5,4,128]{3,2,1,0:T(4,128)}, f32[5,4,8,128]{3,2,1,0:T(8,128)}) custom-call(s32[2]{0:T(128)} %pad_add_fusion.pos, f32[5,4,8,128]{3,2,1,0:T(8,128)} %copy-done.13, f32[5,4,8,128]{3,2,1,0:T(8,128)} %copy-done.8, f32[5,4,8,128]{3,2,1,0:T(8,128)} %shard_map.30.own, f32[5,4,8,128]{3,2,1,0:T(8,128)} %copy-done.9, ...), custom_call_target="tpu_custom_call" | custom-call | flops 60000000 | bytes 2293768 | tf_op jit(solution)/shard_map/pallas_call | solution.py:377
  92.0 5.7 %all-to-all-start = ((f32[16,5,4,128]{3,2,1,0:T(4,128)}), f32[16,5,4,128]{3,2,1,0:T(4,128)S(1)}, u32[]{:S(2)}, u32[]{:S(2)}) async-start(f32[16,5,4,128]{3,2,1,0:T(4,128)} %get-tuple-element.17), calls=%async_computation | async-start | bytes 327680 | tf_op jit(solution)/shard_map/all_to_all | solution.py:856
  97.6 5.6 %all-to-all-done = f32[16,5,4,128]{3,2,1,0:T(4,128)S(1)} async-done(((f32[16,5,4,128]{3,2,1,0:T(4,128)}), f32[16,5,4,128]{3,2,1,0:T(4,128)S(1)}, u32[]{:S(2)}, u32[]{:S(2)}) %all-to-all-start) | async-done | bytes 163872 | tf_op jit(solution)/shard_map/all_to_all | solution.py:856
  103.3 0.0 copy-start.12
  103.3 2.2 %collective-permute-start.14 = (f32[5,7,4,128]{3,2,1,0:T(4,128)S(1)}, f32[5,7,4,128]{3,2,1,0:T(4,128)S(1)}, u32[]{:S(2)}, u32[]{:S(2)}) collective-permute-start(f32[5,7,4,128]{3,2,1,0:T(4,128)S(1)} %copy_bitcast_fusion.own), channel_id=1, source_target_pairs={{0,2},{1,3},{2,0},{3,1},{4,6},{5,7},{6,4},{7,5},{8,10},{9,11},{10,... | collective-permute-start | bytes 215048 | tf_op jit(solution)/shard_map/ppermute | solution.py:743
  105.5 1.6 collective-permute-start.15
  107.0 1.9 %collective-permute-start.16 = (f32[5,7,4,128]{3,2,1,0:T(4,128)S(1)}, f32[5,7,4,128]{3,2,1,0:T(4,128)S(1)}, u32[]{:S(2)}, u32[]{:S(2)}) collective-permute-start(f32[5,7,4,128]{3,2,1,0:T(4,128)S(1)} %copy_bitcast_fusion.own), channel_id=1, source_target_pairs={{1,2},{2,1},{3,4},{4,3},{5,6},{6,5},{9,10},{10,9},{11,12},{12,11},... | collective-permute-start | bytes 215048 | tf_op jit(solution)/shard_map/ppermute | solution.py:743
  109.0 0.7 collective-permute-start.17
  109.6 3.0 %shard_map.33.fields = f32[3,14,24,128]{3,2,1,0:T(8,128)} custom-call(s32[2]{0:T(128)} %pad_add_fusion.pos, s32[128,4,128]{2,1,0:T(4,128)} %code.5), custom_call_target="tpu_custom_call" | custom-call | flops 1000000 | bytes 778248 | tf_op jit(solution)/shard_map/pallas_call | solution.py:377
  112.6 0.0 collective-permute-done.14.two0
  112.6 0.0 collective-permute-done.15.one0
  112.7 0.0 collective-permute-done.16.one1
  112.7 0.6 copy-done.17
  113.3 0.0 copy-done.18
  113.3 0.0 copy-done.19
  113.3 0.0 copy-done.20
  113.4 7.1 %shard_map.34.own = f32[5,8,16,128]{3,2,1,0:T(8,128)} custom-call(s32[2]{0:T(128)} %pad_add_fusion.pos, f32[5,7,4,128]{3,2,1,0:T(4,128)} %copy-done.12, f32[5,7,4,128]{3,2,1,0:T(4,128)} %copy-done.17, f32[5,7,4,128]{3,2,1,0:T(4,128)} %copy-done.18, f32[5,7,4,128]{3,2,1,0:T(4,128)} %copy-done.19, f32[5,7,4,128]{3,2,1,0:T(4,128)} %copy-done.20, ...), custom_call_target="tpu_custom_call" | custom-call | flops 20000000 | bytes 1611784 | tf_op jit(solution)/shard_map/pallas_call | solution.py:377
  120.4 0.1 collective-permute-start.18
  120.5 4.4 %collective-permute-start.19 = (f32[5,8,16,128]{3,2,1,0:T(8,128)}, f32[5,8,16,128]{3,2,1,0:T(8,128)S(1)}, u32[]{:S(2)}, u32[]{:S(2)}) collective-permute-start(f32[5,8,16,128]{3,2,1,0:T(8,128)} %shard_map.34.own), channel_id=1, source_target_pairs={{8,16},{16,8},{24,32},{32,24},{40,48},{48,40},{56,64},{64,56},{72,... | collective-permute-start | bytes 983048 | tf_op jit(solution)/shard_map/ppermute | solution.py:743
  124.9 1.0 constant_dynamic-slice_fusion.1
  125.9 3.6 %collective-permute-done.18.ax0 = f32[5,8,16,128]{3,2,1,0:T(8,128)S(1)} collective-permute-done((f32[5,8,16,128]{3,2,1,0:T(8,128)}, f32[5,8,16,128]{3,2,1,0:T(8,128)S(1)}, u32[]{:S(2)}, u32[]{:S(2)}) %collective-permute-start.18) | collective-permute-done | bytes 327712 | tf_op jit(solution)/shard_map/ppermute | solution.py:743
  129.6 4.1 %collective-permute-done.19.ax1 = f32[5,8,16,128]{3,2,1,0:T(8,128)S(1)} collective-permute-done((f32[5,8,16,128]{3,2,1,0:T(8,128)}, f32[5,8,16,128]{3,2,1,0:T(8,128)S(1)}, u32[]{:S(2)}, u32[]{:S(2)}) %collective-permute-start.19) | collective-permute-done | bytes 327712 | tf_op jit(solution)/shard_map/ppermute | solution.py:743
  133.7 7.4 %collective-permute-start.21 = (f32[5,20,8,128]{3,2,1,0:T(8,128)S(1)}, f32[5,20,8,128]{3,2,1,0:T(8,128)S(1)}, u32[]{:S(2)}, u32[]{:S(2)}) collective-permute-start(f32[5,20,8,128]{3,2,1,0:T(8,128)S(1)} %pad_maximum_fusion.3), channel_id=1, source_target_pairs={{1,2},{2,1},{3,4},{4,3},{5,6},{6,5},{9,10},{10,9},{11,12},{12,11},... | collective-permute-start | bytes 1228808 | tf_op jit(solution)/shard_map/ppermute | solution.py:743
  141.1 0.1 collective-permute-start.20
  141.2 5.5 %collective-permute-done.21.xs1 = f32[5,20,8,128]{3,2,1,0:T(8,128)S(1)} collective-permute-done((f32[5,20,8,128]{3,2,1,0:T(8,128)S(1)}, f32[5,20,8,128]{3,2,1,0:T(8,128)S(1)}, u32[]{:S(2)}, u32[]{:S(2)}) %collective-permute-start.21) | collective-permute-done | bytes 409632 | tf_op jit(solution)/shard_map/ppermute | solution.py:743
  146.7 0.7 copy-done.5
  147.5 0.7 copy-done.7
  148.2 15.2 %shard_map.35 = f32[5,8,16,128]{3,2,1,0:T(8,128)} custom-call(s32[2]{0:T(128)} %pad_add_fusion.pos, f32[5,8,16,128]{3,2,1,0:T(8,128)} %shard_map.34.own, f32[5,8,16,128]{3,2,1,0:T(8,128)} %copy-done.2, f32[5,8,16,128]{3,2,1,0:T(8,128)} %copy-done.3, f32[5,20,8,128]{3,2,1,0:T(8,128)} %copy-done.7, f32[5,20,8,128]{3,2,1,0:T(8,128)} %copy-done.5, ...), custom_call_target="tpu_custom_call" | custom-call | flops 80000000 | bytes 3604488 | tf_op jit(solution)/shard_map/pallas_call | solution.py:377
  (53 shorter events, 0.3 us)
Async XLA Ops:
  0.0 8.8 %collective-permute-start = (f32[5,8,16,128]{3,2,1,0:T(8,128)}, f32[5,8,16,128]{3,2,1,0:T(8,128)S(1)}, u32[]{:S(2)}, u32[]{:S(2)}) collective-permute-start(f32[5,8,16,128]{3,2,1,0:T(8,128)} %own.1), channel_id=1, source_target_pairs={{0,8},{8,0},{16,24},{24,16},{32,40},{40,32},{48,56},{56,48},{64,72... | collective-permute-start | bytes 983048 | tf_op jit(solution)/shard_map/ppermute | solution.py:743
  1.3 12.5 %collective-permute-start.1 = (f32[5,8,16,128]{3,2,1,0:T(8,128)}, f32[5,8,16,128]{3,2,1,0:T(8,128)S(1)}, u32[]{:S(2)}, u32[]{:S(2)}) collective-permute-start(f32[5,8,16,128]{3,2,1,0:T(8,128)} %own.1), channel_id=1, source_target_pairs={{8,16},{16,8},{24,32},{32,24},{40,48},{48,40},{56,64},{64,56},{72,... | collective-permute-start | bytes 983048 | tf_op jit(solution)/shard_map/ppermute | solution.py:743
  8.8 14.9 %copy-start = (f32[5,8,16,128]{3,2,1,0:T(8,128)}, f32[5,8,16,128]{3,2,1,0:T(8,128)S(1)}, u32[]{:S(2)}) copy-start(f32[5,8,16,128]{3,2,1,0:T(8,128)S(1)} %collective-permute-done.ax0) | copy-start | bytes 983044
  13.8 9.9 %copy-start.1 = (f32[5,8,16,128]{3,2,1,0:T(8,128)}, f32[5,8,16,128]{3,2,1,0:T(8,128)S(1)}, u32[]{:S(2)}) copy-start(f32[5,8,16,128]{3,2,1,0:T(8,128)S(1)} %collective-permute-done.1.ax1) | copy-start | bytes 983044
  13.9 10.9 %collective-permute-start.3 = (f32[5,20,8,128]{3,2,1,0:T(8,128)S(1)}, f32[5,20,8,128]{3,2,1,0:T(8,128)S(1)}, u32[]{:S(2)}, u32[]{:S(2)}) collective-permute-start(f32[5,20,8,128]{3,2,1,0:T(8,128)S(1)} %pad_maximum_fusion.1), channel_id=1, source_target_pairs={{1,2},{2,1},{3,4},{4,3},{5,6},{6,5},{9,10},{10,9},{11,12},{12,11},... | collective-permute-start | bytes 1228808 | tf_op jit(solution)/shard_map/ppermute | solution.py:743
  19.2 5.6 %collective-permute-start.2 = (f32[5,20,8,128]{3,2,1,0:T(8,128)S(1)}, f32[5,20,8,128]{3,2,1,0:T(8,128)S(1)}, u32[]{:S(2)}, u32[]{:S(2)}) collective-permute-start(f32[5,20,8,128]{3,2,1,0:T(8,128)S(1)} %pad_maximum_fusion), channel_id=1, source_target_pairs={{0,1},{1,0},{2,3},{3,2},{4,5},{5,4},{6,7},{7,6},{8,9},{9,8},{10,11... | collective-permute-start | bytes 1228808 | tf_op jit(solution)/shard_map/ppermute | solution.py:743
  24.7 0.8 copy-start.4
  25.5 0.7 copy-start.6
  41.4 9.7 %collective-permute-start.4 = (f32[5,2,16,128]{3,2,1,0:T(8,128)}, f32[5,2,16,128]{3,2,1,0:T(8,128)S(1)}, u32[]{:S(2)}, u32[]{:S(2)}) collective-permute-start(f32[5,2,16,128]{3,2,1,0:T(8,128)} %get-tuple-element.13), channel_id=1, source_target_pairs={{0,8},{8,0},{16,24},{24,16},{32,40},{40,32},{48,56},{56,48},{64,72... | collective-permute-start | bytes 245768 | tf_op jit(solution)/shard_map/ppermute | solution.py:743
  41.4 9.7 %collective-permute-start.5 = (f32[5,2,16,128]{3,2,1,0:T(8,128)}, f32[5,2,16,128]{3,2,1,0:T(8,128)S(1)}, u32[]{:S(2)}, u32[]{:S(2)}) collective-permute-start(f32[5,2,16,128]{3,2,1,0:T(8,128)} %get-tuple-element.14), channel_id=1, source_target_pairs={{8,16},{16,8},{24,32},{32,24},{40,48},{48,40},{56,64},{64,56},{72,... | collective-permute-start | bytes 245768 | tf_op jit(solution)/shard_map/ppermute | solution.py:743
  45.2 4.0 %collective-permute-start.6 = (f32[5,8,2,128]{3,2,1,0:T(2,128)}, f32[5,8,2,128]{3,2,1,0:T(2,128)S(1)}, u32[]{:S(2)}, u32[]{:S(2)}) collective-permute-start(f32[5,8,2,128]{3,2,1,0:T(2,128)} %get-tuple-element.15), channel_id=1, source_target_pairs={{0,1},{1,0},{2,3},{3,2},{4,5},{5,4},{6,7},{7,6},{8,9},{9,8},{10,11... | collective-permute-start | bytes 122888 | tf_op jit(solution)/shard_map/ppermute | solution.py:743
  45.2 5.8 %collective-permute-start.7 = (f32[5,8,2,128]{3,2,1,0:T(2,128)}, f32[5,8,2,128]{3,2,1,0:T(2,128)S(1)}, u32[]{:S(2)}, u32[]{:S(2)}) collective-permute-start(f32[5,8,2,128]{3,2,1,0:T(2,128)} %get-tuple-element.16), channel_id=1, source_target_pairs={{1,2},{2,1},{3,4},{4,3},{5,6},{6,5},{9,10},{10,9},{11,12},{12,11},... | collective-permute-start | bytes 122888 | tf_op jit(solution)/shard_map/ppermute | solution.py:743
  49.2 1.9 %copy-start.21 = (f32[5,8,2,128]{3,2,1,0:T(2,128)}, f32[5,8,2,128]{3,2,1,0:T(2,128)S(1)}, u32[]{:S(2)}) copy-start(f32[5,8,2,128]{3,2,1,0:T(2,128)S(1)} %collective-permute-done.6.xs0) | copy-start | bytes 122884
  51.1 0.6 copy-start.22
  51.1 0.6 copy-start.15
  51.1 0.7 copy-start.16
  55.8 8.5 %collective-permute-start.8 = (f32[5,4,8,128]{3,2,1,0:T(8,128)}, f32[5,4,8,128]{3,2,1,0:T(8,128)S(1)}, u32[]{:S(2)}, u32[]{:S(2)}) collective-permute-start(f32[5,4,8,128]{3,2,1,0:T(8,128)} %shard_map.30.own), channel_id=1, source_target_pairs={{0,16},{8,24},{16,0},{24,8},{32,48},{40,56},{48,32},{56,40},{64,80... | collective-permute-start | bytes 245768 | tf_op jit(solution)/shard_map/ppermute | solution.py:743
  57.5 6.9 %collective-permute-start.9 = (f32[5,4,8,128]{3,2,1,0:T(8,128)}, f32[5,4,8,128]{3,2,1,0:T(8,128)S(1)}, u32[]{:S(2)}, u32[]{:S(2)}) collective-permute-start(f32[5,4,8,128]{3,2,1,0:T(8,128)} %shard_map.30.own), channel_id=1, source_target_pairs={{0,8},{8,0},{16,24},{24,16},{32,40},{40,32},{48,56},{56,48},{64,72... | collective-permute-start | bytes 245768 | tf_op jit(solution)/shard_map/ppermute | solution.py:743
  58.2 8.1 %collective-permute-start.10 = (f32[5,4,8,128]{3,2,1,0:T(8,128)}, f32[5,4,8,128]{3,2,1,0:T(8,128)S(1)}, u32[]{:S(2)}, u32[]{:S(2)}) collective-permute-start(f32[5,4,8,128]{3,2,1,0:T(8,128)} %shard_map.30.own), channel_id=1, source_target_pairs={{8,16},{16,8},{24,32},{32,24},{40,48},{48,40},{56,64},{64,56},{72,... | collective-permute-start | bytes 245768 | tf_op jit(solution)/shard_map/ppermute | solution.py:743
  61.3 8.0 %collective-permute-start.11 = (f32[5,4,8,128]{3,2,1,0:T(8,128)}, f32[5,4,8,128]{3,2,1,0:T(8,128)S(1)}, u32[]{:S(2)}, u32[]{:S(2)}) collective-permute-start(f32[5,4,8,128]{3,2,1,0:T(8,128)} %shard_map.30.own), channel_id=1, source_target_pairs={{16,32},{24,40},{32,16},{40,24},{48,64},{56,72},{64,48},{72,56},{8... | collective-permute-start | bytes 245768 | tf_op jit(solution)/shard_map/ppermute | solution.py:743
  64.4 14.8 %copy-start.13 = (f32[5,4,8,128]{3,2,1,0:T(8,128)}, f32[5,4,8,128]{3,2,1,0:T(8,128)S(1)}, u32[]{:S(2)}) copy-start(f32[5,4,8,128]{3,2,1,0:T(8,128)S(1)} %collective-permute-done.8.two0) | copy-start | bytes 245764
  64.4 14.8 %copy-start.8 = (f32[5,4,8,128]{3,2,1,0:T(8,128)}, f32[5,4,8,128]{3,2,1,0:T(8,128)S(1)}, u32[]{:S(2)}) copy-start(f32[5,4,8,128]{3,2,1,0:T(8,128)S(1)} %collective-permute-done.9.one0) | copy-start | bytes 245764
  66.3 12.9 %copy-start.9 = (f32[5,4,8,128]{3,2,1,0:T(8,128)}, f32[5,4,8,128]{3,2,1,0:T(8,128)S(1)}, u32[]{:S(2)}) copy-start(f32[5,4,8,128]{3,2,1,0:T(8,128)S(1)} %collective-permute-done.10.one1) | copy-start | bytes 245764
  69.3 9.9 %copy-start.14 = (f32[5,4,8,128]{3,2,1,0:T(8,128)}, f32[5,4,8,128]{3,2,1,0:T(8,128)S(1)}, u32[]{:S(2)}) copy-start(f32[5,4,8,128]{3,2,1,0:T(8,128)S(1)} %collective-permute-done.11.two1) | copy-start | bytes 245764
  69.3 8.7 %collective-permute-start.12 = (f32[5,16,8,128]{3,2,1,0:T(8,128)S(1)}, f32[5,16,8,128]{3,2,1,0:T(8,128)S(1)}, u32[]{:S(2)}, u32[]{:S(2)}) collective-permute-start(f32[5,16,8,128]{3,2,1,0:T(8,128)S(1)} %dynamic-slice_dynamic-update-slice_fusion), channel_id=1, source_target_pairs={{0,1},{1,0},{2,3},{3,2},{4,5},{5,4},{6,7},{7,6},{8,9},{9,8},{10,11... | collective-permute-start | bytes 983048 | tf_op jit(solution)/shard_map/ppermute | solution.py:743
  69.4 9.8 %collective-permute-start.13 = (f32[5,16,8,128]{3,2,1,0:T(8,128)S(1)}, f32[5,16,8,128]{3,2,1,0:T(8,128)S(1)}, u32[]{:S(2)}, u32[]{:S(2)}) collective-permute-start(f32[5,16,8,128]{3,2,1,0:T(8,128)S(1)} %dynamic-slice_dynamic-update-slice_fusion), channel_id=1, source_target_pairs={{1,2},{2,1},{3,4},{4,3},{5,6},{6,5},{9,10},{10,9},{11,12},{12,11},... | collective-permute-start | bytes 983048 | tf_op jit(solution)/shard_map/ppermute | solution.py:743
  78.1 1.2 copy-start.10
  79.2 0.7 copy-start.11
  92.0 11.3 %all-to-all-start = ((f32[16,5,4,128]{3,2,1,0:T(4,128)}), f32[16,5,4,128]{3,2,1,0:T(4,128)S(1)}, u32[]{:S(2)}, u32[]{:S(2)}) async-start(f32[16,5,4,128]{3,2,1,0:T(4,128)} %get-tuple-element.17), calls=%async_computation | async-start | bytes 327680 | tf_op jit(solution)/shard_map/all_to_all | solution.py:856
  103.3 9.4 %copy-start.12 = (f32[5,7,4,128]{3,2,1,0:T(4,128)}, f32[5,7,4,128]{3,2,1,0:T(4,128)S(1)}, u32[]{:S(2)}) copy-start(f32[5,7,4,128]{3,2,1,0:T(4,128)S(1)} %copy_bitcast_fusion.own) | copy-start | bytes 215044
  103.3 9.4 %collective-permute-start.14 = (f32[5,7,4,128]{3,2,1,0:T(4,128)S(1)}, f32[5,7,4,128]{3,2,1,0:T(4,128)S(1)}, u32[]{:S(2)}, u32[]{:S(2)}) collective-permute-start(f32[5,7,4,128]{3,2,1,0:T(4,128)S(1)} %copy_bitcast_fusion.own), channel_id=1, source_target_pairs={{0,2},{1,3},{2,0},{3,1},{4,6},{5,7},{6,4},{7,5},{8,10},{9,11},{10,... | collective-permute-start | bytes 215048 | tf_op jit(solution)/shard_map/ppermute | solution.py:743
  105.5 7.2 %collective-permute-start.15 = (f32[5,7,4,128]{3,2,1,0:T(4,128)S(1)}, f32[5,7,4,128]{3,2,1,0:T(4,128)S(1)}, u32[]{:S(2)}, u32[]{:S(2)}) collective-permute-start(f32[5,7,4,128]{3,2,1,0:T(4,128)S(1)} %copy_bitcast_fusion.own), channel_id=1, source_target_pairs={{0,1},{1,0},{2,3},{3,2},{4,5},{5,4},{6,7},{7,6},{8,9},{9,8},{10,11... | collective-permute-start | bytes 215048 | tf_op jit(solution)/shard_map/ppermute | solution.py:743
  107.0 5.6 %collective-permute-start.16 = (f32[5,7,4,128]{3,2,1,0:T(4,128)S(1)}, f32[5,7,4,128]{3,2,1,0:T(4,128)S(1)}, u32[]{:S(2)}, u32[]{:S(2)}) collective-permute-start(f32[5,7,4,128]{3,2,1,0:T(4,128)S(1)} %copy_bitcast_fusion.own), channel_id=1, source_target_pairs={{1,2},{2,1},{3,4},{4,3},{5,6},{6,5},{9,10},{10,9},{11,12},{12,11},... | collective-permute-start | bytes 215048 | tf_op jit(solution)/shard_map/ppermute | solution.py:743
  109.0 3.7 %collective-permute-start.17 = (f32[5,7,4,128]{3,2,1,0:T(4,128)S(1)}, f32[5,7,4,128]{3,2,1,0:T(4,128)S(1)}, u32[]{:S(2)}, u32[]{:S(2)}) collective-permute-start(f32[5,7,4,128]{3,2,1,0:T(4,128)S(1)} %copy_bitcast_fusion.own), channel_id=1, source_target_pairs={{2,4},{3,5},{4,2},{5,3},{10,12},{11,13},{12,10},{13,11},{18,20},{1... | collective-permute-start | bytes 215048 | tf_op jit(solution)/shard_map/ppermute | solution.py:743
  112.6 0.6 copy-start.17
  112.6 0.7 copy-start.18
  112.7 0.7 copy-start.19
  112.7 0.7 copy-start.20
  120.4 9.1 %collective-permute-start.18 = (f32[5,8,16,128]{3,2,1,0:T(8,128)}, f32[5,8,16,128]{3,2,1,0:T(8,128)S(1)}, u32[]{:S(2)}, u32[]{:S(2)}) collective-permute-start(f32[5,8,16,128]{3,2,1,0:T(8,128)} %shard_map.34.own), channel_id=1, source_target_pairs={{0,8},{8,0},{16,24},{24,16},{32,40},{40,32},{48,56},{56,48},{64,72... | collective-permute-start | bytes 983048 | tf_op jit(solution)/shard_map/ppermute | solution.py:743
  120.5 13.1 %collective-permute-start.19 = (f32[5,8,16,128]{3,2,1,0:T(8,128)}, f32[5,8,16,128]{3,2,1,0:T(8,128)S(1)}, u32[]{:S(2)}, u32[]{:S(2)}) collective-permute-start(f32[5,8,16,128]{3,2,1,0:T(8,128)} %shard_map.34.own), channel_id=1, source_target_pairs={{8,16},{16,8},{24,32},{32,24},{40,48},{48,40},{56,64},{64,56},{72,... | collective-permute-start | bytes 983048 | tf_op jit(solution)/shard_map/ppermute | solution.py:743
  129.6 17.2 %copy-start.2 = (f32[5,8,16,128]{3,2,1,0:T(8,128)}, f32[5,8,16,128]{3,2,1,0:T(8,128)S(1)}, u32[]{:S(2)}) copy-start(f32[5,8,16,128]{3,2,1,0:T(8,128)S(1)} %collective-permute-done.18.ax0) | copy-start | bytes 983044
  133.7 13.1 %copy-start.3 = (f32[5,8,16,128]{3,2,1,0:T(8,128)}, f32[5,8,16,128]{3,2,1,0:T(8,128)S(1)}, u32[]{:S(2)}) copy-start(f32[5,8,16,128]{3,2,1,0:T(8,128)S(1)} %collective-permute-done.19.ax1) | copy-start | bytes 983044
  133.7 13.0 %collective-permute-start.21 = (f32[5,20,8,128]{3,2,1,0:T(8,128)S(1)}, f32[5,20,8,128]{3,2,1,0:T(8,128)S(1)}, u32[]{:S(2)}, u32[]{:S(2)}) collective-permute-start(f32[5,20,8,128]{3,2,1,0:T(8,128)S(1)} %pad_maximum_fusion.3), channel_id=1, source_target_pairs={{1,2},{2,1},{3,4},{4,3},{5,6},{6,5},{9,10},{10,9},{11,12},{12,11},... | collective-permute-start | bytes 1228808 | tf_op jit(solution)/shard_map/ppermute | solution.py:743
  141.1 5.6 %collective-permute-start.20 = (f32[5,20,8,128]{3,2,1,0:T(8,128)S(1)}, f32[5,20,8,128]{3,2,1,0:T(8,128)S(1)}, u32[]{:S(2)}, u32[]{:S(2)}) collective-permute-start(f32[5,20,8,128]{3,2,1,0:T(8,128)S(1)} %pad_maximum_fusion.2), channel_id=1, source_target_pairs={{0,1},{1,0},{2,3},{3,2},{4,5},{5,4},{6,7},{7,6},{8,9},{9,8},{10,11... | collective-permute-start | bytes 1228808 | tf_op jit(solution)/shard_map/ppermute | solution.py:743
  146.7 0.8 copy-start.5
  147.5 0.7 copy-start.7

commit v3 on v2

--- a/solution.py
+++ b/solution.py
@@ -587,7 +587,7 @@
 
 
 def chain(level, plan, area, rows, cols, v0, wa, wb, force, prim_v, prim_a, prim_b, rate, half):
-    @pl.loop(0, rows, unroll=2)
+    @pl.loop(0, rows, unroll=4 if rows % 4 == 0 else 7)
     def _(r):
         every = pl.ds(0, cols)
         v = [v0[c, r, every] for c in range(5)]
@@ -670,7 +670,7 @@
     ax_extent = 2 * ends[0]
     origin = 2 * jnp.clip(pos[0] - 3, 0, ends[0] - 7)
 
-    @pl.loop(0, 14, unroll=2)
+    @pl.loop(0, 14, unroll=7)
     def _(r):
         g = begin + r
         at = mirror(g, ax_extent)

time: 164 us -> 163 us (level)
  no operation moved by 1% of the time
where the time goes in v3:
time: 163 us; the launch traced here: 162 us
  Pallas kernels  62.8 us (39%)
  starting transfers between devices  55.8 us (34%)
  waiting for transfers between devices  34.5 us (21%)
  local copies, waits for them, and re-layouts  8.11 us (5%)
    pallas_call x8, Pallas kernels, call(): pl.pallas_call(kernel, out_shape=outs[0] if single else outs, in_specs=sp...  62.8 us
    ppermute x22, starting transfers between devices, swapped(): return lax.ppermute(x, axis, sorted(pairs))  50.1 us
    ppermute x22, waiting for transfers between devices, swapped(): return lax.ppermute(x, axis, sorted(pairs))  28.9 us
    unnamed x50, local copies, waits for them, and re-layouts  5.98 us
    all_to_all x1, starting transfers between devices, per_device(): column = lax.all_to_all(block, 'ax', 0, 0)  5.66 us
    all_to_all x1, waiting for transfers between devices, per_device(): column = lax.all_to_all(block, 'ax', 0, 0)  5.6 us
  transfers between devices with their start and end apart: 23, of which 11 were waited for; matrix products, arithmetic and copies ran while one was open for 2% of the time, Pallas kernels for 6%

profile of v3, /device:TPU:3, one launch (start us, length us, event | category | flops | bytes accessed | tf_op | source)
XLA Modules:
  0.0 162.3 jit_solution(3347589192581832976)
XLA Ops:
  0.0 1.3 collective-permute-start
  1.3 3.8 %collective-permute-start.1 = (f32[5,8,16,128]{3,2,1,0:T(8,128)}, f32[5,8,16,128]{3,2,1,0:T(8,128)S(1)}, u32[]{:S(2)}, u32[]{:S(2)}) collective-permute-start(f32[5,8,16,128]{3,2,1,0:T(8,128)} %own.1), channel_id=1, source_target_pairs={{8,16},{16,8},{24,32},{32,24},{40,48},{48,40},{56,64},{64,56},{72,... | collective-permute-start | bytes 983048 | tf_op jit(solution)/shard_map/ppermute | solution.py:743
  5.1 1.0 constant_dynamic-slice_fusion.8
  6.1 2.7 %collective-permute-done.ax0 = f32[5,8,16,128]{3,2,1,0:T(8,128)S(1)} collective-permute-done((f32[5,8,16,128]{3,2,1,0:T(8,128)}, f32[5,8,16,128]{3,2,1,0:T(8,128)S(1)}, u32[]{:S(2)}, u32[]{:S(2)}) %collective-permute-start) | collective-permute-done | bytes 327712 | tf_op jit(solution)/shard_map/ppermute | solution.py:743
  8.8 5.0 %collective-permute-done.1.ax1 = f32[5,8,16,128]{3,2,1,0:T(8,128)S(1)} collective-permute-done((f32[5,8,16,128]{3,2,1,0:T(8,128)}, f32[5,8,16,128]{3,2,1,0:T(8,128)S(1)}, u32[]{:S(2)}, u32[]{:S(2)}) %collective-permute-start.1) | collective-permute-done | bytes 327712 | tf_op jit(solution)/shard_map/ppermute | solution.py:743
  13.9 5.2 %collective-permute-start.3 = (f32[5,20,8,128]{3,2,1,0:T(8,128)S(1)}, f32[5,20,8,128]{3,2,1,0:T(8,128)S(1)}, u32[]{:S(2)}, u32[]{:S(2)}) collective-permute-start(f32[5,20,8,128]{3,2,1,0:T(8,128)S(1)} %pad_maximum_fusion.1), channel_id=1, source_target_pairs={{1,2},{2,1},{3,4},{4,3},{5,6},{6,5},{9,10},{10,9},{11,12},{12,11},... | collective-permute-start | bytes 1228808 | tf_op jit(solution)/shard_map/ppermute | solution.py:743
  19.2 0.1 collective-permute-start.2
  19.3 0.6 pad_add_fusion.pos
  19.9 3.8 %shard_map.28.fields = f32[3,24,40,128]{3,2,1,0:T(8,128)} custom-call(s32[2]{0:T(128)} %pad_add_fusion.pos, s32[128,4,128]{2,1,0:T(4,128)} %code.5), custom_call_target="tpu_custom_call" | custom-call | flops 1000000 | bytes 1736712 | tf_op jit(solution)/shard_map/pallas_call | solution.py:377
  23.7 1.1 collective-permute-done.3.xs1
  24.7 0.0 collective-permute-done.2.xs0
  24.8 0.8 copy-done.4
  25.5 0.7 copy-done.6
  26.3 15.1 %shard_map.29 = (f32[5,8,16,128]{3,2,1,0:T(8,128)}, f32[5,2,16,128]{3,2,1,0:T(8,128)}, f32[5,2,16,128]{3,2,1,0:T(8,128)}, f32[5,8,2,128]{3,2,1,0:T(2,128)}, f32[5,8,2,128]{3,2,1,0:T(2,128)}) custom-call(s32[2]{0:T(128)} %pad_add_fusion.pos, f32[5,8,16,128]{3,2,1,0:T(8,128)} %own.1, f32[5,8,16,128]{3,2,1,0:T(8,128)} %copy-done, f32[5,8,16,128]{3,2,1,0:T(8,128)} %copy-done.1, ...), custom_call_target="tpu_custom_call" | custom-call | flops 80000000 | bytes 3850248 | tf_op jit(solution)/shard_map/pallas_call | solution.py:377
  41.4 3.8 %collective-permute-start.5 = (f32[5,2,16,128]{3,2,1,0:T(8,128)}, f32[5,2,16,128]{3,2,1,0:T(8,128)S(1)}, u32[]{:S(2)}, u32[]{:S(2)}) collective-permute-start(f32[5,2,16,128]{3,2,1,0:T(8,128)} %get-tuple-element.14), channel_id=1, source_target_pairs={{8,16},{16,8},{24,32},{32,24},{40,48},{48,40},{56,64},{64,56},{72,... | collective-permute-start | bytes 245768 | tf_op jit(solution)/shard_map/ppermute | solution.py:743
  45.2 0.1 collective-permute-start.6
  45.2 3.9 %collective-permute-start.7 = (f32[5,8,2,128]{3,2,1,0:T(2,128)}, f32[5,8,2,128]{3,2,1,0:T(2,128)S(1)}, u32[]{:S(2)}, u32[]{:S(2)}) collective-permute-start(f32[5,8,2,128]{3,2,1,0:T(2,128)} %get-tuple-element.16), channel_id=1, source_target_pairs={{1,2},{2,1},{3,4},{4,3},{5,6},{6,5},{9,10},{10,9},{11,12},{12,11},... | collective-permute-start | bytes 122888 | tf_op jit(solution)/shard_map/ppermute | solution.py:743
  49.2 0.0 collective-permute-done.6.xs0
  49.2 1.9 %collective-permute-done.7.xs1 = f32[5,8,2,128]{3,2,1,0:T(2,128)S(1)} collective-permute-done((f32[5,8,2,128]{3,2,1,0:T(2,128)}, f32[5,8,2,128]{3,2,1,0:T(2,128)S(1)}, u32[]{:S(2)}, u32[]{:S(2)}) %collective-permute-start.7) | collective-permute-done | bytes 40992 | tf_op jit(solution)/shard_map/ppermute | solution.py:743
  51.1 0.6 copy-done.22
  51.7 0.0 copy-done.15
  51.7 0.0 copy-done.16
  51.7 4.1 %shard_map.30.own = f32[5,4,8,128]{3,2,1,0:T(8,128)} custom-call(s32[2]{0:T(128)} %pad_add_fusion.pos, f32[5,8,16,128]{3,2,1,0:T(8,128)} %get-tuple-element.12.own.smoothed, f32[5,2,16,128]{3,2,1,0:T(8,128)} %copy-done.15, f32[5,2,16,128]{3,2,1,0:T(8,128)} %copy-done.16, f32[5,8,2,128]{3,2,1,0:T(2,128)} %copy-done.21, f32[5,8,2,128]{3,2,1,0:T(2,128)} %copy-done.22, ...), custom_call_target="tpu_custom_call" | custom-call | flops 8000000 | bytes 2129928 | tf_op jit(solution)/shard_map/pallas_call | solution.py:377
  55.8 1.6 %collective-permute-start.8 = (f32[5,4,8,128]{3,2,1,0:T(8,128)}, f32[5,4,8,128]{3,2,1,0:T(8,128)S(1)}, u32[]{:S(2)}, u32[]{:S(2)}) collective-permute-start(f32[5,4,8,128]{3,2,1,0:T(8,128)} %shard_map.30.own), channel_id=1, source_target_pairs={{0,16},{8,24},{16,0},{24,8},{32,48},{40,56},{48,32},{56,40},{64,80... | collective-permute-start | bytes 245768 | tf_op jit(solution)/shard_map/ppermute | solution.py:743
  57.5 0.7 collective-permute-start.9
  58.2 3.1 %collective-permute-start.10 = (f32[5,4,8,128]{3,2,1,0:T(8,128)}, f32[5,4,8,128]{3,2,1,0:T(8,128)S(1)}, u32[]{:S(2)}, u32[]{:S(2)}) collective-permute-start(f32[5,4,8,128]{3,2,1,0:T(8,128)} %shard_map.30.own), channel_id=1, source_target_pairs={{8,16},{16,8},{24,32},{32,24},{40,48},{48,40},{56,64},{64,56},{72,... | collective-permute-start | bytes 245768 | tf_op jit(solution)/shard_map/ppermute | solution.py:743
  61.3 3.1 %collective-permute-start.11 = (f32[5,4,8,128]{3,2,1,0:T(8,128)}, f32[5,4,8,128]{3,2,1,0:T(8,128)S(1)}, u32[]{:S(2)}, u32[]{:S(2)}) collective-permute-start(f32[5,4,8,128]{3,2,1,0:T(8,128)} %shard_map.30.own), channel_id=1, source_target_pairs={{16,32},{24,40},{32,16},{40,24},{48,64},{56,72},{64,48},{72,56},{8... | collective-permute-start | bytes 245768 | tf_op jit(solution)/shard_map/ppermute | solution.py:743
  64.4 0.0 collective-permute-done.8.two0
  64.4 0.0 collective-permute-done.9.one0
  64.5 0.9 constant_dynamic-update-slice_fusion.1
  65.4 0.9 collective-permute-done.10.one1
  66.3 3.0 %collective-permute-done.11.two1 = f32[5,4,8,128]{3,2,1,0:T(8,128)S(1)} collective-permute-done((f32[5,4,8,128]{3,2,1,0:T(8,128)}, f32[5,4,8,128]{3,2,1,0:T(8,128)S(1)}, u32[]{:S(2)}, u32[]{:S(2)}) %collective-permute-start.11) | collective-permute-done | bytes 81952 | tf_op jit(solution)/shard_map/ppermute | solution.py:743
  69.3 0.0 collective-permute-start.12
  69.4 5.1 %collective-permute-start.13 = (f32[5,16,8,128]{3,2,1,0:T(8,128)S(1)}, f32[5,16,8,128]{3,2,1,0:T(8,128)S(1)}, u32[]{:S(2)}, u32[]{:S(2)}) collective-permute-start(f32[5,16,8,128]{3,2,1,0:T(8,128)S(1)} %dynamic-slice_dynamic-update-slice_fusion), channel_id=1, source_target_pairs={{1,2},{2,1},{3,4},{4,3},{5,6},{6,5},{9,10},{10,9},{11,12},{12,11},... | collective-permute-start | bytes 983048 | tf_op jit(solution)/shard_map/ppermute | solution.py:743
  74.4 3.6 %shard_map.31.fields = f32[3,20,32,128]{3,2,1,0:T(8,128)} custom-call(s32[2]{0:T(128)} %pad_add_fusion.pos, s32[128,4,128]{2,1,0:T(4,128)} %code.5), custom_call_target="tpu_custom_call" | custom-call | flops 1000000 | bytes 1245192 | tf_op jit(solution)/shard_map/pallas_call | solution.py:377
  78.1 1.1 collective-permute-done.13.xs1
  79.2 0.7 copy-done.11
  79.9 11.7 %shard_map.32 = (f32[16,5,4,128]{3,2,1,0:T(4,128)}, f32[5,4,8,128]{3,2,1,0:T(8,128)}) custom-call(s32[2]{0:T(128)} %pad_add_fusion.pos, f32[5,4,8,128]{3,2,1,0:T(8,128)} %copy-done.13, f32[5,4,8,128]{3,2,1,0:T(8,128)} %copy-done.8, f32[5,4,8,128]{3,2,1,0:T(8,128)} %shard_map.30.own, f32[5,4,8,128]{3,2,1,0:T(8,128)} %copy-done.9, ...), custom_call_target="tpu_custom_call" | custom-call | flops 60000000 | bytes 2293768 | tf_op jit(solution)/shard_map/pallas_call | solution.py:377
  91.6 5.7 %all-to-all-start = ((f32[16,5,4,128]{3,2,1,0:T(4,128)}), f32[16,5,4,128]{3,2,1,0:T(4,128)S(1)}, u32[]{:S(2)}, u32[]{:S(2)}) async-start(f32[16,5,4,128]{3,2,1,0:T(4,128)} %get-tuple-element.17), calls=%async_computation | async-start | bytes 327680 | tf_op jit(solution)/shard_map/all_to_all | solution.py:856
  97.3 5.6 %all-to-all-done = f32[16,5,4,128]{3,2,1,0:T(4,128)S(1)} async-done(((f32[16,5,4,128]{3,2,1,0:T(4,128)}), f32[16,5,4,128]{3,2,1,0:T(4,128)S(1)}, u32[]{:S(2)}, u32[]{:S(2)}) %all-to-all-start) | async-done | bytes 163872 | tf_op jit(solution)/shard_map/all_to_all | solution.py:856
  102.9 0.0 copy-start.12
  102.9 2.2 %collective-permute-start.14 = (f32[5,7,4,128]{3,2,1,0:T(4,128)S(1)}, f32[5,7,4,128]{3,2,1,0:T(4,128)S(1)}, u32[]{:S(2)}, u32[]{:S(2)}) collective-permute-start(f32[5,7,4,128]{3,2,1,0:T(4,128)S(1)} %copy_bitcast_fusion.own), channel_id=1, source_target_pairs={{0,2},{1,3},{2,0},{3,1},{4,6},{5,7},{6,4},{7,5},{8,10},{9,11},{10,... | collective-permute-start | bytes 215048 | tf_op jit(solution)/shard_map/ppermute | solution.py:743
  105.1 1.6 collective-permute-start.15
  106.6 1.9 %collective-permute-start.16 = (f32[5,7,4,128]{3,2,1,0:T(4,128)S(1)}, f32[5,7,4,128]{3,2,1,0:T(4,128)S(1)}, u32[]{:S(2)}, u32[]{:S(2)}) collective-permute-start(f32[5,7,4,128]{3,2,1,0:T(4,128)S(1)} %copy_bitcast_fusion.own), channel_id=1, source_target_pairs={{1,2},{2,1},{3,4},{4,3},{5,6},{6,5},{9,10},{10,9},{11,12},{12,11},... | collective-permute-start | bytes 215048 | tf_op jit(solution)/shard_map/ppermute | solution.py:743
  108.6 0.7 collective-permute-start.17
  109.2 3.0 %shard_map.33.fields = f32[3,14,24,128]{3,2,1,0:T(8,128)} custom-call(s32[2]{0:T(128)} %pad_add_fusion.pos, s32[128,4,128]{2,1,0:T(4,128)} %code.5), custom_call_target="tpu_custom_call" | custom-call | flops 1000000 | bytes 778248 | tf_op jit(solution)/shard_map/pallas_call | solution.py:377
  112.3 0.0 collective-permute-done.15.one0
  112.3 0.0 collective-permute-done.16.one1
  112.3 0.6 copy-done.17
  112.9 0.0 copy-done.18
  112.9 0.0 copy-done.19
  112.9 0.0 copy-done.20
  113.0 6.3 %shard_map.34.own = f32[5,8,16,128]{3,2,1,0:T(8,128)} custom-call(s32[2]{0:T(128)} %pad_add_fusion.pos, f32[5,7,4,128]{3,2,1,0:T(4,128)} %copy-done.12, f32[5,7,4,128]{3,2,1,0:T(4,128)} %copy-done.17, f32[5,7,4,128]{3,2,1,0:T(4,128)} %copy-done.18, f32[5,7,4,128]{3,2,1,0:T(4,128)} %copy-done.19, f32[5,7,4,128]{3,2,1,0:T(4,128)} %copy-done.20, ...), custom_call_target="tpu_custom_call" | custom-call | flops 20000000 | bytes 1611784 | tf_op jit(solution)/shard_map/pallas_call | solution.py:377
  119.3 0.1 collective-permute-start.18
  119.4 4.4 %collective-permute-start.19 = (f32[5,8,16,128]{3,2,1,0:T(8,128)}, f32[5,8,16,128]{3,2,1,0:T(8,128)S(1)}, u32[]{:S(2)}, u32[]{:S(2)}) collective-permute-start(f32[5,8,16,128]{3,2,1,0:T(8,128)} %shard_map.34.own), channel_id=1, source_target_pairs={{8,16},{16,8},{24,32},{32,24},{40,48},{48,40},{56,64},{64,56},{72,... | collective-permute-start | bytes 983048 | tf_op jit(solution)/shard_map/ppermute | solution.py:743
  123.8 1.0 constant_dynamic-slice_fusion.1
  124.8 3.6 %collective-permute-done.18.ax0 = f32[5,8,16,128]{3,2,1,0:T(8,128)S(1)} collective-permute-done((f32[5,8,16,128]{3,2,1,0:T(8,128)}, f32[5,8,16,128]{3,2,1,0:T(8,128)S(1)}, u32[]{:S(2)}, u32[]{:S(2)}) %collective-permute-start.18) | collective-permute-done | bytes 327712 | tf_op jit(solution)/shard_map/ppermute | solution.py:743
  128.5 4.1 %collective-permute-done.19.ax1 = f32[5,8,16,128]{3,2,1,0:T(8,128)S(1)} collective-permute-done((f32[5,8,16,128]{3,2,1,0:T(8,128)}, f32[5,8,16,128]{3,2,1,0:T(8,128)S(1)}, u32[]{:S(2)}, u32[]{:S(2)}) %collective-permute-start.19) | collective-permute-done | bytes 327712 | tf_op jit(solution)/shard_map/ppermute | solution.py:743
  132.6 7.4 %collective-permute-start.21 = (f32[5,20,8,128]{3,2,1,0:T(8,128)S(1)}, f32[5,20,8,128]{3,2,1,0:T(8,128)S(1)}, u32[]{:S(2)}, u32[]{:S(2)}) collective-permute-start(f32[5,20,8,128]{3,2,1,0:T(8,128)S(1)} %pad_maximum_fusion.3), channel_id=1, source_target_pairs={{1,2},{2,1},{3,4},{4,3},{5,6},{6,5},{9,10},{10,9},{11,12},{12,11},... | collective-permute-start | bytes 1228808 | tf_op jit(solution)/shard_map/ppermute | solution.py:743
  140.0 0.1 collective-permute-start.20
  140.1 5.5 %collective-permute-done.21.xs1 = f32[5,20,8,128]{3,2,1,0:T(8,128)S(1)} collective-permute-done((f32[5,20,8,128]{3,2,1,0:T(8,128)S(1)}, f32[5,20,8,128]{3,2,1,0:T(8,128)S(1)}, u32[]{:S(2)}, u32[]{:S(2)}) %collective-permute-start.21) | collective-permute-done | bytes 409632 | tf_op jit(solution)/shard_map/ppermute | solution.py:743
  145.6 0.7 copy-done.5
  146.4 0.7 copy-done.7
  147.1 15.2 %shard_map.35 = f32[5,8,16,128]{3,2,1,0:T(8,128)} custom-call(s32[2]{0:T(128)} %pad_add_fusion.pos, f32[5,8,16,128]{3,2,1,0:T(8,128)} %shard_map.34.own, f32[5,8,16,128]{3,2,1,0:T(8,128)} %copy-done.2, f32[5,8,16,128]{3,2,1,0:T(8,128)} %copy-done.3, f32[5,20,8,128]{3,2,1,0:T(8,128)} %copy-done.7, f32[5,20,8,128]{3,2,1,0:T(8,128)} %copy-done.5, ...), custom_call_target="tpu_custom_call" | custom-call | flops 80000000 | bytes 3604488 | tf_op jit(solution)/shard_map/pallas_call | solution.py:377
  (53 shorter events, 0.3 us)
Async XLA Ops:
  0.0 8.8 %collective-permute-start = (f32[5,8,16,128]{3,2,1,0:T(8,128)}, f32[5,8,16,128]{3,2,1,0:T(8,128)S(1)}, u32[]{:S(2)}, u32[]{:S(2)}) collective-permute-start(f32[5,8,16,128]{3,2,1,0:T(8,128)} %own.1), channel_id=1, source_target_pairs={{0,8},{8,0},{16,24},{24,16},{32,40},{40,32},{48,56},{56,48},{64,72... | collective-permute-start | bytes 983048 | tf_op jit(solution)/shard_map/ppermute | solution.py:743
  1.3 12.5 %collective-permute-start.1 = (f32[5,8,16,128]{3,2,1,0:T(8,128)}, f32[5,8,16,128]{3,2,1,0:T(8,128)S(1)}, u32[]{:S(2)}, u32[]{:S(2)}) collective-permute-start(f32[5,8,16,128]{3,2,1,0:T(8,128)} %own.1), channel_id=1, source_target_pairs={{8,16},{16,8},{24,32},{32,24},{40,48},{48,40},{56,64},{64,56},{72,... | collective-permute-start | bytes 983048 | tf_op jit(solution)/shard_map/ppermute | solution.py:743
  8.8 14.9 %copy-start = (f32[5,8,16,128]{3,2,1,0:T(8,128)}, f32[5,8,16,128]{3,2,1,0:T(8,128)S(1)}, u32[]{:S(2)}) copy-start(f32[5,8,16,128]{3,2,1,0:T(8,128)S(1)} %collective-permute-done.ax0) | copy-start | bytes 983044
  13.8 9.9 %copy-start.1 = (f32[5,8,16,128]{3,2,1,0:T(8,128)}, f32[5,8,16,128]{3,2,1,0:T(8,128)S(1)}, u32[]{:S(2)}) copy-start(f32[5,8,16,128]{3,2,1,0:T(8,128)S(1)} %collective-permute-done.1.ax1) | copy-start | bytes 983044
  13.9 10.9 %collective-permute-start.3 = (f32[5,20,8,128]{3,2,1,0:T(8,128)S(1)}, f32[5,20,8,128]{3,2,1,0:T(8,128)S(1)}, u32[]{:S(2)}, u32[]{:S(2)}) collective-permute-start(f32[5,20,8,128]{3,2,1,0:T(8,128)S(1)} %pad_maximum_fusion.1), channel_id=1, source_target_pairs={{1,2},{2,1},{3,4},{4,3},{5,6},{6,5},{9,10},{10,9},{11,12},{12,11},... | collective-permute-start | bytes 1228808 | tf_op jit(solution)/shard_map/ppermute | solution.py:743
  19.2 5.6 %collective-permute-start.2 = (f32[5,20,8,128]{3,2,1,0:T(8,128)S(1)}, f32[5,20,8,128]{3,2,1,0:T(8,128)S(1)}, u32[]{:S(2)}, u32[]{:S(2)}) collective-permute-start(f32[5,20,8,128]{3,2,1,0:T(8,128)S(1)} %pad_maximum_fusion), channel_id=1, source_target_pairs={{0,1},{1,0},{2,3},{3,2},{4,5},{5,4},{6,7},{7,6},{8,9},{9,8},{10,11... | collective-permute-start | bytes 1228808 | tf_op jit(solution)/shard_map/ppermute | solution.py:743
  24.7 0.8 copy-start.4
  25.5 0.7 copy-start.6
  41.4 9.7 %collective-permute-start.4 = (f32[5,2,16,128]{3,2,1,0:T(8,128)}, f32[5,2,16,128]{3,2,1,0:T(8,128)S(1)}, u32[]{:S(2)}, u32[]{:S(2)}) collective-permute-start(f32[5,2,16,128]{3,2,1,0:T(8,128)} %get-tuple-element.13), channel_id=1, source_target_pairs={{0,8},{8,0},{16,24},{24,16},{32,40},{40,32},{48,56},{56,48},{64,72... | collective-permute-start | bytes 245768 | tf_op jit(solution)/shard_map/ppermute | solution.py:743
  41.4 9.7 %collective-permute-start.5 = (f32[5,2,16,128]{3,2,1,0:T(8,128)}, f32[5,2,16,128]{3,2,1,0:T(8,128)S(1)}, u32[]{:S(2)}, u32[]{:S(2)}) collective-permute-start(f32[5,2,16,128]{3,2,1,0:T(8,128)} %get-tuple-element.14), channel_id=1, source_target_pairs={{8,16},{16,8},{24,32},{32,24},{40,48},{48,40},{56,64},{64,56},{72,... | collective-permute-start | bytes 245768 | tf_op jit(solution)/shard_map/ppermute | solution.py:743
  45.2 4.0 %collective-permute-start.6 = (f32[5,8,2,128]{3,2,1,0:T(2,128)}, f32[5,8,2,128]{3,2,1,0:T(2,128)S(1)}, u32[]{:S(2)}, u32[]{:S(2)}) collective-permute-start(f32[5,8,2,128]{3,2,1,0:T(2,128)} %get-tuple-element.15), channel_id=1, source_target_pairs={{0,1},{1,0},{2,3},{3,2},{4,5},{5,4},{6,7},{7,6},{8,9},{9,8},{10,11... | collective-permute-start | bytes 122888 | tf_op jit(solution)/shard_map/ppermute | solution.py:743
  45.2 5.8 %collective-permute-start.7 = (f32[5,8,2,128]{3,2,1,0:T(2,128)}, f32[5,8,2,128]{3,2,1,0:T(2,128)S(1)}, u32[]{:S(2)}, u32[]{:S(2)}) collective-permute-start(f32[5,8,2,128]{3,2,1,0:T(2,128)} %get-tuple-element.16), channel_id=1, source_target_pairs={{1,2},{2,1},{3,4},{4,3},{5,6},{6,5},{9,10},{10,9},{11,12},{12,11},... | collective-permute-start | bytes 122888 | tf_op jit(solution)/shard_map/ppermute | solution.py:743
  49.2 1.9 %copy-start.21 = (f32[5,8,2,128]{3,2,1,0:T(2,128)}, f32[5,8,2,128]{3,2,1,0:T(2,128)S(1)}, u32[]{:S(2)}) copy-start(f32[5,8,2,128]{3,2,1,0:T(2,128)S(1)} %collective-permute-done.6.xs0) | copy-start | bytes 122884
  51.1 0.6 copy-start.22
  51.1 0.6 copy-start.15
  51.1 0.7 copy-start.16
  55.8 8.5 %collective-permute-start.8 = (f32[5,4,8,128]{3,2,1,0:T(8,128)}, f32[5,4,8,128]{3,2,1,0:T(8,128)S(1)}, u32[]{:S(2)}, u32[]{:S(2)}) collective-permute-start(f32[5,4,8,128]{3,2,1,0:T(8,128)} %shard_map.30.own), channel_id=1, source_target_pairs={{0,16},{8,24},{16,0},{24,8},{32,48},{40,56},{48,32},{56,40},{64,80... | collective-permute-start | bytes 245768 | tf_op jit(solution)/shard_map/ppermute | solution.py:743
  57.5 6.9 %collective-permute-start.9 = (f32[5,4,8,128]{3,2,1,0:T(8,128)}, f32[5,4,8,128]{3,2,1,0:T(8,128)S(1)}, u32[]{:S(2)}, u32[]{:S(2)}) collective-permute-start(f32[5,4,8,128]{3,2,1,0:T(8,128)} %shard_map.30.own), channel_id=1, source_target_pairs={{0,8},{8,0},{16,24},{24,16},{32,40},{40,32},{48,56},{56,48},{64,72... | collective-permute-start | bytes 245768 | tf_op jit(solution)/shard_map/ppermute | solution.py:743
  58.2 8.1 %collective-permute-start.10 = (f32[5,4,8,128]{3,2,1,0:T(8,128)}, f32[5,4,8,128]{3,2,1,0:T(8,128)S(1)}, u32[]{:S(2)}, u32[]{:S(2)}) collective-permute-start(f32[5,4,8,128]{3,2,1,0:T(8,128)} %shard_map.30.own), channel_id=1, source_target_pairs={{8,16},{16,8},{24,32},{32,24},{40,48},{48,40},{56,64},{64,56},{72,... | collective-permute-start | bytes 245768 | tf_op jit(solution)/shard_map/ppermute | solution.py:743
  61.3 8.0 %collective-permute-start.11 = (f32[5,4,8,128]{3,2,1,0:T(8,128)}, f32[5,4,8,128]{3,2,1,0:T(8,128)S(1)}, u32[]{:S(2)}, u32[]{:S(2)}) collective-permute-start(f32[5,4,8,128]{3,2,1,0:T(8,128)} %shard_map.30.own), channel_id=1, source_target_pairs={{16,32},{24,40},{32,16},{40,24},{48,64},{56,72},{64,48},{72,56},{8... | collective-permute-start | bytes 245768 | tf_op jit(solution)/shard_map/ppermute | solution.py:743
  64.4 14.8 %copy-start.13 = (f32[5,4,8,128]{3,2,1,0:T(8,128)}, f32[5,4,8,128]{3,2,1,0:T(8,128)S(1)}, u32[]{:S(2)}) copy-start(f32[5,4,8,128]{3,2,1,0:T(8,128)S(1)} %collective-permute-done.8.two0) | copy-start | bytes 245764
  64.4 14.8 %copy-start.8 = (f32[5,4,8,128]{3,2,1,0:T(8,128)}, f32[5,4,8,128]{3,2,1,0:T(8,128)S(1)}, u32[]{:S(2)}) copy-start(f32[5,4,8,128]{3,2,1,0:T(8,128)S(1)} %collective-permute-done.9.one0) | copy-start | bytes 245764
  66.3 12.9 %copy-start.9 = (f32[5,4,8,128]{3,2,1,0:T(8,128)}, f32[5,4,8,128]{3,2,1,0:T(8,128)S(1)}, u32[]{:S(2)}) copy-start(f32[5,4,8,128]{3,2,1,0:T(8,128)S(1)} %collective-permute-done.10.one1) | copy-start | bytes 245764
  69.3 9.9 %copy-start.14 = (f32[5,4,8,128]{3,2,1,0:T(8,128)}, f32[5,4,8,128]{3,2,1,0:T(8,128)S(1)}, u32[]{:S(2)}) copy-start(f32[5,4,8,128]{3,2,1,0:T(8,128)S(1)} %collective-permute-done.11.two1) | copy-start | bytes 245764
  69.3 8.7 %collective-permute-start.12 = (f32[5,16,8,128]{3,2,1,0:T(8,128)S(1)}, f32[5,16,8,128]{3,2,1,0:T(8,128)S(1)}, u32[]{:S(2)}, u32[]{:S(2)}) collective-permute-start(f32[5,16,8,128]{3,2,1,0:T(8,128)S(1)} %dynamic-slice_dynamic-update-slice_fusion), channel_id=1, source_target_pairs={{0,1},{1,0},{2,3},{3,2},{4,5},{5,4},{6,7},{7,6},{8,9},{9,8},{10,11... | collective-permute-start | bytes 983048 | tf_op jit(solution)/shard_map/ppermute | solution.py:743
  69.4 9.8 %collective-permute-start.13 = (f32[5,16,8,128]{3,2,1,0:T(8,128)S(1)}, f32[5,16,8,128]{3,2,1,0:T(8,128)S(1)}, u32[]{:S(2)}, u32[]{:S(2)}) collective-permute-start(f32[5,16,8,128]{3,2,1,0:T(8,128)S(1)} %dynamic-slice_dynamic-update-slice_fusion), channel_id=1, source_target_pairs={{1,2},{2,1},{3,4},{4,3},{5,6},{6,5},{9,10},{10,9},{11,12},{12,11},... | collective-permute-start | bytes 983048 | tf_op jit(solution)/shard_map/ppermute | solution.py:743
  78.1 1.2 copy-start.10
  79.2 0.7 copy-start.11
  91.6 11.3 %all-to-all-start = ((f32[16,5,4,128]{3,2,1,0:T(4,128)}), f32[16,5,4,128]{3,2,1,0:T(4,128)S(1)}, u32[]{:S(2)}, u32[]{:S(2)}) async-start(f32[16,5,4,128]{3,2,1,0:T(4,128)} %get-tuple-element.17), calls=%async_computation | async-start | bytes 327680 | tf_op jit(solution)/shard_map/all_to_all | solution.py:856
  102.9 9.4 %copy-start.12 = (f32[5,7,4,128]{3,2,1,0:T(4,128)}, f32[5,7,4,128]{3,2,1,0:T(4,128)S(1)}, u32[]{:S(2)}) copy-start(f32[5,7,4,128]{3,2,1,0:T(4,128)S(1)} %copy_bitcast_fusion.own) | copy-start | bytes 215044
  102.9 9.4 %collective-permute-start.14 = (f32[5,7,4,128]{3,2,1,0:T(4,128)S(1)}, f32[5,7,4,128]{3,2,1,0:T(4,128)S(1)}, u32[]{:S(2)}, u32[]{:S(2)}) collective-permute-start(f32[5,7,4,128]{3,2,1,0:T(4,128)S(1)} %copy_bitcast_fusion.own), channel_id=1, source_target_pairs={{0,2},{1,3},{2,0},{3,1},{4,6},{5,7},{6,4},{7,5},{8,10},{9,11},{10,... | collective-permute-start | bytes 215048 | tf_op jit(solution)/shard_map/ppermute | solution.py:743
  105.1 7.2 %collective-permute-start.15 = (f32[5,7,4,128]{3,2,1,0:T(4,128)S(1)}, f32[5,7,4,128]{3,2,1,0:T(4,128)S(1)}, u32[]{:S(2)}, u32[]{:S(2)}) collective-permute-start(f32[5,7,4,128]{3,2,1,0:T(4,128)S(1)} %copy_bitcast_fusion.own), channel_id=1, source_target_pairs={{0,1},{1,0},{2,3},{3,2},{4,5},{5,4},{6,7},{7,6},{8,9},{9,8},{10,11... | collective-permute-start | bytes 215048 | tf_op jit(solution)/shard_map/ppermute | solution.py:743
  106.6 5.6 %collective-permute-start.16 = (f32[5,7,4,128]{3,2,1,0:T(4,128)S(1)}, f32[5,7,4,128]{3,2,1,0:T(4,128)S(1)}, u32[]{:S(2)}, u32[]{:S(2)}) collective-permute-start(f32[5,7,4,128]{3,2,1,0:T(4,128)S(1)} %copy_bitcast_fusion.own), channel_id=1, source_target_pairs={{1,2},{2,1},{3,4},{4,3},{5,6},{6,5},{9,10},{10,9},{11,12},{12,11},... | collective-permute-start | bytes 215048 | tf_op jit(solution)/shard_map/ppermute | solution.py:743
  108.6 3.7 %collective-permute-start.17 = (f32[5,7,4,128]{3,2,1,0:T(4,128)S(1)}, f32[5,7,4,128]{3,2,1,0:T(4,128)S(1)}, u32[]{:S(2)}, u32[]{:S(2)}) collective-permute-start(f32[5,7,4,128]{3,2,1,0:T(4,128)S(1)} %copy_bitcast_fusion.own), channel_id=1, source_target_pairs={{2,4},{3,5},{4,2},{5,3},{10,12},{11,13},{12,10},{13,11},{18,20},{1... | collective-permute-start | bytes 215048 | tf_op jit(solution)/shard_map/ppermute | solution.py:743
  112.3 0.6 copy-start.17
  112.3 0.7 copy-start.18
  112.3 0.7 copy-start.19
  112.3 0.7 copy-start.20
  119.3 9.1 %collective-permute-start.18 = (f32[5,8,16,128]{3,2,1,0:T(8,128)}, f32[5,8,16,128]{3,2,1,0:T(8,128)S(1)}, u32[]{:S(2)}, u32[]{:S(2)}) collective-permute-start(f32[5,8,16,128]{3,2,1,0:T(8,128)} %shard_map.34.own), channel_id=1, source_target_pairs={{0,8},{8,0},{16,24},{24,16},{32,40},{40,32},{48,56},{56,48},{64,72... | collective-permute-start | bytes 983048 | tf_op jit(solution)/shard_map/ppermute | solution.py:743
  119.4 13.1 %collective-permute-start.19 = (f32[5,8,16,128]{3,2,1,0:T(8,128)}, f32[5,8,16,128]{3,2,1,0:T(8,128)S(1)}, u32[]{:S(2)}, u32[]{:S(2)}) collective-permute-start(f32[5,8,16,128]{3,2,1,0:T(8,128)} %shard_map.34.own), channel_id=1, source_target_pairs={{8,16},{16,8},{24,32},{32,24},{40,48},{48,40},{56,64},{64,56},{72,... | collective-permute-start | bytes 983048 | tf_op jit(solution)/shard_map/ppermute | solution.py:743
  128.5 17.2 %copy-start.2 = (f32[5,8,16,128]{3,2,1,0:T(8,128)}, f32[5,8,16,128]{3,2,1,0:T(8,128)S(1)}, u32[]{:S(2)}) copy-start(f32[5,8,16,128]{3,2,1,0:T(8,128)S(1)} %collective-permute-done.18.ax0) | copy-start | bytes 983044
  132.6 13.1 %copy-start.3 = (f32[5,8,16,128]{3,2,1,0:T(8,128)}, f32[5,8,16,128]{3,2,1,0:T(8,128)S(1)}, u32[]{:S(2)}) copy-start(f32[5,8,16,128]{3,2,1,0:T(8,128)S(1)} %collective-permute-done.19.ax1) | copy-start | bytes 983044
  132.6 13.0 %collective-permute-start.21 = (f32[5,20,8,128]{3,2,1,0:T(8,128)S(1)}, f32[5,20,8,128]{3,2,1,0:T(8,128)S(1)}, u32[]{:S(2)}, u32[]{:S(2)}) collective-permute-start(f32[5,20,8,128]{3,2,1,0:T(8,128)S(1)} %pad_maximum_fusion.3), channel_id=1, source_target_pairs={{1,2},{2,1},{3,4},{4,3},{5,6},{6,5},{9,10},{10,9},{11,12},{12,11},... | collective-permute-start | bytes 1228808 | tf_op jit(solution)/shard_map/ppermute | solution.py:743
  140.0 5.6 %collective-permute-start.20 = (f32[5,20,8,128]{3,2,1,0:T(8,128)S(1)}, f32[5,20,8,128]{3,2,1,0:T(8,128)S(1)}, u32[]{:S(2)}, u32[]{:S(2)}) collective-permute-start(f32[5,20,8,128]{3,2,1,0:T(8,128)S(1)} %pad_maximum_fusion.2), channel_id=1, source_target_pairs={{0,1},{1,0},{2,3},{3,2},{4,5},{5,4},{6,7},{7,6},{8,9},{9,8},{10,11... | collective-permute-start | bytes 1228808 | tf_op jit(solution)/shard_map/ppermute | solution.py:743
  145.6 0.8 copy-start.5
  146.4 0.7 copy-start.7
